TPU v7x, 32 devices: a whole 2x2x4 slice. The times are simulated.
32 devices in a mesh: ctx: 8 (over z, y), fsdp: 4 (over x, core).
Axes of the slice: x: 2, y: 2, z: 4, core: 2. Of those that a mesh axis runs over, the one named last changes fastest.
Arguments:
- layer_in: bfloat16 [4, 8192, 1472], P('fsdp', 'ctx'), may hold values from -6 to 6
- out_grad: bfloat16 [4, 8192, 1472], P('fsdp', 'ctx'), may hold values from -6 to 6
- w_query: bfloat16 [1472, 384], P('fsdp'), may hold values from -0.0546875 to 0.0546875
- w_key: bfloat16 [1472, 384], P('fsdp'), may hold values from -0.0546875 to 0.0546875
- w_value: bfloat16 [1472, 384], P('fsdp'), may hold values from -0.15625 to 0.15625
- w_out: bfloat16 [384, 1472], P(None, 'fsdp'), may hold values from -3.59375 to 3.59375
- w_gate: bfloat16 [1472, 3584], P(None, 'fsdp'), may hold values from -0.15625 to 0.15625
- w_up: bfloat16 [1472, 3584], P(None, 'fsdp'), may hold values from -0.15625 to 0.15625
- w_down: bfloat16 [3584, 1472], P('fsdp'), may hold values from -0.09375 to 0.09375
- norm_attn: bfloat16 [1472], P('fsdp'), may hold values from 0.099609375 to 1.8984375
- norm_ffn: bfloat16 [1472], P('fsdp'), may hold values from 0.099609375 to 1.8984375
- rel_bias: bfloat16 [32, 6], P('fsdp'), may hold values from -4 to 4
- deal_table: int32 [128], replicated, may hold values from 0 to 127, as said below
- seg_ids: int32 [4, 4096], P('fsdp'), may hold values from 0 to 7, never falling along the last dimension, each value on 1 to 768 neighbouring positions
Outputs:
- layer_out: bfloat16 [4, 8192, 1472], P('fsdp', 'ctx')
- in_grad: bfloat16 [4, 8192, 1472], P('fsdp', 'ctx')
- grad_query: float32 [1472, 384], P('fsdp')
- grad_key: float32 [1472, 384], P('fsdp')
- grad_value: float32 [1472, 384], P('fsdp')
- grad_out: float32 [384, 1472], P(None, 'fsdp')
- grad_gate: float32 [1472, 3584], P(None, 'fsdp')
- grad_up: float32 [1472, 3584], P(None, 'fsdp')
- grad_down: float32 [3584, 1472], P('fsdp')
- grad_norm_attn: float32 [1472], P('fsdp')
- grad_norm_ffn: float32 [1472], P('fsdp')
- grad_bias: float32 [32, 6], P('fsdp')
Inputs may be any that keep to these rules, and one draw needn't show every extreme that they name: deal_table is a permutation of the 128 blocks of a group, the same for all groups.
All inputs are finite; a program needn't handle non-finite values.
Results may differ from a plain program's by a relative error of at most 0.017.
Values may be sent and summed in bfloat16 or wider, within the bound.
A program may use at most 512 MiB of HBM per device.

v0:
```python
import math

import jax
import jax.numpy as jnp
from jax import lax
from jax.sharding import PartitionSpec as P

HEADS = 6
HDIM = 64
PROMPT = 4096
NCONT = 8
BLK = 64
CONTS = 4096
GROUP = 8192


epsilon = 1e-06
masked_score = -1e30
thresholds = [math.ceil(16 * 8 ** (step_t / 16)) for step_t in range(1, 16)]


def bucket_of(distance):
    distance = jnp.maximum(distance, 0)
    far_bucket = jnp.full(distance.shape, 16, jnp.int32)
    for threshold in thresholds:
        far_bucket = far_bucket + (distance >= threshold).astype(jnp.int32)
    return jnp.where(distance < 16, distance, far_bucket)


def layout(deal_table, seg_row):
    row_index = jnp.arange(GROUP, dtype=jnp.int32)
    dealt_pos = deal_table[row_index // BLK] * BLK + row_index % BLK
    is_cont = dealt_pos >= PROMPT
    offset = jnp.clip(dealt_pos - PROMPT, 0, CONTS - 1)
    labels = jnp.arange(NCONT, dtype=jnp.int32)
    counts = jnp.sum((seg_row[:, None] == labels[None, :]).astype(jnp.int32), axis=0)
    starts = jnp.cumsum(counts) - counts
    own_seg = seg_row[offset]
    seg_start = jnp.sum(jnp.where(own_seg[:, None] == labels[None, :], starts[None, :], 0), axis=1)
    segment = jnp.where(is_cont, own_seg, -1)
    token_pos = jnp.where(is_cont, PROMPT + offset - seg_start, dealt_pos)
    return (dealt_pos, segment, token_pos)


def rms_norm(row_block, gain_vec):
    return (
        row_block
        * lax.rsqrt(jnp.mean(row_block * row_block, axis=-1, keepdims=True) + epsilon)
        * gain_vec
    )


def gelu_mix(gate_pre, up_pre):
    return jax.nn.gelu(gate_pre, approximate=True) * up_pre


def contract_rows(left, right):
    return lax.dot_general(
        left, right, (((0,), (0,)), ((), ())), preferred_element_type=jnp.float32
    )


def contract_cols(left, right):
    return lax.dot_general(
        left, right, (((1,), (1,)), ((), ())), preferred_element_type=jnp.float32
    )


def heads_major(row_block):
    return jnp.transpose(row_block).reshape(HEADS, HDIM, row_block.shape[0])


def rows_major(head_block):
    return jnp.transpose(head_block.reshape(HEADS * HDIM, head_block.shape[2]))


def tile_scores(q_heads, key_t, bias_t):
    return jnp.einsum(
        "hdr,hdk->hrk", q_heads, key_t, preferred_element_type=jnp.float32
    ) + bias_t.astype(jnp.float32)


def log_sum_exp(q_heads, key_stack, bias_tiles):
    head_count, row_count = (q_heads.shape[0], q_heads.shape[2])

    def lse_step(running, pieces):
        run_max, run_sum = running
        key_t, bias_t = pieces
        scores = tile_scores(q_heads, key_t, bias_t)
        new_max = jnp.maximum(run_max, jnp.max(scores, axis=-1))
        run_sum = run_sum * jnp.exp(run_max - new_max) + jnp.sum(
            jnp.exp(scores - new_max[:, :, None]), axis=-1
        )
        return ((new_max, run_sum), None)

    start_state = (
        jnp.full((head_count, row_count), -jnp.inf, jnp.float32),
        jnp.zeros((head_count, row_count), jnp.float32),
    )
    (run_max, run_sum), _ = lax.scan(lse_step, start_state, (key_stack, bias_tiles))
    return run_max + jnp.log(run_sum)


def attend(q_heads, key_stack, value_stack, bias_tiles, lse_rows):

    def out_step(acc_total, pieces):
        key_t, value_t, bias_t = pieces
        prob_tile = jnp.exp(tile_scores(q_heads, key_t, bias_t) - lse_rows[:, :, None]).astype(
            jnp.bfloat16
        )
        return (
            acc_total
            + jnp.einsum("hrk,hdk->hdr", prob_tile, value_t, preferred_element_type=jnp.float32),
            None,
        )

    acc_total, _ = lax.scan(
        out_step, jnp.zeros(q_heads.shape, jnp.float32), (key_stack, value_stack, bias_tiles)
    )
    return acc_total


def attend_back(
    q_heads, do_heads, key_stack, value_stack, bias_tiles, bucket_tiles, lse_rows, bucket_ids
):

    def delta_step(acc_total, pieces):
        key_t, value_t, bias_t = pieces
        prob_tile = jnp.exp(tile_scores(q_heads, key_t, bias_t) - lse_rows[:, :, None])
        dprob_tile = jnp.einsum(
            "hdr,hdk->hrk", do_heads, value_t, preferred_element_type=jnp.float32
        )
        return (acc_total + jnp.sum(prob_tile * dprob_tile, axis=-1), None)

    row_delta, _ = lax.scan(
        delta_step, jnp.zeros(lse_rows.shape, jnp.float32), (key_stack, value_stack, bias_tiles)
    )

    def grad_step(running, pieces):
        d_query, d_table = running
        key_t, value_t, bias_t, bucket_t = pieces
        prob_tile = jnp.exp(tile_scores(q_heads, key_t, bias_t) - lse_rows[:, :, None])
        dprob_tile = jnp.einsum(
            "hdr,hdk->hrk", do_heads, value_t, preferred_element_type=jnp.float32
        )
        d_score = (prob_tile * (dprob_tile - row_delta[:, :, None])).astype(jnp.bfloat16)
        d_query = d_query + jnp.einsum(
            "hrk,hdk->hdr", d_score, key_t, preferred_element_type=jnp.float32
        )
        d_key_t = jnp.einsum("hrk,hdr->hdk", d_score, q_heads, preferred_element_type=jnp.float32)
        d_value_t = jnp.einsum(
            "hrk,hdr->hdk",
            prob_tile.astype(jnp.bfloat16),
            do_heads,
            preferred_element_type=jnp.float32,
        )
        one_hot = (bucket_ids[:, None, None] == bucket_t[None]).astype(jnp.bfloat16)
        d_table = d_table + jnp.einsum(
            "hrk,brk->bh", d_score, one_hot, preferred_element_type=jnp.float32
        )
        return ((d_query, d_table), (d_key_t, d_value_t))

    start_state = (
        jnp.zeros(q_heads.shape, jnp.float32),
        jnp.zeros((bucket_ids.shape[0], q_heads.shape[0]), jnp.float32),
    )
    (d_query, d_table), (d_key_tiles, d_value_tiles) = lax.scan(
        grad_step, start_state, (key_stack, value_stack, bias_tiles, bucket_tiles)
    )
    return (d_query, d_table, d_key_tiles, d_value_tiles)


def on_device(
    layer_in,
    out_grad,
    w_query,
    w_key,
    w_value,
    w_out,
    w_gate,
    w_up,
    w_down,
    norm_attn,
    norm_ffn,
    rel_bias,
    deal_table,
    seg_ids,
):
    group_count, ctx_rows, model_width = layer_in.shape
    all_rows = group_count * ctx_rows
    full_query, full_key, full_value, full_out, gain_attn, gain_ffn, bias_table = (
        lax.all_gather(w_query, "fsdp", axis=0, tiled=True),
        lax.all_gather(w_key, "fsdp", axis=0, tiled=True),
        lax.all_gather(w_value, "fsdp", axis=0, tiled=True),
        lax.all_gather(w_out, "fsdp", axis=1, tiled=True),
        lax.all_gather(norm_attn, "fsdp", axis=0, tiled=True),
        lax.all_gather(norm_ffn, "fsdp", axis=0, tiled=True),
        lax.all_gather(rel_bias, "fsdp", axis=0, tiled=True),
    )
    gain_attn = gain_attn.astype(jnp.float32)
    gain_ffn = gain_ffn.astype(jnp.float32)
    rows_in = layer_in.reshape(all_rows, model_width).astype(jnp.float32)
    normed = rms_norm(rows_in, gain_attn).astype(jnp.bfloat16)
    queries = jnp.dot(normed, full_query, preferred_element_type=jnp.float32).astype(jnp.bfloat16)
    key_rows = jnp.dot(normed, full_key, preferred_element_type=jnp.float32).astype(jnp.bfloat16)
    value_rows = jnp.dot(normed, full_value, preferred_element_type=jnp.float32).astype(
        jnp.bfloat16
    )
    ctx_here = lax.axis_index("ctx")
    key_tile = min(512, GROUP)
    tile_count = GROUP // key_tile
    bucket_ids = jnp.arange(bias_table.shape[0], dtype=jnp.int32)

    def make_bias(pieces):
        bucket_t, allowed_t = pieces
        one_hot = (bucket_ids[:, None, None] == bucket_t[None]).astype(jnp.bfloat16)
        bias_t = jnp.einsum("brk,bh->hrk", one_hot, bias_table, preferred_element_type=jnp.float32)
        return jnp.where(allowed_t[None], bias_t, masked_score).astype(jnp.bfloat16)

    def to_tiles(gathered):
        return jnp.transpose(gathered.reshape(HEADS, HDIM, tile_count, key_tile), (2, 0, 1, 3))

    def from_tiles(tiles):
        return jnp.transpose(tiles, (1, 2, 0, 3)).reshape(HEADS * HDIM, GROUP)

    group_index = 0
    own_keys = jnp.transpose(key_rows)
    own_values = jnp.transpose(value_rows)
    gathered_keys = lax.all_gather(own_keys, "ctx", axis=1, tiled=True)
    gathered_values = lax.all_gather(own_values, "ctx", axis=1, tiled=True)
    dealt_pos, segment, token_pos = layout(deal_table, seg_ids[group_index])
    first_row = ctx_here * ctx_rows
    my_pos = lax.dynamic_slice_in_dim(dealt_pos, first_row, ctx_rows)
    my_seg = lax.dynamic_slice_in_dim(segment, first_row, ctx_rows)
    my_tok = lax.dynamic_slice_in_dim(token_pos, first_row, ctx_rows)
    allowed = (dealt_pos[None, :] <= my_pos[:, None]) & (
        (dealt_pos[None, :] < PROMPT) | (segment[None, :] == my_seg[:, None])
    )
    buckets = bucket_of(my_tok[:, None] - token_pos[None, :])
    bucket_tiles = jnp.transpose(buckets.reshape(ctx_rows, tile_count, key_tile), (1, 0, 2))
    allowed_tiles = jnp.transpose(allowed.reshape(ctx_rows, tile_count, key_tile), (1, 0, 2))
    bias_tiles = lax.map(make_bias, (bucket_tiles, allowed_tiles))
    q_heads = heads_major(queries)
    key_stack = to_tiles(gathered_keys)
    value_stack = to_tiles(gathered_values)
    lse_rows = log_sum_exp(q_heads, key_stack, bias_tiles)
    attended = attend(q_heads, key_stack, value_stack, bias_tiles, lse_rows)
    attn_parts = rows_major(attended).astype(jnp.bfloat16)
    kept_state = [(bias_tiles, bucket_tiles, lse_rows, q_heads)]
    kept_keys = [(key_stack, value_stack)]
    mid_rows = rows_in + jnp.dot(attn_parts, full_out, preferred_element_type=jnp.float32)
    normed_ffn = rms_norm(mid_rows, gain_ffn).astype(jnp.bfloat16)
    grad_rows = out_grad.reshape(all_rows, model_width)
    full_gate, full_up, full_down = (
        lax.all_gather(w_gate, "fsdp", axis=1, tiled=True),
        lax.all_gather(w_up, "fsdp", axis=1, tiled=True),
        lax.all_gather(w_down, "fsdp", axis=0, tiled=True),
    )
    gate_pre = jnp.dot(normed_ffn, full_gate, preferred_element_type=jnp.float32)
    up_pre = jnp.dot(normed_ffn, full_up, preferred_element_type=jnp.float32)
    hidden, mix_back = jax.vjp(gelu_mix, gate_pre, up_pre)
    hidden_low = hidden.astype(jnp.bfloat16)
    ffn_term = jnp.dot(hidden_low, full_down, preferred_element_type=jnp.float32)
    layer_out = (mid_rows + ffn_term).astype(jnp.bfloat16).reshape(layer_in.shape)
    d_hidden = contract_cols(grad_rows, full_down)
    grad_down_here = contract_rows(hidden_low, grad_rows)
    d_gate, d_up = mix_back(d_hidden)
    d_gate = d_gate.astype(jnp.bfloat16)
    d_up = d_up.astype(jnp.bfloat16)
    grad_gate_here = contract_rows(normed_ffn, d_gate)
    grad_up_here = contract_rows(normed_ffn, d_up)
    d_ffn_in = contract_cols(d_gate, full_gate) + contract_cols(d_up, full_up)
    _, norm_back_ffn = jax.vjp(rms_norm, mid_rows, gain_ffn)
    d_mid_norm, grad_gain_ffn = norm_back_ffn(d_ffn_in)
    d_mid = grad_rows.astype(jnp.float32) + d_mid_norm
    d_branch = d_mid.astype(jnp.bfloat16)
    grad_out_full = contract_rows(attn_parts, d_branch)
    d_attn = contract_cols(d_branch, full_out).astype(jnp.bfloat16)
    group_index = 0
    bias_tiles, bucket_tiles, lse_rows, q_heads = kept_state[group_index]
    key_stack, value_stack = kept_keys[group_index]
    do_heads = heads_major(d_attn)
    d_query, d_table, d_key_tiles, d_value_tiles = attend_back(
        q_heads, do_heads, key_stack, value_stack, bias_tiles, bucket_tiles, lse_rows, bucket_ids
    )
    own_dk = lax.psum_scatter(from_tiles(d_key_tiles), "ctx", scatter_dimension=1, tiled=True)
    own_dv = lax.psum_scatter(from_tiles(d_value_tiles), "ctx", scatter_dimension=1, tiled=True)
    dq_parts = rows_major(d_query).astype(jnp.bfloat16)
    dk_parts = jnp.transpose(own_dk).astype(jnp.bfloat16)
    dv_parts = jnp.transpose(own_dv).astype(jnp.bfloat16)
    grad_query_full = contract_rows(normed, dq_parts)
    grad_key_full = contract_rows(normed, dk_parts)
    grad_value_full = contract_rows(normed, dv_parts)
    d_normed = (
        contract_cols(dq_parts, full_query)
        + contract_cols(dk_parts, full_key)
        + contract_cols(dv_parts, full_value)
    )
    _, norm_back_attn = jax.vjp(rms_norm, rows_in, gain_attn)
    d_in_norm, grad_gain_attn = norm_back_attn(d_normed)
    in_grad = (d_mid + d_in_norm).astype(jnp.bfloat16).reshape(layer_in.shape)
    part_query, part_key, part_value, part_out, part_norm_attn, part_norm_ffn, part_bias = (
        lax.psum_scatter(
            grad_query_full.astype(jnp.bfloat16), "fsdp", scatter_dimension=0, tiled=True
        ).astype(jnp.float32),
        lax.psum_scatter(
            grad_key_full.astype(jnp.bfloat16), "fsdp", scatter_dimension=0, tiled=True
        ).astype(jnp.float32),
        lax.psum_scatter(
            grad_value_full.astype(jnp.bfloat16), "fsdp", scatter_dimension=0, tiled=True
        ).astype(jnp.float32),
        lax.psum_scatter(
            grad_out_full.astype(jnp.bfloat16), "fsdp", scatter_dimension=1, tiled=True
        ).astype(jnp.float32),
        lax.psum_scatter(
            grad_gain_attn.astype(jnp.bfloat16), "fsdp", scatter_dimension=0, tiled=True
        ).astype(jnp.float32),
        lax.psum_scatter(
            grad_gain_ffn.astype(jnp.bfloat16), "fsdp", scatter_dimension=0, tiled=True
        ).astype(jnp.float32),
        lax.psum_scatter(
            d_table.astype(jnp.bfloat16), "fsdp", scatter_dimension=0, tiled=True
        ).astype(jnp.float32),
    )
    part_gate, part_up, part_down = (
        lax.psum_scatter(
            grad_gate_here.astype(jnp.bfloat16), "fsdp", scatter_dimension=1, tiled=True
        ).astype(jnp.float32),
        lax.psum_scatter(
            grad_up_here.astype(jnp.bfloat16), "fsdp", scatter_dimension=1, tiled=True
        ).astype(jnp.float32),
        lax.psum_scatter(
            grad_down_here.astype(jnp.bfloat16), "fsdp", scatter_dimension=0, tiled=True
        ).astype(jnp.float32),
    )
    totals = lax.psum(
        (
            part_query,
            part_key,
            part_value,
            part_out,
            part_gate,
            part_up,
            part_down,
            part_norm_attn,
            part_norm_ffn,
            part_bias,
        ),
        "ctx",
    )
    return (
        layer_out,
        in_grad,
        totals[0],
        totals[1],
        totals[2],
        totals[3],
        totals[4],
        totals[5],
        totals[6],
        totals[7],
        totals[8],
        totals[9],
    )


def solution(mesh):
    in_specs = (
        P("fsdp", "ctx", None),
        P("fsdp", "ctx", None),
        P("fsdp", None),
        P("fsdp", None),
        P("fsdp", None),
        P(None, "fsdp"),
        P(None, "fsdp"),
        P(None, "fsdp"),
        P("fsdp", None),
        P("fsdp"),
        P("fsdp"),
        P("fsdp", None),
        P(),
        P("fsdp", None),
    )
    out_specs = (
        P("fsdp", "ctx", None),
        P("fsdp", "ctx", None),
        P("fsdp", None),
        P("fsdp", None),
        P("fsdp", None),
        P(None, "fsdp"),
        P(None, "fsdp"),
        P(None, "fsdp"),
        P("fsdp", None),
        P("fsdp"),
        P("fsdp"),
        P("fsdp", None),
    )
    return jax.shard_map(
        on_device, mesh=mesh, in_specs=in_specs, out_specs=out_specs, check_vma=False
    )
```

profile of v0, /device:TPU:0, one launch (start us, length us, event | category | flops | bytes accessed | tf_op | source)
XLA Modules:
  0.0 3979.7 jit_solution(13089457623395572307)
XLA Ops:
  34.6 13.7 all-gather.10.cloned.1.call-done
  55.4 48.9 %gather_fusion = s32[8192]{0:T(1024)S(1)} fusion(s32[128]{0:T(128)S(1)} %copy-done, s32[8192]{0:T(1024)S(1)} %broadcast_clamp_fusion.1), kind=kCustom, calls=%fused_computation | custom fusion | bytes 98304 | tf_op jit(solution)/shard_map/gather | solution.py:32
  104.7 45.5 %gather_fusion.1 = s32[8192]{0:T(1024)S(1)} fusion(s32[4096]{0:T(1024)S(1)} %bitcast.301, s32[8192]{0:T(1024)S(1)} %broadcast_clamp_fusion), kind=kCustom, calls=%fused_computation.1 | custom fusion | bytes 98304 | tf_op jit(solution)/shard_map/gather | solution.py:38
  155.9 56.8 %compare_select_fusion = s32[16,1024,512]{1,2,0:T(8,128)} fusion(s32[16,512]{1,0:T(8,128)S(1)} %get-tuple-element.660, s32[1024]{0:T(1024)S(1)} %get-tuple-element.667), kind=kLoop, calls=%fused_computation.82 | loop fusion | flops 411041792 | bytes 33591296 | tf_op jit(solution)/shard_map/jit(_where)/select_n | solution.py:27
  223.7 660.4 %while.63 = (s32[]{:T(128)}, bf16[16,6,1024,512]{2,3,1,0:T(8,128)(2,1)}, pred[16,1024,512]{2,1,0:T(8,128)(4,1)}, s32[16,1024,512]{1,2,0:T(8,128)}, bf16[32,6]{0,1:T(8,128)(2,1)S(1)}, /*index=5*/s32[]{:T(128)}) while((s32[]{:T(128)}, bf16[16,6,1024,512]{2,3,1,0:T(8,128)(2,1)}, pred[16,1024,512]{2,1,0:T(8,128)(4,1)}, ...), condition=%wide.region_5.6_spmd.clone, body=%wide.region_4.5_spmd.clone.sunk | while | flops 224395264 | bytes 43516876 | solution.py:242
  228.5 18.3 fusion.224
  269.8 18.3 fusion.224
  311.7 18.3 fusion.224
  352.9 18.3 fusion.224
  394.4 18.3 fusion.224
  435.7 18.3 fusion.224
  476.9 18.3 fusion.224
  518.1 18.3 fusion.224
  559.2 18.3 fusion.224
  600.4 18.3 fusion.224
  641.5 18.3 fusion.224
  682.7 18.3 fusion.224
  723.9 18.3 fusion.224
  765.2 18.3 fusion.224
  806.3 18.3 fusion.224
  847.5 18.3 fusion.224
  910.2 295.1 %while.64 = (s32[]{:T(128)}, f32[6,1024]{1,0:T(8,128)S(1)}, f32[6,1024]{1,0:T(8,128)S(1)}, bf16[16,6,64,512]{3,2,1,0:T(8,128)(2,1)}, bf16[6,64,1024]{2,1,0:T(8,1...) while((s32[]{:T(128)}, f32[6,1024]{1,0:T(8,128)S(1)}, ...), condition=%wide.region_9.10_spmd.clone, body=%wide.region_6.9_spmd.clone.sunk | while | flops 424704000 | bytes 39248992 | solution.py:100
  1227.5 113.9 %while.65 = (s32[]{:T(128)}, f32[6,64,1024]{2,1,0:T(8,128)S(1)}, bf16[16,6,64,512]{3,2,1,0:T(8,128)(2,1)}, bf16[16,6,64,512]{3,2,1,0:T(8,128)(2,1)}, bf16[6,64,1...) while((s32[]{:T(128)}, f32[6,64,1024]{2,1,0:T(8,128)S(1)}, ...), condition=%wide.region_11.12_spmd.clone, body=%wide.region_10.11_spmd.clone.sunk | while | flops 818675712 | bytes 11036263 | solution.py:117
  1353.2 18.4 fusion.150
  1371.6 18.7 fusion.151
  1390.4 32.6 multiply_convert_fusion
  1423.0 17.9 fusion.152
  1440.9 22.4 multiply_reduce_fusion
  1471.3 137.2 %while.66 = (s32[]{:T(128)}, f32[6,1024]{1,0:T(8,128)S(1)}, bf16[16,6,64,512]{3,2,1,0:T(8,128)(2,1)}, bf16[6,64,1024]{2,1,0:T(8,128)(2,1)S(1)}, bf16[16,6,1024,5...) while((s32[]{:T(128)}, f32[6,1024]{1,0:T(8,128)S(1)}, ...), condition=%wide.region_16.17_spmd.clone, body=%wide.region_14.16_spmd.clone.sunk | while | flops 821041152 | bytes 33941100 | solution.py:135
  1608.4 823.2 %while.67 = (s32[]{:T(128)}, f32[6,64,1024]{2,1,0:T(8,128)}, f32[32,6]{0,1:T(8,128)S(1)}, f32[16,6,64,512]{3,2,1,0:T(8,128)}, f32[16,6,64,512]{3,2,1,0:T(8,128)}...) while((s32[]{:T(128)}, f32[6,64,1024]{2,1,0:T(8,128)}, ...), condition=%wide.region_18.19_spmd.clone, body=%wide.region_17.18_spmd.clone.sunk | while | flops 2263613952 | bytes 178992496 | solution.py:167
  1632.4 14.1 fusion.251
  1683.7 14.1 fusion.251
  1735.2 14.1 fusion.251
  1786.6 14.1 fusion.251
  1838.0 14.1 fusion.251
  1889.5 14.1 fusion.251
  1940.9 14.1 fusion.251
  1992.3 14.1 fusion.251
  2043.7 14.1 fusion.251
  2095.1 14.1 fusion.251
  2146.5 14.1 fusion.251
  2197.9 14.1 fusion.251
  2249.3 14.1 fusion.251
  2300.7 14.1 fusion.251
  2352.0 14.1 fusion.251
  2403.5 14.1 fusion.251
  2431.6 16.4 copy.127
  2448.0 21.9 copy.145
  2483.2 16.7 convolution_convert_fusion.1
  2499.8 14.6 copy.136
  2514.6 16.3 convolution_convert_fusion.2
  2546.5 16.3 convolution_convert_fusion
  2562.8 14.6 copy.138
  2577.6 16.7 copy.128
  2594.3 22.4 copy.146
  2618.3 60.4 %reduce-scatter.16.cloned.1.call-done = f32[384,1024]{1,0:T(8,128)} async-done(((f32[384,8192]{1,0:T(8,128)}), f32[384,1024]{1,0:T(8,128)}) %reduce-scatter.16.cloned.1.call-update) | async-done | bytes 1572880 | tf_op jit(solution)/shard_map/reduce_scatter | solution.py:286
  2683.3 18.4 fusion.110
  2707.5 27.5 reduce-scatter.20.cloned.1.call-done
  2735.0 91.3 %reduce-scatter.30.cloned.1.call-done = bf16[896,1472]{1,0:T(8,128)(2,1)} async-done(((bf16[3584,1472]{1,0:T(8,128)(2,1)}), bf16[896,1472]{1,0:T(8,128)(2,1)}) %reduce-scatter.30.cloned.1.call-update) | async-done | bytes 2637840
  2830.9 86.7 %reduce-scatter.28.cloned.1.call-done = bf16[896,1472]{1,0:T(8,128)(2,1)} async-done(((bf16[3584,1472]{1,0:T(8,128)(2,1)}), bf16[896,1472]{1,0:T(8,128)(2,1)}) %reduce-scatter.28.cloned.1.call-update) | async-done | bytes 2637840
  2922.0 86.7 %reduce-scatter.32.cloned.1.call-done = bf16[896,1472]{1,0:T(8,128)(2,1)} async-done(((bf16[3584,1472]{1,0:T(8,128)(2,1)}), bf16[896,1472]{1,0:T(8,128)(2,1)}) %reduce-scatter.32.cloned.1.call-update) | async-done | bytes 2637840
  3013.2 206.8 %reduce-scatter.18.cloned.1.call-done = f32[384,1024]{1,0:T(8,128)} async-done(((f32[384,8192]{1,0:T(8,128)}), f32[384,1024]{1,0:T(8,128)}) %reduce-scatter.18.cloned.1.call-update) | async-done | bytes 1572880 | tf_op jit(solution)/shard_map/reduce_scatter | solution.py:287
  3253.5 22.8 reduce-scatter.24.cloned.1.call-done
  3276.3 696.1 %all-reduce.9 = (f32[368,384]{1,0:T(8,128)}, f32[368,384]{1,0:T(8,128)}, f32[368,384]{1,0:T(8,128)}, f32[384,368]{0,1:T(8,128)}, f32[1472,896]{1,0:T(8,128)}, /*...) all-reduce(bf16[368,384]{1,0:T(8,128)(2,1)} %reduce-scatter.20.clon, ...), channel_id=1, replica_groups=mesh['ctx'=8,'fsdp'=4] {'ctx'}, use_global_device_ids=true, to_apply=%region_23.24 | all-reduce | flops 4522768 | bytes 27138176 | tf_op jit(solution)/shard_map/psum | solution.py:336
  (758 shorter events, 1712.1 us)
Async XLA Ops:
  7.2 48.2 %copy-start = (s32[128]{0:T(128)S(1)}, s32[128]{0:T(128)}, u32[]{:S(2)}) copy-start(s32[128]{0:T(128)} %param.36) | copy-start | bytes 1540
  7.2 22.3 all-gather.14.cloned.1.call-start
  7.9 40.4 %all-gather.10.cloned.1.call-start = ((), (), s32[]{:S(2)}) async-start(), calls=%async_computation.9 | async-start | bytes 1413120 | tf_op jit(solution)/shard_map/all_gather | solution.py:194
  8.7 875.4 %all-gather.18.cloned.1.call-start = ((), (), s32[]{:S(2)}) async-start(), calls=%async_computation.13 | async-start | bytes 1413120 | tf_op jit(solution)/shard_map/all_gather | solution.py:192
  9.4 878.4 %all-gather.16.cloned.1.call-start = ((), (), s32[]{:S(2)}) async-start(), calls=%async_computation.12 | async-start | bytes 7077888 | tf_op jit(solution)/shard_map/all_gather | solution.py:229
  21.7 862.4 %copy-start.28 = (f32[1472]{0:T(1024)}, f32[1472]{0:T(1024)S(1)}, u32[]{:S(2)}) copy-start(f32[1472]{0:T(1024)S(1)} %convert_element_type.270) | copy-start | bytes 17668
  24.9 859.2 %copy-start.30 = (f32[1024]{0:T(1024)}, f32[1024]{0:T(1024)S(1)}, u32[]{:S(2)}) copy-start(f32[1024]{0:T(1024)S(1)} %fusion.140) | copy-start | bytes 12292
  24.9 23.4 copy-start.10
  34.5 1170.8 %all-gather.12.cloned.1.call-start = ((), (), s32[]{:S(2)}) async-start(), calls=%async_computation.10 | async-start | bytes 7077888 | tf_op jit(solution)/shard_map/all_gather | solution.py:230
  52.5 1291.7 %all-gather.20.cloned.1.call-start = ((), (), s32[]{:S(2)}) async-start(), calls=%async_computation.14 | async-start | bytes 1413120 | tf_op jit(solution)/shard_map/all_gather | solution.py:195
  53.0 1300.2 %all-gather.22.cloned.1.call-start = ((), (), s32[]{:S(2)}) async-start(), calls=%async_computation.15 | async-start | bytes 13189120 | tf_op jit(solution)/shard_map/all_gather | solution.py:255
  53.8 1317.9 %all-gather.24.cloned.1.call-start = ((), (), s32[]{:S(2)}) async-start(), calls=%async_computation.16 | async-start | bytes 13189120 | tf_op jit(solution)/shard_map/all_gather | solution.py:256
  54.5 1335.8 %all-gather.26.cloned.1.call-start = ((), (), s32[]{:S(2)}) async-start(), calls=%async_computation.17 | async-start | bytes 13189120 | tf_op jit(solution)/shard_map/all_gather | solution.py:257
  55.3 2623.4 %reduce-scatter.16.cloned.1.call-start = ((), (), s32[]{:S(2)}) async-start(), calls=%async_computation.18 | async-start | bytes 14155776 | tf_op jit(solution)/shard_map/reduce_scatter | solution.py:286
  55.4 49.2 %copy-start.2 = (s32[1,4096]{1,0:T(1,128)S(1)}, s32[1,4096]{1,0:T(1,128)}, u32[]{:S(2)}) copy-start(s32[1,4096]{1,0:T(1,128)} %param.37) | copy-start | bytes 49156
  104.7 46.0 %copy-start.38 = (bf16[8,6]{1,0:T(8,128)(2,1)S(1)}, bf16[8,6]{1,0:T(8,128)(2,1)}, u32[]{:S(2)}) copy-start(bf16[8,6]{1,0:T(8,128)(2,1)} %param.35) | copy-start | bytes 292
  1423.0 17.9 copy-start.39
  1423.0 40.4 %slice-start.2 = ((s8[6029312]{0:T(1024)(128)(4,1)}), s8[4194304]{0:T(1024)(128)(4,1)S(1)}, s32[]{:S(2)}) async-start(s8[6029312]{0:T(1024)(128)(4,1)} %bitcast.306), calls=%async_computation.29 | async-start | bytes 8388608
  1440.9 22.5 slice-start.3
  1440.9 22.5 copy-start.21
  1471.2 137.2 %copy-start.34 = (f32[32,6]{0,1:T(8,128)S(1)}, f32[32,6]{0,1:T(8,128)}, u32[]{:S(2)}) copy-start(f32[32,6]{0,1:T(8,128)} %custom-call.5) | copy-start | bytes 2308
  1629.0 17.4 slice-start
  1632.4 14.2 copy-start.6
  1680.4 17.4 slice-start
  1683.7 14.2 copy-start.6
  1731.9 17.4 slice-start
  1735.2 14.2 copy-start.6
  1783.3 17.4 slice-start
  1786.6 14.2 copy-start.6
  1834.7 17.4 slice-start
  1838.0 14.2 copy-start.6
  1886.1 17.4 slice-start
  1889.5 14.2 copy-start.6
  1937.6 17.4 slice-start
  1940.9 14.2 copy-start.6
  1989.0 17.4 slice-start
  1992.3 14.2 copy-start.6
  2040.4 17.4 slice-start
  2043.7 14.2 copy-start.6
  2091.8 17.4 slice-start
  2143.2 17.4 slice-start
  2146.5 14.2 copy-start.6
  2194.6 17.4 slice-start
  2246.0 17.4 slice-start
  2297.3 17.4 slice-start
  2300.7 14.2 copy-start.6
  2348.7 17.4 slice-start
  2352.0 14.2 copy-start.6
  2400.2 17.4 slice-start
  2403.5 14.2 copy-start.6
  2431.6 16.4 copy-start.35
  2470.0 237.5 %reduce-scatter.26.cloned.1.call-start = ((), (), s32[]{:S(2)}) async-start(), calls=%async_computation.23 | async-start | bytes 1413120 | tf_op jit(solution)/shard_map/reduce_scatter | solution.py:312
  2476.6 258.4 %reduce-scatter.20.cloned.1.call-start = ((), (), s32[]{:S(2)}) async-start(), calls=%async_computation.20 | async-start | bytes 1413120 | tf_op jit(solution)/shard_map/reduce_scatter | solution.py:303
  2483.1 343.3 %reduce-scatter.30.cloned.1.call-start = ((), (), s32[]{:S(2)}) async-start(), calls=%async_computation.25 | async-start | bytes 13762560
  2514.5 403.1 %reduce-scatter.28.cloned.1.call-start = ((), (), s32[]{:S(2)}) async-start(), calls=%async_computation.24 | async-start | bytes 13762560
  2544.6 464.1 %reduce-scatter.32.cloned.1.call-start = ((), (), s32[]{:S(2)}) async-start(), calls=%async_computation.26 | async-start | bytes 13762560
  2577.4 642.6 %reduce-scatter.18.cloned.1.call-start = ((), (), s32[]{:S(2)}) async-start(), calls=%async_computation.19 | async-start | bytes 14155776 | tf_op jit(solution)/shard_map/reduce_scatter | solution.py:287
  2616.7 62.0 %copy-start.11 = (bf16[1,1024,1472]{1,2,0:T(8,128)(2,1)S(1)}, bf16[1,1024,1472]{1,2,0:T(8,128)(2,1)}, u32[]{:S(2)}) copy-start(bf16[1,1024,1472]{1,2,0:T(8,128)(2,1)} %param.24) | copy-start | bytes 9043972
  2616.8 636.7 %reduce-scatter.22.cloned.1.call-start = ((), (), s32[]{:S(2)}) async-start(), calls=%async_computation.21 | async-start | bytes 1413120 | tf_op jit(solution)/shard_map/reduce_scatter | solution.py:306
  2683.0 18.7 copy-start.36
  2683.0 593.3 %reduce-scatter.24.cloned.1.call-start = ((), (), s32[]{:S(2)}) async-start(), calls=%async_computation.22 | async-start | bytes 1413120 | tf_op jit(solution)/shard_map/reduce_scatter | solution.py:309
  3228.0 18.8 copy-start.33
  3246.8 29.5 copy-start.27
  3246.8 725.5 %copy-start.1 = (s32[128]{0:T(128)S(1)}, s32[128]{0:T(128)}, u32[]{:S(2)}) copy-start(s32[128]{0:T(128)} %param.36) | copy-start | bytes 1540
  (103 other events, 759.7 us)
Sparse Core Ops, SparseCore 0:
  9.6 19.8 all-gather.13
  31.1 17.1 all-gather.9
  49.8 17.1 all-gather.17
  69.7 99.0 all-gather.15
  171.4 97.1 all-gather.11
  270.0 15.3 all-gather.19
  287.0 70.4 all-gather.21
  359.1 70.4 all-gather.23
  431.2 70.5 all-gather.25
  2470.1 208.5 reduce-scatter.15
  2681.8 24.4 reduce-scatter.25
  2709.5 25.4 reduce-scatter.19
  2737.6 88.7 reduce-scatter.29
  2828.8 88.7 reduce-scatter.27
  2920.0 88.7 reduce-scatter.31
  3012.2 207.7 reduce-scatter.17
  3223.0 24.6 reduce-scatter.21
  3250.8 25.4 reduce-scatter.23
where the time goes:
time: 4000 us; the launch traced here: 3980 us
  matrix products  1670 us (42%)
  local copies, waits for them, and re-layouts  726 us (18%)
  blocking collectives  721 us (18%)
  waiting for transfers between devices  605 us (15%)
  other arithmetic  231 us (6%)
    psum x1, blocking collectives, on_device(): lax.psum((part_query, part_key, part_value, part_out, part_gate, part_up,...  696 us
    dynamic_update_slice x32, local copies, waits for them, and re-layouts, on_device(): bias_tiles = lax.map(make_bias, (bucket_tiles, allowed_tiles))  294 us
    dot_general x16, matrix products, make_bias(): jnp.einsum('brk,bh->hrk', one_hot, bias_table, preferred_element_type=jnp...  292 us
    unnamed x21, waiting for transfers between devices  270 us
    dot_general x48, matrix products, tile_scores(): jnp.einsum('hdr,hdk->hrk', q_heads, key_t, preferred_element_type=jnp.flo...  244 us
    dot_general x16, matrix products, grad_step(): jnp.einsum('hrk,brk->bh', d_score, one_hot, preferred_element_type=jnp.fl...  226 us
    reduce_scatter x1, waiting for transfers between devices, on_device(): lax.psum_scatter(from_tiles(d_value_tiles), 'ctx', scatter_dimension=1, t...  207 us
    dot_general x16, matrix products, grad_step(): jnp.einsum('hdr,hdk->hrk', do_heads, value_t, preferred_element_type=jnp....  181 us
  transfers between devices with their start and end apart: 18, of which 9 were waited for; matrix products, arithmetic and copies ran while one was open for 39% of the time, Pallas kernels for 0%

commit v1 on v0

v1 whole, which is shorter than its diff:
```python
import functools
import math

import jax
import jax.numpy as jnp
from jax import lax
from jax.experimental import pallas as pl
from jax.experimental.pallas import tpu as pltpu
from jax.sharding import Mesh, PartitionSpec as P

HEADS = 6
HDIM = 64
PROMPT = 4096
NCONT = 8
BLK = 64
CONTS = 4096
GROUP = 8192
NBLK = GROUP // BLK
PBLK = PROMPT // BLK
LOG2E = 1.4426950408889634
NEG = -3e30
M_INIT = -1e30
WIN = 3
WK = WIN * BLK
FARB = 8
FK = FARB * BLK
thresholds = [math.ceil(16 * 8 ** (step_t / 16)) for step_t in range(1, 16)]
epsilon = 1e-06
BF = jnp.bfloat16
F32 = jnp.float32


def dot_nt(a, b):
    return lax.dot_general(a, b, (((1,), (1,)), ((), ())), preferred_element_type=F32)


def dot_nn(a, b):
    return lax.dot_general(a, b, (((1,), (0,)), ((), ())), preferred_element_type=F32)


def dot_tn(a, b):
    return lax.dot_general(a, b, (((0,), (0,)), ((), ())), preferred_element_type=F32)


class Tab:
    def __init__(self, n):
        self.src = 0
        self.slot = NBLK
        self.blk = NBLK + n
        self.nch = NBLK + 2 * n
        self.zf = NBLK + 3 * n
        self.lim = NBLK + 4 * n
        self.size = NBLK + 5 * n


def lane(shape):
    return lax.broadcasted_iota(jnp.int32, shape, len(shape) - 1)


def sub(shape):
    return lax.broadcasted_iota(jnp.int32, shape, len(shape) - 2)


def stack_super(src, dst, base, hi_c):
    low = lane((BLK, 128)) < 64
    for j in range(4):
        blk = src[base + j]
        pair, one = blk[:, :128], blk[:, 128:]
        zero = jnp.zeros_like(pair)
        u, r = j // 2, (j % 2) * 128
        dst[u, r : r + 64, :] = jnp.where(low, pair, zero)
        dst[u, r + 64 : r + 128, :] = jnp.where(low, zero, pair)
        dst[2, j * 64 : (j + 1) * 64, :] = jnp.where(low, zero, one) if hi_c else jnp.where(low, one, zero)


def near_setup(tab, t, base, z_ref, oo_ref, bias_a, bias_c, oh):
    low = lane((WK, 128)) < 64
    for j in range(4):
        oh[j] = (sub((128, 128)) == oo_ref[base + j]).astype(BF)
    zsum = [lambda x, h=h: dot_nn(z_ref[0, h], x) + dot_nn(z_ref[1, h], x) for h in range(3)]
    for j in range(4):
        bias_a[1, j] = jnp.where(low, zsum[0](oh[j]), zsum[1](oh[j]))
    for p in range(2):
        ohc = jnp.where(lane((128, 128)) < 64, oh[2 * p], oh[2 * p + 1])
        bias_c[1, p] = zsum[2](ohc)


def near_scalars(tab, t, base, i):
    offs, act = [], []
    for j in range(4):
        b = tab[t.blk + base + j]
        off = jnp.where(i == 0, b, jnp.where(i == 1, PBLK - WIN + 2, b - WIN * (i - 1)))
        active = i < tab[t.nch + base + j]
        offs.append(jnp.where(active, off, 2))
        act.append(active)
    return offs, act


def near_low(lo_ref, base, j, i, act):
    lo = lo_ref[base + j]
    lo = jnp.where(i == 1, jnp.zeros_like(lo), lo)
    return jnp.where(act[j], lo, jnp.full_like(lo, 1 << 20))


def far_mask(tab, t, base, u, c, shape):
    pos = c * FK + sub(shape)
    ln = lane(shape)
    if u < 2:
        lim = jnp.where(ln < 128, tab[t.lim + base + 2 * u], tab[t.lim + base + 2 * u + 1])
    else:
        lim = jnp.where(
            ln < 128,
            jnp.where(ln < 64, tab[t.lim + base], tab[t.lim + base + 1]),
            jnp.where(ln < 192, tab[t.lim + base + 2], tab[t.lim + base + 3]),
        )
    return pos < lim


def far_counts(tab, t, base):
    lims = [tab[t.lim + base + j] for j in range(4)]
    least = jnp.minimum(jnp.minimum(lims[0], lims[1]), jnp.minimum(lims[2], lims[3]))
    most = jnp.maximum(jnp.maximum(lims[0], lims[1]), jnp.maximum(lims[2], lims[3]))
    return least // FK, (most + FK - 1) // FK


def near_count(tab, t, base):
    ns = [tab[t.nch + base + j] for j in range(4)]
    return jnp.maximum(jnp.maximum(ns[0], ns[1]), jnp.maximum(ns[2], ns[3]))


def load_sorted(tab, t, n, pairs, kv_hbm, kv, sems):
    def kv_start(p, carry):
        pltpu.make_async_copy(kv_hbm.at[tab[t.src + p]], kv.at[p + 2], sems.at[0]).start()
        return carry

    lax.fori_loop(0, NBLK, kv_start, 0)
    for which, (src, dst) in enumerate(pairs):
        def start(r, carry, src=src, dst=dst, which=which):
            pltpu.make_async_copy(src.at[tab[t.slot + r]], dst.at[r], sems.at[which + 1]).start()
            return carry

        lax.fori_loop(0, n, start, 0)
    pltpu.make_async_copy(kv_hbm, kv.at[pl.ds(2, NBLK)], sems.at[0]).wait()
    for which, (src, dst) in enumerate(pairs):
        pltpu.make_async_copy(src, dst, sems.at[which + 1]).wait()


def k_lanes(u):
    return (0, 128) if u < 2 else (256, 384)


def v_lanes(u):
    return (128, 256) if u < 2 else (256, 384)


def flat(x):
    return x.reshape(x.shape[0] * x.shape[1], x.shape[2])


def transpose_far(kv, dst, lanes):
    def step(c, carry):
        for which, (a, b) in enumerate(lanes):
            x = flat(kv[pl.ds(2 + c * FARB, FARB), :, a:b])
            dst[which, :, pl.ds(pl.multiple_of(c * FK, FK), FK)] = jnp.transpose(x)
        return carry

    lax.fori_loop(0, PROMPT // FK, step, 0)


def fwd_kernel(n, tab, kv_hbm, q_hbm, t_ref, z_ref, lo_ref, oo_ref, o_ref, lse_ref,
               kv, qs, qst, vt, bias_a, bias_c, oh, m, l, acc, sems):
    t = Tab(n)
    kv[0:2] = jnp.zeros((2, BLK, 384), BF)
    load_sorted(tab, t, n, [(q_hbm, qs)], kv_hbm, kv, sems)
    transpose_far(kv, vt, [(128, 256), (256, 384)])
    for j in range(4):
        bias_a[0, j] = t_ref[0]
        bias_a[2, j] = jnp.zeros((WK, 128), F32)
    for p in range(2):
        bias_c[0, p] = t_ref[1]
        bias_c[2, p] = jnp.zeros((WK, 128), F32)

    def update(u, a, b, s, pv):
        m_old = m[u, :, a:b]
        m_new = jnp.maximum(m_old, jnp.max(s, axis=0, keepdims=True))
        p = jnp.exp2(s - m_new)
        alpha = jnp.exp2(m_old - m_new)
        m[u, :, a:b] = m_new
        l[u, :, a:b] = l[u, :, a:b] * alpha + jnp.sum(p, axis=0, keepdims=True)
        acc[u, :, a:b] = acc[u, :, a:b] * alpha + pv(p.astype(BF))

    def super_tile(s_i, carry):
        base = s_i * 4
        stack_super(qs, qst, base, False)
        m[...] = jnp.full(m.shape, M_INIT, F32)
        l[...] = jnp.zeros(l.shape, F32)
        acc[...] = jnp.zeros(acc.shape, F32)
        n_near = near_count(tab, t, base)

        @pl.when(n_near > 1)
        def _():
            near_setup(tab, t, base, z_ref, oo_ref, bias_a, bias_c, oh)

        def near(i, carry):
            offs, act = near_scalars(tab, t, base, i)
            kind = jnp.minimum(i, 2)
            low = lane((WK, 128)) < 64
            for j in range(4):
                u, a = j // 2, (j % 2) * 128
                k = flat(kv[pl.ds(offs[j], WIN), :, 0:128])
                v = flat(kv[pl.ds(offs[j], WIN), :, 128:256])
                s = dot_nt(k, qst[u, a : a + 128, :]) * LOG2E + bias_a[kind, j]
                pos = (offs[j] - 2) * BLK + sub((WK, 128))
                s = jnp.where(pos >= near_low(lo_ref, base, j, i, act), s, NEG)
                update(u, a, a + 128, s, lambda p, v=v: dot_tn(v, p))
            for pr in range(2):
                a = pr * 128
                j0, j1 = 2 * pr, 2 * pr + 1
                x0 = flat(kv[pl.ds(offs[j0], WIN), :, 256:384])
                x1 = flat(kv[pl.ds(offs[j1], WIN), :, 256:384])
                q = qst[2, a : a + 128, :]
                s = jnp.where(low, dot_nt(x0, q), dot_nt(x1, q)) * LOG2E + bias_c[kind, pr]
                half = lane((1, 128)) < 64
                pos0 = jnp.where(half, (offs[j0] - 2) * BLK, (offs[j1] - 2) * BLK)
                lows = jnp.where(
                    half, near_low(lo_ref, base, j0, i, act), near_low(lo_ref, base, j1, i, act)
                )
                s = jnp.where(sub((WK, 128)) >= lows - pos0, s, NEG)
                update(
                    2, a, a + 128, s,
                    lambda p, x0=x0, x1=x1: jnp.where(
                        lane((128, 128)) < 64, dot_tn(x0, p), dot_tn(x1, p)
                    ),
                )
            return carry

        lax.fori_loop(0, n_near, near, 0)

        def far(masked, c, carry):
            for u in range(3):
                a, b = k_lanes(u)
                k = flat(kv[pl.ds(2 + c * FARB, FARB), :, a:b])
                s = dot_nt(k, qst[u]) * LOG2E
                if masked:
                    s = jnp.where(far_mask(tab, t, base, u, c, s.shape), s, NEG)
                v = vt[u // 2, :, pl.ds(pl.multiple_of(c * FK, FK), FK)]
                update(u, 0, 256, s, lambda p, v=v: dot_nn(v, p))
            return carry

        n_full, n_far = far_counts(tab, t, base)
        lax.fori_loop(0, n_full, functools.partial(far, False), 0)
        lax.fori_loop(n_full, n_far, functools.partial(far, True), 0)
        low = lane((BLK, 128)) < 64
        for u in range(3):
            lse_ref[s_i, u] = m[u] + jnp.log(l[u]) * LOG2E
            o = jnp.transpose(acc[u] / l[u])
            if u < 2:
                for k in range(2):
                    r = k * 128
                    slot = tab[t.slot + base + 2 * u + k]
                    o_ref[slot, :, 0:128] = jnp.where(low, o[r : r + 64], o[r + 64 : r + 128]).astype(BF)
            else:
                for j in range(4):
                    slot = tab[t.slot + base + j]
                    piece = o[j * 64 : (j + 1) * 64]
                    o_ref[slot, :, 128:256] = jnp.where(low, jnp.zeros_like(piece), piece).astype(BF)
        return carry

    lax.fori_loop(0, n // 4, super_tile, 0)


def bwd_kernel(n, tab, kv_hbm, q_hbm, do_hbm, at_hbm, t_ref, z_ref, lo_ref, oo_ref, lse_ref,
               dq_ref, dkv_hbm, gt_ref, gz_ref,
               kv, dkv, qs, dos, ats, qst, dst, qcm, dcm, kt, bias_a, bias_c, oh, ga, gc, dq, delta, sems):
    t = Tab(n)
    kv[0:2] = jnp.zeros((2, BLK, 384), BF)
    load_sorted(tab, t, n, [(q_hbm, qs), (do_hbm, dos), (at_hbm, ats)], kv_hbm, kv, sems)
    transpose_far(kv, kt, [(0, 128), (256, 384)])

    def clear(p, carry):
        dkv[p] = jnp.zeros((BLK, 384), F32)
        return carry

    lax.fori_loop(0, NBLK + 2, clear, 0)
    for j in range(4):
        bias_a[0, j] = t_ref[0]
        bias_a[2, j] = jnp.zeros((WK, 128), F32)
    for p in range(2):
        bias_c[0, p] = t_ref[1]
        bias_c[2, p] = jnp.zeros((WK, 128), F32)
    ga[...] = jnp.zeros(ga.shape, F32)
    gc[...] = jnp.zeros(gc.shape, F32)
    gz_ref[...] = jnp.zeros(gz_ref.shape, F32)

    def add_rows(first, count, a, b, val):
        dkv[pl.ds(first, count), :, a:b] += val.reshape(count, BLK, b - a)

    def super_tile(s_i, carry):
        base = s_i * 4
        stack_super(qs, qst, base, False)
        stack_super(dos, dst, base, True)
        half_rows = sub((128, 128)) < 64
        for pr in range(2):
            q = qst[2, pr * 128 : (pr + 1) * 128, :]
            d = dst[2, pr * 128 : (pr + 1) * 128, :]
            for k in range(2):
                keep = half_rows if k == 0 else jnp.logical_not(half_rows)
                qcm[pr, k] = jnp.where(keep, q, jnp.zeros_like(q))
                dcm[pr, k] = jnp.where(keep, d, jnp.zeros_like(d))
        prods = []
        for j in range(4):
            prods.append(dos[base + j].astype(F32) * ats[base + j].astype(F32))
        low = lane((BLK, 128)) < 64
        zero = jnp.zeros((BLK, 128), F32)
        for u in range(2):
            parts = []
            for k in range(2):
                pair = prods[2 * u + k][:, :128]
                parts += [jnp.where(low, pair, zero), jnp.where(low, zero, pair)]
            stacked = jnp.concatenate(parts, axis=0)
            delta[u] = jnp.sum(jnp.transpose(stacked), axis=0, keepdims=True)
        stacked = jnp.concatenate([jnp.where(low, zero, pr[:, 128:]) for pr in prods], axis=0)
        delta[2] = jnp.sum(jnp.transpose(stacked), axis=0, keepdims=True)
        dq[...] = jnp.zeros(dq.shape, F32)
        n_near = near_count(tab, t, base)

        @pl.when(n_near > 1)
        def _():
            near_setup(tab, t, base, z_ref, oo_ref, bias_a, bias_c, oh)

        def near(i, carry):
            offs, act = near_scalars(tab, t, base, i)
            kind = jnp.minimum(i, 2)
            low = lane((WK, 128)) < 64
            for j in range(4):
                u, a = j // 2, (j % 2) * 128
                k = flat(kv[pl.ds(offs[j], WIN), :, 0:128])
                v = flat(kv[pl.ds(offs[j], WIN), :, 128:256])
                q = qst[u, a : a + 128, :]
                d = dst[u, a : a + 128, :]
                s = dot_nt(k, q) * LOG2E + bias_a[kind, j]
                pos = (offs[j] - 2) * BLK + sub((WK, 128))
                s = jnp.where(pos >= near_low(lo_ref, base, j, i, act), s, NEG)
                p = jnp.exp2(s - lse_ref[s_i, u, :, a : a + 128])
                ds = (p * (dot_nt(v, d) - delta[u, :, a : a + 128])).astype(BF)
                add_rows(offs[j], WIN, 0, 128, dot_nn(ds, q))
                add_rows(offs[j], WIN, 128, 256, dot_nn(p.astype(BF), d))
                dq[u, :, a : a + 128] += dot_tn(k, ds)
                slot = jnp.where(i == 0, 0, jnp.where(i == 1, 1 + j, 5))
                ga[slot] += ds.astype(F32)
            for pr in range(2):
                a = pr * 128
                j0, j1 = 2 * pr, 2 * pr + 1
                x0 = flat(kv[pl.ds(offs[j0], WIN), :, 256:384])
                x1 = flat(kv[pl.ds(offs[j1], WIN), :, 256:384])
                q = qst[2, a : a + 128, :]
                d = dst[2, a : a + 128, :]
                s = jnp.where(low, dot_nt(x0, q), dot_nt(x1, q)) * LOG2E + bias_c[kind, pr]
                half = lane((1, 128)) < 64
                pos0 = jnp.where(half, (offs[j0] - 2) * BLK, (offs[j1] - 2) * BLK)
                lows = jnp.where(
                    half, near_low(lo_ref, base, j0, i, act), near_low(lo_ref, base, j1, i, act)
                )
                s = jnp.where(sub((WK, 128)) >= lows - pos0, s, NEG)
                p = jnp.exp2(s - lse_ref[s_i, 2, :, a : a + 128])
                dp = jnp.where(low, dot_nt(x0, d), dot_nt(x1, d))
                ds = (p * (dp - delta[2, :, a : a + 128])).astype(BF)
                pb = p.astype(BF)
                for k, jj in enumerate((j0, j1)):
                    add_rows(offs[jj], WIN, 256, 384, dot_nn(ds, qcm[pr, k]) + dot_nn(pb, dcm[pr, k]))
                dq[2, :, a : a + 128] += jnp.where(
                    lane((128, 128)) < 64, dot_tn(x0, ds), dot_tn(x1, ds)
                )
                slot = jnp.where(i == 0, 0, jnp.where(i == 1, 1 + pr, 3))
                gc[slot] += ds.astype(F32)
            return carry

        lax.fori_loop(0, n_near, near, 0)

        @pl.when(n_near > 1)
        def _():
            half = lane((128, 128)) < 64
            none = jnp.zeros((128, 128), BF)
            for j in range(4):
                g = ga[1 + j].astype(BF)
                gz_ref[0] += dot_nt(g, jnp.where(half, oh[j], none))
                gz_ref[1] += dot_nt(g, jnp.where(half, none, oh[j]))
                ga[1 + j] = jnp.zeros((WK, 128), F32)
            for pr in range(2):
                g = gc[1 + pr].astype(BF)
                gz_ref[2] += dot_nt(g, jnp.where(half, oh[2 * pr], oh[2 * pr + 1]))
                gc[1 + pr] = jnp.zeros((WK, 128), F32)

        def far(masked, c, carry):
            first = 2 + c * FARB
            for u in range(3):
                a, b = k_lanes(u)
                k = flat(kv[pl.ds(first, FARB), :, a:b])
                s = dot_nt(k, qst[u]) * LOG2E
                if masked:
                    s = jnp.where(far_mask(tab, t, base, u, c, s.shape), s, NEG)
                p = jnp.exp2(s - lse_ref[s_i, u])
                va, vb = v_lanes(u)
                v = k if u == 2 else flat(kv[pl.ds(first, FARB), :, va:vb])
                ds = (p * (dot_nt(v, dst[u]) - delta[u])).astype(BF)
                pb = p.astype(BF)
                if u < 2:
                    add_rows(first, FARB, a, b, dot_nn(ds, qst[u]))
                    add_rows(first, FARB, va, vb, dot_nn(pb, dst[u]))
                else:
                    add_rows(first, FARB, a, b, dot_nn(ds, qst[u]) + dot_nn(pb, dst[u]))
                dq[u] += dot_nn(kt[u // 2, :, pl.ds(pl.multiple_of(c * FK, FK), FK)], ds)
            return carry

        n_full, n_far = far_counts(tab, t, base)
        lax.fori_loop(0, n_full, functools.partial(far, False), 0)
        lax.fori_loop(n_full, n_far, functools.partial(far, True), 0)
        for u in range(3):
            o = jnp.transpose(dq[u])
            if u < 2:
                for k in range(2):
                    r = k * 128
                    slot = tab[t.slot + base + 2 * u + k]
                    dq_ref[slot, :, 0:128] = jnp.where(low, o[r : r + 64], o[r + 64 : r + 128]).astype(BF)
            else:
                for j in range(4):
                    slot = tab[t.slot + base + j]
                    piece = o[j * 64 : (j + 1) * 64]
                    dq_ref[slot, :, 128:256] = jnp.where(low, piece, jnp.zeros_like(piece)).astype(BF)
        return carry

    lax.fori_loop(0, n // 4, super_tile, 0)
    gt_ref[0] = ga[0]
    gt_ref[1] = gc[0]

    def give(p, carry):
        kv[p + 2] = dkv[p + 2].astype(BF)
        pltpu.make_async_copy(kv.at[p + 2], dkv_hbm.at[tab[t.src + p]], sems.at[0]).start()
        return carry

    lax.fori_loop(0, NBLK, give, 0)
    pltpu.make_async_copy(kv.at[pl.ds(2, NBLK)], dkv_hbm, sems.at[0]).wait()


VM = pl.BlockSpec(memory_space=pltpu.VMEM)
HB = pl.BlockSpec(memory_space=pl.ANY)
SM = pl.BlockSpec(memory_space=pltpu.SMEM)


def attn_fwd(tab, kv, q, t_tab, z_tab, lo, oo):
    n = q.shape[0]
    pairs = n * BLK * 2600 * 3
    return pl.pallas_call(
        functools.partial(fwd_kernel, n),
        out_shape=(
            jax.ShapeDtypeStruct((n, BLK, 256), BF),
            jax.ShapeDtypeStruct((n // 4, 3, 1, 256), F32),
        ),
        in_specs=[SM, HB, HB, VM, VM, VM, VM],
        out_specs=(VM, VM),
        scratch_shapes=[
            pltpu.VMEM((NBLK + 2, BLK, 384), BF),
            pltpu.VMEM((n, BLK, 256), BF),
            pltpu.VMEM((3, 256, 128), BF),
            pltpu.VMEM((2, 128, PROMPT), BF),
            pltpu.VMEM((3, 4, WK, 128), F32),
            pltpu.VMEM((3, 2, WK, 128), F32),
            pltpu.VMEM((4, 128, 128), BF),
            pltpu.VMEM((3, 1, 256), F32),
            pltpu.VMEM((3, 1, 256), F32),
            pltpu.VMEM((3, 128, 256), F32),
            pltpu.SemaphoreType.DMA((2,)),
        ],
        compiler_params=pltpu.CompilerParams(vmem_limit_bytes=36 << 20),
        cost_estimate=pl.CostEstimate(
            flops=pairs * 1024, bytes_accessed=8 << 20, transcendentals=pairs
        ),
        name="attn_fwd",
    )(tab, kv, q, t_tab, z_tab, lo, oo)


def attn_bwd(tab, kv, q, do, at, t_tab, z_tab, lo, oo, lse):
    n = q.shape[0]
    pairs = n * BLK * 2600 * 3
    return pl.pallas_call(
        functools.partial(bwd_kernel, n),
        out_shape=(
            jax.ShapeDtypeStruct((n, BLK, 256), BF),
            jax.ShapeDtypeStruct((NBLK, BLK, 384), BF),
            jax.ShapeDtypeStruct((2, WK, 128), F32),
            jax.ShapeDtypeStruct((3, WK, 128), F32),
        ),
        in_specs=[SM, HB, HB, HB, HB, VM, VM, VM, VM, VM],
        out_specs=(VM, HB, VM, VM),
        scratch_shapes=[
            pltpu.VMEM((NBLK + 2, BLK, 384), BF),
            pltpu.VMEM((NBLK + 2, BLK, 384), F32),
            pltpu.VMEM((n, BLK, 256), BF),
            pltpu.VMEM((n, BLK, 256), BF),
            pltpu.VMEM((n, BLK, 256), BF),
            pltpu.VMEM((3, 256, 128), BF),
            pltpu.VMEM((3, 256, 128), BF),
            pltpu.VMEM((2, 2, 128, 128), BF),
            pltpu.VMEM((2, 2, 128, 128), BF),
            pltpu.VMEM((2, 128, PROMPT), BF),
            pltpu.VMEM((3, 4, WK, 128), F32),
            pltpu.VMEM((3, 2, WK, 128), F32),
            pltpu.VMEM((4, 128, 128), BF),
            pltpu.VMEM((6, WK, 128), F32),
            pltpu.VMEM((4, WK, 128), F32),
            pltpu.VMEM((3, 128, 256), F32),
            pltpu.VMEM((3, 1, 256), F32),
            pltpu.SemaphoreType.DMA((4,)),
        ],
        compiler_params=pltpu.CompilerParams(vmem_limit_bytes=52 << 20),
        cost_estimate=pl.CostEstimate(
            flops=pairs * 2560, bytes_accessed=16 << 20, transcendentals=pairs
        ),
        name="attn_bwd",
    )(tab, kv, q, do, at, t_tab, z_tab, lo, oo, lse)


def bucket_of(distance):
    distance = jnp.maximum(distance, 0)
    far_bucket = jnp.full(distance.shape, 16, jnp.int32)
    for threshold in thresholds:
        far_bucket = far_bucket + (distance >= threshold).astype(jnp.int32)
    return jnp.where(distance < 16, distance, far_bucket)


def near_distance():
    diag = (WIN - 1) * BLK + jnp.arange(BLK)[None, :] - jnp.arange(WK)[:, None]
    tail = WK + jnp.arange(128)[None, :] - jnp.arange(WK)[:, None]
    return diag.astype(jnp.int32), tail.astype(jnp.int32)


def bias_tables(table):
    last = table.shape[0] - 1
    rel = (table - table[last:]) * LOG2E
    diag, tail = near_distance()

    def pick(dist):
        bucket = bucket_of(dist)
        out = jnp.zeros((3,) + dist.shape, F32)
        for b in range(last):
            out = jnp.where(bucket[None] == b, rel[b][:, None, None], out)
        return out

    d = jnp.where(diag[None] >= 0, pick(diag), NEG)
    z = pick(tail)
    t_tab = jnp.stack([jnp.concatenate([d[0], d[1]], axis=1), jnp.concatenate([d[2], d[2]], axis=1)])
    z_hi = z.astype(BF)
    z_lo = (z - z_hi.astype(F32)).astype(BF)
    return t_tab, jnp.stack([z_hi, z_lo])


def bias_grads(gt, gz, buckets):
    diag, tail = near_distance()
    gd = jnp.stack([gt[0, :, :64], gt[0, :, 64:], gt[1, :, :64] + gt[1, :, 64:]])
    bd, bt = bucket_of(diag), bucket_of(tail)
    labels = jnp.arange(buckets - 1, dtype=jnp.int32)[:, None, None, None]
    seen = diag >= 0
    one = jnp.sum(jnp.where((bd[None, None] == labels) & seen[None, None], gd[None], 0.0), axis=(2, 3))
    two = jnp.sum(jnp.where(bt[None, None] == labels, gz[None], 0.0), axis=(2, 3))
    near = one + two
    return jnp.concatenate([near, -jnp.sum(near, axis=0, keepdims=True)], axis=0)


def plan(deal_table, seg_row, ctx, nb):
    n = 2 * nb
    par = ctx % 2
    slot = jnp.arange(NBLK, dtype=jnp.int32)
    owner = slot // nb
    where_kv = ((owner // 2) * 2 + (owner % 2 + par) % 2) * nb + slot % nb
    src = jnp.sum(jnp.where(deal_table[None, :] == slot[:, None], where_kv[None, :], 0), axis=1)
    own = lax.dynamic_slice_in_dim(deal_table, ctx * nb, nb)
    other = lax.dynamic_slice_in_dim(deal_table, (ctx + 1 - 2 * par) * nb, nb)
    rb = jnp.concatenate([own, other])
    rank = jnp.sum((rb[None, :] < rb[:, None]).astype(jnp.int32), axis=1)
    pos = jnp.arange(n, dtype=jnp.int32)
    pick = (rank[None, :] == pos[:, None]).astype(jnp.int32)
    rslot = jnp.sum(pick * pos[None, :], axis=1)
    rblk = jnp.sum(pick * rb[None, :], axis=1)
    labels = jnp.arange(NCONT, dtype=jnp.int32)
    starts = jnp.sum((seg_row[None, :] < labels[:, None]).astype(jnp.int32), axis=1)
    cpos = rblk[:, None] * BLK + jnp.arange(BLK, dtype=jnp.int32)[None, :] - PROMPT
    ss = jnp.max(jnp.where(starts[None, None, :] <= cpos[:, :, None], starts[None, None, :], 0), axis=2)
    is_cont = rblk >= PBLK
    lo = jnp.where(is_cont[:, None], PROMPT + ss, 0)
    oo = jnp.where(is_cont[:, None], jnp.minimum(cpos - ss, 127), 127)
    first = (PROMPT + ss[:, 0]) // BLK
    more = jnp.maximum(rblk - (WIN - 1) - first, 0)
    nch = jnp.where(is_cont, 2 + (more + WIN - 1) // WIN, 1)
    zf = jnp.zeros_like(nch)
    lim = jnp.where(is_cont, PROMPT - WK, jnp.maximum(rblk - (WIN - 1), 0) * BLK)
    tab = jnp.concatenate([src, rslot, rblk, nch, zf, lim]).astype(jnp.int32)
    dup = lambda x: jnp.concatenate([x, x], axis=1)[:, None, :].astype(jnp.int32)
    return tab, dup(lo), dup(oo)


def rms_norm(row_block, gain_vec):
    return (
        row_block
        * lax.rsqrt(jnp.mean(row_block * row_block, axis=-1, keepdims=True) + epsilon)
        * gain_vec
    )


def gelu_mix(gate_pre, up_pre):
    return jax.nn.gelu(gate_pre, approximate=True) * up_pre


def head_cols(w, h):
    return w[:, h * HDIM : (h + 1) * HDIM]


def swap(x, axis):
    return lax.ppermute(x, axis, [(0, 1), (1, 0)])


def pick_half(par, even, odd):
    return jnp.where(par == 0, even, odd)


def on_device(
    layer_in, out_grad, w_query, w_key, w_value, w_out, w_gate, w_up, w_down,
    norm_attn, norm_ffn, rel_bias, deal_table, seg_ids,
):
    _, rows, width = layer_in.shape
    nb = rows // BLK
    cz, par = lax.axis_index("cz"), lax.axis_index("cy")
    steps = lax.axis_size("cz")
    ctx = cz * 2 + par
    share = w_query.shape[0]
    fs = ("fx", "fc")
    cs = ("cz", "cy")
    shards = width // share

    none = jnp.zeros((share, HDIM), BF)
    out_t = jnp.transpose(w_out)
    packs, outs = [], []
    for p in range(2):
        a, b, c = 3 * p, 3 * p + 1, 3 * p + 2
        packs.append(jnp.concatenate(
            [head_cols(w_key, a), head_cols(w_key, b), head_cols(w_value, a), head_cols(w_value, b),
             head_cols(w_key, c), head_cols(w_value, c), head_cols(w_query, a), head_cols(w_query, b),
             head_cols(w_query, c)], axis=1))
        outs.append(jnp.concatenate(
            [head_cols(out_t, a), head_cols(out_t, b), none, head_cols(out_t, c)], axis=1))
    extra = jnp.zeros((share, HDIM), BF)
    extra = jnp.concatenate(
        [norm_attn[:, None], norm_ffn[:, None],
         jnp.pad(rel_bias, ((0, share - rel_bias.shape[0]), (0, 0))),
         jnp.zeros((share, HDIM - 2 - HEADS), BF)], axis=1)
    w_qkv = jnp.concatenate(
        [pick_half(par, packs[0], packs[1]), extra, pick_half(par, packs[1], packs[0]), none], axis=1)
    w_o = jnp.concatenate([pick_half(par, outs[0], outs[1]), pick_half(par, outs[1], outs[0])], axis=1)
    w_qkv = lax.all_gather(w_qkv, fs, axis=0, tiled=True)
    w_o = lax.all_gather(w_o, fs, axis=0, tiled=True)
    gain_attn = w_qkv[:, 576].astype(F32)
    gain_ffn = w_qkv[:, 577].astype(F32)
    bias_rows = rel_bias.shape[0]
    table = w_qkv.reshape(shards, share, 1280)[:, :bias_rows, 578 : 578 + HEADS]
    table = table.reshape(shards * bias_rows, HEADS).astype(F32)
    my_table = pick_half(par, table[:, :3], table[:, 3:])

    def spread(w):
        far = swap(w, "fx")
        return [w, swap(w, "fc"), far, swap(far, "fc")]

    gates, ups, downs = spread(w_gate), spread(w_up), spread(w_down)

    rows_in = layer_in.reshape(rows, width).astype(F32)
    normed = rms_norm(rows_in, gain_attn).astype(BF)
    qkv = jnp.dot(normed, w_qkv, preferred_element_type=F32).astype(BF)
    mine, other = qkv[:, :640], swap(qkv[:, 640:], "cy")
    kv = jnp.stack([mine[:, :384], other[:, :384]])
    q = jnp.stack([mine[:, 384:], other[:, 384:]]).reshape(2 * nb, BLK, 256)
    kv = lax.all_gather(kv, "cz", axis=0, tiled=True).reshape(NBLK, BLK, 384)
    tab, lo, oo = plan(deal_table, seg_ids[0], ctx, nb)
    t_tab, z_tab = bias_tables(my_table)
    att, lse = attn_fwd(tab, kv, q, t_tab, z_tab, lo, oo)
    halves = att.reshape(2, rows, 256)
    att_rows = jnp.concatenate([halves[0], swap(halves[1], "cy")], axis=1)

    mid = rows_in + dot_nt(att_rows, w_o)
    normed_ffn = rms_norm(mid, gain_ffn).astype(BF)
    dy = out_grad.reshape(rows, width)
    total, d_ffn_in = mid, None
    parts = []
    for r in range(4):
        gate_pre = jnp.dot(normed_ffn, gates[r], preferred_element_type=F32)
        up_pre = jnp.dot(normed_ffn, ups[r], preferred_element_type=F32)
        hidden, mix_back = jax.vjp(gelu_mix, gate_pre, up_pre)
        hidden = hidden.astype(BF)
        total = total + jnp.dot(hidden, downs[r], preferred_element_type=F32)
        d_gate, d_up = mix_back(dot_nt(dy, downs[r]))
        d_gate, d_up = d_gate.astype(BF), d_up.astype(BF)
        back = dot_nt(d_gate, gates[r]) + dot_nt(d_up, ups[r])
        d_ffn_in = back if d_ffn_in is None else d_ffn_in + back
        parts.append((dot_tn(normed_ffn, d_gate), dot_tn(normed_ffn, d_up), dot_tn(hidden, dy)))
    layer_out = total.astype(BF).reshape(layer_in.shape)

    def fold(g):
        near = g[0] + swap(g[1].astype(BF), "fc").astype(F32)
        far = g[2] + swap(g[3].astype(BF), "fc").astype(F32)
        return near + swap(far.astype(BF), "fx").astype(F32)

    def over_ctx(g):
        piece = lax.psum_scatter(g.astype(BF), cs, scatter_dimension=0, tiled=True)
        return lax.all_gather(piece, cs, axis=0, tiled=True).astype(F32)

    grad_gate, grad_up, grad_down = [over_ctx(fold([p[k] for p in parts])) for k in range(3)]

    _, norm_back_ffn = jax.vjp(rms_norm, mid, gain_ffn)
    d_mid_norm, g_gain_ffn = norm_back_ffn(d_ffn_in)
    d_mid = dy.astype(F32) + d_mid_norm
    d_branch = d_mid.astype(BF)
    d_att = jnp.dot(d_branch, w_o, preferred_element_type=F32).astype(BF)
    do = jnp.stack([d_att[:, :256], swap(d_att[:, 256:], "cy")]).reshape(2 * nb, BLK, 256)
    g_out = dot_tn(d_branch, att_rows)
    dq, dkv, gt, gz = attn_bwd(tab, kv, q, do, att, t_tab, z_tab, lo, oo, lse)
    dq = dq.reshape(2, rows, 256)
    dq_other = swap(dq[1], "cy")
    dkv = lax.psum_scatter(dkv.reshape(GROUP, 384), "cz", scatter_dimension=0, tiled=True)
    dkv_other = swap(dkv[rows:], "cy")
    d_qkv = jnp.concatenate([dkv[:rows], dq[0], dkv_other, dq_other], axis=1)
    g_qkv = dot_tn(normed, d_qkv)
    d_normed = dot_nt(d_qkv, w_qkv)
    _, norm_back_attn = jax.vjp(rms_norm, rows_in, gain_attn)
    d_in_norm, g_gain_attn = norm_back_attn(d_normed)
    in_grad = (d_mid + d_in_norm).astype(BF).reshape(layer_in.shape)

    f_here = lax.axis_index("fx") * 2 + lax.axis_index("fc")

    def reduce_attn(g):
        half = g.shape[1] // 2
        g = pick_half(par, g, jnp.concatenate([g[:, half:], g[:, :half]], axis=1))
        blocks = g.reshape(shards, share, g.shape[1])
        away = lambda r: lax.dynamic_index_in_dim(blocks, f_here ^ r, keepdims=False)
        own = fold([away(r) for r in range(4)])
        pad = (-share) % 64
        return over_ctx(jnp.pad(own, ((0, pad), (0, 0))))[:share]

    g_out = reduce_attn(g_out)
    g_qkv = reduce_attn(g_qkv)
    cols = lambda g, at: g[:, at : at + HDIM]
    p0, p1 = 0, 640
    grad_key = jnp.concatenate([cols(g_qkv, p + o) for p in (p0, p1) for o in (0, 64, 256)], axis=1)
    grad_value = jnp.concatenate([cols(g_qkv, p + o) for p in (p0, p1) for o in (128, 192, 320)], axis=1)
    grad_query = jnp.concatenate([cols(g_qkv, p + o) for p in (p0, p1) for o in (384, 448, 512)], axis=1)
    grad_out = jnp.transpose(
        jnp.concatenate([cols(g_out, p + o) for p in (0, 256) for o in (0, 64, 192)], axis=1))

    g_bias = bias_grads(gt, gz, table.shape[0])
    zero = jnp.zeros_like(g_bias)
    g_bias = jnp.concatenate([pick_half(par, g_bias, zero), pick_half(par, zero, g_bias)], axis=1)
    small = lax.psum((g_gain_attn, g_gain_ffn, g_bias), cs + fs)
    own = lambda v, size: lax.dynamic_slice_in_dim(v, f_here * size, size)
    return (
        layer_out, in_grad, grad_query, grad_key, grad_value, grad_out, grad_gate, grad_up, grad_down,
        own(small[0], share), own(small[1], share), own(small[2], bias_rows),
    )


def solution(mesh):
    devices = mesh.devices
    ctx_size, fsdp_size = mesh.shape["ctx"], mesh.shape["fsdp"]
    split = Mesh(devices.reshape(ctx_size // 2, 2, fsdp_size // 2, 2), ("cz", "cy", "fx", "fc"))
    cs, fs = ("cz", "cy"), ("fx", "fc")
    in_specs = (
        P(fs, cs, None), P(fs, cs, None), P(fs, None), P(fs, None), P(fs, None), P(None, fs),
        P(None, fs), P(None, fs), P(fs, None), P(fs), P(fs), P(fs, None), P(), P(fs, None),
    )
    out_specs = (
        P(fs, cs, None), P(fs, cs, None), P(fs, None), P(fs, None), P(fs, None), P(None, fs),
        P(None, fs), P(None, fs), P(fs, None), P(fs), P(fs), P(fs, None),
    )
    return jax.shard_map(
        on_device, mesh=split, in_specs=in_specs, out_specs=out_specs, check_vma=False
    )
```

time: 4000 us -> 1360 us (0.34)
  matrix products: 1670 us -> 271 us
  local copies, waits for them, and re-layouts: 726 us -> 64.4 us
  blocking collectives: 721 us -> 103 us
  Pallas kernels: 0 us -> 221 us
  other arithmetic: 231 us -> 80 us
    dot_general x197 -> x42, matrix products: 1670 us -> 271 us  [the longest x14 119 us: dot_nt(): lax.dot_general(a, b, (((1,), (1,)), ((), ())), preferred_element_type=F32)]
    psum x1, blocking collectives: 696 us -> 38.4 us  [on_device(): small = lax.psum((g_gain_attn, g_gain_ffn, g_bias), cs + fs)]
    ppermute x0 -> x29, waiting for transfers between devices: none -> 338 us  [swap(): return lax.ppermute(x, axis, [(0, 1), (1, 0)])]
    dynamic_update_slice x32 -> x0, local copies, waits for them, and re-layouts: 294 us -> none  [on_device(): bias_tiles = lax.map(make_bias, (bucket_tiles, allowed_tiles))]
    unnamed x21 -> x14, waiting for transfers between devices: 270 us -> 1.18 us
    pallas_call x0 -> x2, Pallas kernels: none -> 221 us  [the longest x1 115 us: attn_fwd(): pl.pallas_call(functools.partial(fwd_kernel, n), out_shape=(jax.ShapeDtyp...]
    reduce_scatter x6 -> x4, waiting for transfers between devices: 317 us -> 138 us  [the longest x3 138 us: over_ctx(): piece = lax.psum_scatter(g.astype(BF), cs, scatter_dimension=0, tiled=True)]
    reduce_sum x18 -> x7, other arithmetic: 145 us -> 5.15 us  [the longest x1 2.5 us: bias_grads(): jnp.sum(jnp.where(bt[None, None] == labels, gz[None], 0.0), axis=(2, 3))]
  transfers between devices with their start and end apart: 18 -> 41, of which waited for: 9 -> 16; matrix products, arithmetic and copies ran while one was open for 39% -> 28% of each run, Pallas kernels for 0% -> 16%
where the time goes in v1:
time: 1360 us; the launch traced here: 1350 us
  waiting for transfers between devices  576 us (42%)
  matrix products  271 us (20%)
  Pallas kernels  221 us (16%)
  blocking collectives  103 us (8%)
  other arithmetic  80 us (6%)
  local copies, waits for them, and re-layouts  64.4 us (5%)
  starting transfers between devices  21.2 us (2%)
  between operations  15.6 us (1%)
    ppermute x29, waiting for transfers between devices, swap(): return lax.ppermute(x, axis, [(0, 1), (1, 0)])  338 us
    reduce_scatter x3, waiting for transfers between devices, over_ctx(): piece = lax.psum_scatter(g.astype(BF), cs, scatter_dimension=0, tiled=True)  138 us
    dot_general x14, matrix products, dot_nt(): lax.dot_general(a, b, (((1,), (1,)), ((), ())), preferred_element_type=F32)  119 us
    pallas_call x1, Pallas kernels, attn_fwd(): pl.pallas_call(functools.partial(fwd_kernel, n), out_shape=(jax.ShapeDtyp...  115 us
    pallas_call x1, Pallas kernels, attn_bwd(): pl.pallas_call(functools.partial(bwd_kernel, n), out_shape=(jax.ShapeDtyp...  106 us
    all_gather x3, waiting for transfers between devices, over_ctx(): return lax.all_gather(piece, cs, axis=0, tiled=True).astype(F32)  65.6 us
    all_gather x2, blocking collectives, over_ctx(): return lax.all_gather(piece, cs, axis=0, tiled=True).astype(F32)  64.9 us
    dot_general x14, matrix products, dot_tn(): lax.dot_general(a, b, (((0,), (0,)), ((), ())), preferred_element_type=F32)  61 us
  transfers between devices with their start and end apart: 41, of which 16 were waited for; matrix products, arithmetic and copies ran while one was open for 28% of the time, Pallas kernels for 16%

profile of v1, /device:TPU:0, one launch (start us, length us, event | category | flops | bytes accessed | tf_op | source)
XLA Modules:
  0.0 1352.7 jit_solution(6636543825849484130)
XLA Ops:
  25.7 33.6 %all-gather.7.cloned.1.call-done = bf16[1472,1280]{1,0:T(8,128)(2,1)} async-done(((bf16[368,1280]{1,0:T(8,128)(2,1)}), bf16[1472,1280]{1,0:T(8,128)(2,1)}) %all-gather.7.cloned.1.call-update) | async-done | bytes 3768336 | tf_op jit(solution)/shard_map/all_gather | solution.py:658
  61.1 6.9 convolution_convert_fusion
  69.8 29.3 %collective-permute-done = bf16[1024,640]{1,0:T(8,128)(2,1)S(1)} collective-permute-done((bf16[1024,640]{1,0:T(8,128)(2,1)S(1)}, bf16[1024,640]{1,0:T(8,128)(2,1)S(1)}, u32[]{:S(2)}, u32[]{:S(2)}) %collective-permute-start) | collective-permute-done | bytes 1310752 | tf_op jit(solution)/shard_map/ppermute | solution.py:618
  111.6 169.1 %collective-permute-done.7 = bf16[896,1472]{0,1:T(8,128)(2,1)} collective-permute-done((bf16[896,1472]{0,1:T(8,128)(2,1)}, bf16[896,1472]{0,1:T(8,128)(2,1)}, u32[]{:S(2)}, u32[]{:S(2)}) %collective-permute-start.7) | collective-permute-done | bytes 2637856 | tf_op jit(solution)/shard_map/ppermute | solution.py:618
  289.6 114.6 %attn_fwd.1 = (bf16[32,64,256]{2,1,0:T(8,128)(2,1)S(1)}, f32[8,3,1,256]{3,2,1,0:T(1,128)S(1)}) custom-call(s32[288]{0:T(512)S(1)} %concatenate.75.tab, bf16[128,64,384]{2,1,0:T(8,128)(2,1)S(1)} %bitcast.190, bf16[32,64,256]{2,1,0:T(8,128)(2,1)S(1)} %bitcast.183, f32[2,192,128]{2,1,0:T(8,128)S(1)} %pad_maximum_fusion.17.t_ref, ...), custom_call_target="tpu_custom_call" | custom-call | flops 16357785600 | bytes 8388608 | tf_op jit(solution)/shard_map/attn_fwd/pallas_call | solution.py:453
  406.0 7.1 fusion.45
  419.1 4.2 multiply_reduce_fusion.2
  430.6 3.5 fusion.142
  434.2 5.7 fusion.150
  439.9 9.4 fusion.36
  453.0 8.8 multiply_convert_fusion.4
  461.9 5.1 fusion.151
  467.0 5.5 fusion.152
  472.5 5.3 fusion.144
  477.8 5.3 fusion.145
  483.2 9.2 multiply_convert_fusion.3
  501.2 4.7 convolution_convert_fusion.4
  506.3 5.3 fusion.147
  511.6 5.3 fusion.148
  516.9 7.1 fusion.157
  524.1 7.0 fusion.153
  531.1 9.8 multiply_convert_fusion.2
  540.9 8.3 fusion.155
  553.0 7.1 fusion.154
  560.1 7.1 fusion.156
  570.5 4.6 add_convert_fusion.4
  576.8 36.0 %collective-permute-done.22 = bf16[1472,896]{1,0:T(8,128)(2,1)S(1)} collective-permute-done((bf16[1472,896]{1,0:T(8,128)(2,1)S(1)}, bf16[1472,896]{1,0:T(8,128)(2,1)S(1)}, u32[]{:S(2)}, u32[]{:S(2)}) %collective-permute-start.22) | collective-permute-done | bytes 2637856 | tf_op jit(solution)/shard_map/ppermute | solution.py:618
  615.2 21.5 %multiply_reduce_fusion = (f32[1472]{0:T(1024)}, f32[1024]{0:T(1024)S(1)}, f32[1024,1472]{0,1:T(8,128)}) fusion(f32[1024,1472]{0,1:T(8,128)} %copy-done.3, f32[1024]{0:T(1024)S(1)} %copy-done.23, f32[1472]{0:T(1024)S(1)} %copy-done.21, f32[1024,1472]{0,1:T(8,128)} %fusion.157, bf16[1024,896]{1,0:T(8,128)(2,1)S(1)} %get-tuple-element.134, ...), kind=kOutput, calls=%fused_computation.19 | convolution fusion | flops 2720724480 | bytes 58756608 | tf_op jit(solution)/shard_map/dot_general | solution.py:34
  636.7 5.9 fusion.159
  642.6 5.4 fusion.4
  648.1 20.6 %collective-permute-done.25 = bf16[1472,896]{1,0:T(8,128)(2,1)} collective-permute-done((bf16[1472,896]{1,0:T(8,128)(2,1)}, bf16[1472,896]{1,0:T(8,128)(2,1)}, u32[]{:S(2)}, u32[]{:S(2)}) %collective-permute-start.25) | collective-permute-done | bytes 2637856 | tf_op jit(solution)/shard_map/ppermute | solution.py:618
  668.7 4.8 add_convert_fusion.3
  673.6 4.6 fusion.63
  679.9 15.2 %collective-permute-done.11 = bf16[1024,256]{1,0:T(8,128)(2,1)S(1)} collective-permute-done((bf16[1024,256]{1,0:T(8,128)(2,1)S(1)}, bf16[1024,256]{1,0:T(8,128)(2,1)S(1)}, u32[]{:S(2)}, u32[]{:S(2)}) %collective-permute-start.11) | collective-permute-done | bytes 524320 | tf_op jit(solution)/shard_map/ppermute | solution.py:618
  696.2 106.1 %attn_bwd.1 = (bf16[32,64,256]{2,1,0:T(8,128)(2,1)}, bf16[128,64,384]{2,1,0:T(8,128)(2,1)}, f32[2,192,128]{2,1,0:T(8,128)S(1)}, f32[3,192,128]{2,1,0:T(8,128)S(1)}) custom-call(s32[288]{0:T(512)S(1)} %concatenate.75.tab, bf16[128,64,384]{2,1,0:T(8,128)(2,1)} %bitcast.189, bf16[32,64,256]{2,1,0:T(8,128)(2,1)} %bitcast.184, bf16[32,64,256]{2,1,0:T(8,128)(2,1)} %bitcast.198, ...), custom_call_target="tpu_custom_call" | custom-call | flops 40894464000 | bytes 16777216 | tf_op jit(solution)/shard_map/attn_bwd/pallas_call | solution.py:485
  804.1 5.1 convolution_convert_fusion.1
  814.2 4.6 add_convert_fusion.2
  819.3 4.9 fusion.43
  827.5 50.9 %collective-permute-done.28 = bf16[896,1472]{0,1:T(8,128)(2,1)} collective-permute-done((bf16[896,1472]{0,1:T(8,128)(2,1)}, bf16[896,1472]{0,1:T(8,128)(2,1)}, u32[]{:S(2)}, u32[]{:S(2)}) %collective-permute-start.28) | collective-permute-done | bytes 2637856 | tf_op jit(solution)/shard_map/ppermute | solution.py:618
  878.4 4.4 copy.102
  882.8 6.2 add_convert_fusion.1
  889.4 4.7 fusion.59
  900.3 10.5 collective-permute-done.19
  917.0 7.1 fusion.143
  924.1 7.2 fusion.149
  931.4 7.1 fusion.146
  944.2 15.4 %fusion.37 = bf16[1,1024,1472]{1,2,0:T(8,128)(2,1)} fusion(bf16[1024,896]{1,0:T(8,128)(2,1)} %get-tuple-element.136, bf16[896,1472]{0,1:T(8,128)(2,1)} %collective-permute-done.10, f32[1024,1472]{0,1:T(8,128)} %fusion.149, f32[1024,1472]{0,1:T(8,128)} %fusion.146, f32[1024,1472]{0,1:T(8,128)} %copy-done.3, f32[1024,1472]{0,1:T(8,128)} %fusion.143), kind=kOutput, calls=%fused_computation.86 | convolution fusion | flops 2708668416 | bytes 31604736 | tf_op jit(solution)/shard_map/dot_general | solution.py:696
  959.6 50.6 %reduce-scatter.17.cloned.1.call-done = bf16[112,1472]{1,0:T(8,128)(2,1)} async-done(((bf16[896,1472]{1,0:T(8,128)(2,1)}), bf16[112,1472]{1,0:T(8,128)(2,1)}) %reduce-scatter.17.cloned.1.call-update) | async-done | bytes 329744 | tf_op jit(solution)/shard_map/reduce_scatter | solution.py:710
  1010.7 5.9 fusion.68
  1016.6 3.8 fusion.123
  1022.0 9.2 maximum_select_fusion
  1031.1 3.5 fusion.66
  1047.1 27.4 %reduce-scatter.15.cloned.1.call-done = bf16[48,512]{1,0:T(8,128)(2,1)} async-done(((bf16[384,512]{1,0:T(8,128)(2,1)}), bf16[48,512]{1,0:T(8,128)(2,1)}) %reduce-scatter.15.cloned.1.call-update) | async-done | bytes 49168 | tf_op jit(solution)/shard_map/reduce_scatter | solution.py:710
  1074.5 32.2 %all_gather.28 = bf16[384,512]{1,0:T(8,128)(2,1)S(1)} all-gather(bf16[48,512]{1,0:T(8,128)(2,1)} %reduce-scatter.15.cloned.1.call-done), channel_id=1, replica_groups=mesh['cz'=4,'cy'=2,'fx'=2,'fc'=2] {'cz','cy'}, dimensions={0}, use_global_device_ids=true | all-gather | bytes 442368 | tf_op jit(solution)/shard_map/all_gather | solution.py:711
  1111.4 10.7 fusion.3
  1122.1 38.4 %all-reduce.5 = (f32[1472]{0:T(1024)S(1)}, f32[1472]{0:T(1024)S(1)}, f32[32,6]{0,1:T(8,128)S(1)}) all-reduce(f32[1472]{0:T(1024)} %get-tuple-element.86, f32[1472]{0:T(1024)} %get-tuple-element.84, f32[32,6]{0,1:T(8,128)} %pad_maximum_fusion.18), channel_id=1, replica_groups=mesh['cz'=4,'cy'=2,'fx'=2,'fc'=2] {'cz','cy','fx','fc'}, use_global_device_ids=true, to_apply=%region_17.18 | all-reduce | flops 3136 | bytes 25088 | tf_op jit(solution)/shard_map/psum | solution.py:758
  1163.3 6.6 fusion.38
  1169.9 4.5 convert_element_type.5275
  1174.3 13.2 all-gather.15.cloned.1.call-done
  1187.6 4.5 convert_element_type.5283
  1192.0 52.4 %all-gather.17.cloned.1.call-done = bf16[896,1472]{1,0:T(8,128)(2,1)} async-done(((bf16[112,1472]{1,0:T(8,128)(2,1)}), bf16[896,1472]{1,0:T(8,128)(2,1)}) %all-gather.17.cloned.1.call-update) | async-done | bytes 2637840 | tf_op jit(solution)/shard_map/all_gather | solution.py:711
  1244.4 5.0 copy.106
  1249.4 60.3 %reduce-scatter.13.cloned.1.call-done = bf16[48,1280]{1,0:T(8,128)(2,1)} async-done(((bf16[384,1280]{1,0:T(8,128)(2,1)}), bf16[48,1280]{1,0:T(8,128)(2,1)}) %reduce-scatter.13.cloned.1.call-update) | async-done | bytes 122896 | tf_op jit(solution)/shard_map/reduce_scatter | solution.py:710
  1309.7 32.7 %all_gather.27 = bf16[384,1280]{1,0:T(8,128)(2,1)S(1)} all-gather(bf16[48,1280]{1,0:T(8,128)(2,1)} %reduce-scatter.13.cloned.1.call-done), channel_id=1, replica_groups=mesh['cz'=4,'cy'=2,'fx'=2,'fc'=2] {'cz','cy'}, dimensions={0}, use_global_device_ids=true | all-gather | bytes 1105920 | tf_op jit(solution)/shard_map/all_gather | solution.py:711
  (348 shorter events, 138.9 us)
Async XLA Ops:
  7.2 52.1 %all-gather.7.cloned.1.call-start = ((), (), s32[]{:S(2)}) async-start(), calls=%async_computation.6 | async-start | bytes 4710400 | tf_op jit(solution)/shard_map/all_gather | solution.py:658
  24.4 262.1 %all-gather.9.cloned.1.call-start = ((), (), s32[]{:S(2)}) async-start(), calls=%async_computation.7 | async-start | bytes 7864320 | tf_op jit(solution)/shard_map/all_gather | solution.py:679
  25.7 42.3 %copy-start.28 = (f32[1024]{0:T(1024)}, f32[1024]{0:T(1024)S(1)}, u32[]{:S(2)}) copy-start(f32[1024]{0:T(1024)S(1)} %fusion.112) | copy-start | bytes 12292
  61.1 362.3 %copy-start.20 = (f32[1472]{0:T(1024)}, f32[1472]{0:T(1024)S(1)}, u32[]{:S(2)}) copy-start(f32[1472]{0:T(1024)S(1)} %get-tuple-element.88) | copy-start | bytes 17668
  68.2 31.0 %collective-permute-start = (bf16[1024,640]{1,0:T(8,128)(2,1)S(1)}, bf16[1024,640]{1,0:T(8,128)(2,1)S(1)}, u32[]{:S(2)}, u32[]{:S(2)}) collective-permute-start(bf16[1024,640]{1,0:T(8,128)(2,1)S(1)} %slice.461), channel_id=1, source_target_pairs={{0,4},{4,0},{1,5},{5,1},{2,6},{6,2},{3,7},{7,3},{8,12},{12,8},{9,1... | collective-permute-start | bytes 3932168 | tf_op jit(solution)/shard_map/ppermute | solution.py:618
  69.8 33.5 %copy-start.17 = (bf16[384,368]{0,1:T(8,128)(2,1)S(1)}, bf16[384,368]{0,1:T(8,128)(2,1)}, u32[]{:S(2)}) copy-start(bf16[384,368]{0,1:T(8,128)(2,1)} %param.19) | copy-start | bytes 847876
  100.6 9.1 copy-start.35
  100.6 9.6 copy-start.32
  100.6 318.5 %all-gather.11.cloned.1.call-start = ((), (), s32[]{:S(2)}) async-start(), calls=%async_computation.8 | async-start | bytes 1884160 | tf_op jit(solution)/shard_map/all_gather | solution.py:659
  100.6 314.1 %collective-permute-start.5 = (bf16[1472,896]{1,0:T(8,128)(2,1)}, bf16[1472,896]{1,0:T(8,128)(2,1)}, u32[]{:S(2)}, u32[]{:S(2)}) collective-permute-start(bf16[1472,896]{1,0:T(8,128)(2,1)} %param.20), channel_id=1, source_target_pairs={{0,2},{2,0},{1,3},{3,1},{4,6},{6,4},{5,7},{7,5},{8,10},{10,8},{9,1... | collective-permute-start | bytes 7913480 | tf_op jit(solution)/shard_map/ppermute | solution.py:618
  101.0 371.5 %collective-permute-start.2 = (bf16[1472,896]{1,0:T(8,128)(2,1)}, bf16[1472,896]{1,0:T(8,128)(2,1)}, u32[]{:S(2)}, u32[]{:S(2)}) collective-permute-start(bf16[1472,896]{1,0:T(8,128)(2,1)} %param.20), channel_id=1, source_target_pairs={{0,1},{1,0},{2,3},{3,2},{4,5},{5,4},{6,7},{7,6},{8,9},{9,8},{10,11... | collective-permute-start | bytes 7913480 | tf_op jit(solution)/shard_map/ppermute | solution.py:618
  101.0 312.0 %collective-permute-start.6 = (bf16[1472,896]{1,0:T(8,128)(2,1)}, bf16[1472,896]{1,0:T(8,128)(2,1)}, u32[]{:S(2)}, u32[]{:S(2)}) collective-permute-start(bf16[1472,896]{1,0:T(8,128)(2,1)} %param.21), channel_id=1, source_target_pairs={{0,2},{2,0},{1,3},{3,1},{4,6},{6,4},{5,7},{7,5},{8,10},{10,8},{9,1... | collective-permute-start | bytes 7913480 | tf_op jit(solution)/shard_map/ppermute | solution.py:618
  102.7 375.1 %collective-permute-start.3 = (bf16[1472,896]{1,0:T(8,128)(2,1)}, bf16[1472,896]{1,0:T(8,128)(2,1)}, u32[]{:S(2)}, u32[]{:S(2)}) collective-permute-start(bf16[1472,896]{1,0:T(8,128)(2,1)} %param.21), channel_id=1, source_target_pairs={{0,1},{1,0},{2,3},{3,2},{4,5},{5,4},{6,7},{7,6},{8,9},{9,8},{10,11... | collective-permute-start | bytes 7913480 | tf_op jit(solution)/shard_map/ppermute | solution.py:618
  103.0 177.7 %collective-permute-start.7 = (bf16[896,1472]{0,1:T(8,128)(2,1)}, bf16[896,1472]{0,1:T(8,128)(2,1)}, u32[]{:S(2)}, u32[]{:S(2)}) collective-permute-start(bf16[896,1472]{0,1:T(8,128)(2,1)} %param.22), channel_id=1, source_target_pairs={{0,2},{2,0},{1,3},{3,1},{4,6},{6,4},{5,7},{7,5},{8,10},{10,8},{9,1... | collective-permute-start | bytes 7913480 | tf_op jit(solution)/shard_map/ppermute | solution.py:618
  104.4 808.6 %reduce-scatter.19.cloned.1.call-start = ((), (), s32[]{:S(2)}) async-start(), calls=%async_computation.16 | async-start | bytes 2967552
  110.9 169.8 %copy-start.36 = (s32[128]{0:T(128)}, s32[128]{0:T(128)S(1)}, u32[]{:S(2)}) copy-start(s32[128]{0:T(128)S(1)} %iota_add_fusion) | copy-start | bytes 1540
  280.7 123.7 %collective-permute-start.10 = (bf16[896,1472]{0,1:T(8,128)(2,1)}, bf16[896,1472]{0,1:T(8,128)(2,1)}, u32[]{:S(2)}, u32[]{:S(2)}) collective-permute-start(bf16[896,1472]{0,1:T(8,128)(2,1)} %collective-permute-done.7), channel_id=1, source_target_pairs={{0,1},{1,0},{2,3},{3,2},{4,5},{5,4},{6,7},{7,6},{8,9},{9,8},{10,11... | collective-permute-start | bytes 7913480 | tf_op jit(solution)/shard_map/ppermute | solution.py:618
  286.5 117.8 %copy-start = (bf16[2,1024,256]{2,1,0:T(8,128)(2,1)}, bf16[2,1024,256]{2,1,0:T(8,128)(2,1)S(1)}, u32[]{:S(2)}) copy-start(bf16[2,1024,256]{2,1,0:T(8,128)(2,1)S(1)} %pad_maximum_fusion.2) | copy-start | bytes 3145732
  289.6 116.3 %copy-start.9 = (bf16[1,1024,1472]{1,2,0:T(8,128)(2,1)S(1)}, bf16[1,1024,1472]{1,2,0:T(8,128)(2,1)}, u32[]{:S(2)}) copy-start(bf16[1,1024,1472]{1,2,0:T(8,128)(2,1)} %param.15) | copy-start | bytes 9043972
  404.3 8.7 copy-start.1
  404.4 14.7 %copy-start.15 = (bf16[16,64,256]{2,1,0:T(8,128)(2,1)}, bf16[16,64,256]{2,1,0:T(8,128)(2,1)S(1)}, u32[]{:S(2)}) copy-start(bf16[16,64,256]{2,1,0:T(8,128)(2,1)S(1)} %get-tuple-element.156) | copy-start | bytes 1572868
  404.4 13.8 %collective-permute-start.1 = (bf16[1024,256]{1,0:T(8,128)(2,1)S(1)}, bf16[1024,256]{1,0:T(8,128)(2,1)S(1)}, u32[]{:S(2)}, u32[]{:S(2)}) collective-permute-start(bf16[1024,256]{1,0:T(8,128)(2,1)S(1)} %bitcast.203), channel_id=1, source_target_pairs={{0,4},{4,0},{1,5},{5,1},{2,6},{6,2},{3,7},{7,3},{8,12},{12,8},{9,1... | collective-permute-start | bytes 1572872 | tf_op jit(solution)/shard_map/ppermute | solution.py:618
  413.0 70.1 %collective-permute-start.4 = (bf16[896,1472]{0,1:T(8,128)(2,1)}, bf16[896,1472]{0,1:T(8,128)(2,1)}, u32[]{:S(2)}, u32[]{:S(2)}) collective-permute-start(bf16[896,1472]{0,1:T(8,128)(2,1)} %param.22), channel_id=1, source_target_pairs={{0,1},{1,0},{2,3},{3,2},{4,5},{5,4},{6,7},{7,6},{8,9},{9,8},{10,11... | collective-permute-start | bytes 7913480 | tf_op jit(solution)/shard_map/ppermute | solution.py:618
  414.8 19.4 %collective-permute-start.9 = (bf16[1472,896]{1,0:T(8,128)(2,1)}, bf16[1472,896]{1,0:T(8,128)(2,1)}, u32[]{:S(2)}, u32[]{:S(2)}) collective-permute-start(bf16[1472,896]{1,0:T(8,128)(2,1)} %collective-permute-done.6), channel_id=1, source_target_pairs={{0,1},{1,0},{2,3},{3,2},{4,5},{5,4},{6,7},{7,6},{8,9},{9,8},{10,11... | collective-permute-start | bytes 7913480 | tf_op jit(solution)/shard_map/ppermute | solution.py:618
  418.2 21.7 %collective-permute-start.8 = (bf16[1472,896]{1,0:T(8,128)(2,1)}, bf16[1472,896]{1,0:T(8,128)(2,1)}, u32[]{:S(2)}, u32[]{:S(2)}) collective-permute-start(bf16[1472,896]{1,0:T(8,128)(2,1)} %collective-permute-done.5), channel_id=1, source_target_pairs={{0,1},{1,0},{2,3},{3,2},{4,5},{5,4},{6,7},{7,6},{8,9},{9,8},{10,11... | collective-permute-start | bytes 7913480 | tf_op jit(solution)/shard_map/ppermute | solution.py:618
  427.1 143.5 %copy-start.8 = (bf16[1024,1472]{0,1:T(8,128)(2,1)}, bf16[1024,1472]{0,1:T(8,128)(2,1)S(1)}, u32[]{:S(2)}) copy-start(bf16[1024,1472]{0,1:T(8,128)(2,1)S(1)} %multiply_convert_fusion) | copy-start | bytes 9043972
  452.8 96.4 %collective-permute-start.21 = (bf16[1472,896]{1,0:T(8,128)(2,1)S(1)}, bf16[1472,896]{1,0:T(8,128)(2,1)S(1)}, u32[]{:S(2)}, u32[]{:S(2)}) collective-permute-start(bf16[1472,896]{1,0:T(8,128)(2,1)S(1)} %convolution_convert_fusion.5), channel_id=1, source_target_pairs={{0,1},{1,0},{2,3},{3,2},{4,5},{5,4},{6,7},{7,6},{8,9},{9,8},{10,11... | collective-permute-start | bytes 7913480 | tf_op jit(solution)/shard_map/ppermute | solution.py:618
  497.1 79.7 %collective-permute-start.20 = (bf16[1472,896]{1,0:T(8,128)(2,1)S(1)}, bf16[1472,896]{1,0:T(8,128)(2,1)S(1)}, u32[]{:S(2)}, u32[]{:S(2)}) collective-permute-start(bf16[1472,896]{1,0:T(8,128)(2,1)S(1)} %convolution_convert_fusion.6), channel_id=1, source_target_pairs={{0,1},{1,0},{2,3},{3,2},{4,5},{5,4},{6,7},{7,6},{8,9},{9,8},{10,11... | collective-permute-start | bytes 7913480 | tf_op jit(solution)/shard_map/ppermute | solution.py:618
  501.0 69.6 %collective-permute-start.24 = (bf16[1472,896]{1,0:T(8,128)(2,1)S(1)}, bf16[1472,896]{1,0:T(8,128)(2,1)S(1)}, u32[]{:S(2)}, u32[]{:S(2)}) collective-permute-start(bf16[1472,896]{1,0:T(8,128)(2,1)S(1)} %convolution_convert_fusion.3), channel_id=1, source_target_pairs={{0,1},{1,0},{2,3},{3,2},{4,5},{5,4},{6,7},{7,6},{8,9},{9,8},{10,11... | collective-permute-start | bytes 7913480 | tf_op jit(solution)/shard_map/ppermute | solution.py:618
  505.9 142.1 %collective-permute-start.23 = (bf16[1472,896]{1,0:T(8,128)(2,1)}, bf16[1472,896]{1,0:T(8,128)(2,1)}, u32[]{:S(2)}, u32[]{:S(2)}) collective-permute-start(bf16[1472,896]{1,0:T(8,128)(2,1)} %convolution_convert_fusion.4), channel_id=1, source_target_pairs={{0,1},{1,0},{2,3},{3,2},{4,5},{5,4},{6,7},{7,6},{8,9},{9,8},{10,11... | collective-permute-start | bytes 7913480 | tf_op jit(solution)/shard_map/ppermute | solution.py:618
  540.8 8.3 copy-start.58
  552.7 60.1 %collective-permute-start.22 = (bf16[1472,896]{1,0:T(8,128)(2,1)S(1)}, bf16[1472,896]{1,0:T(8,128)(2,1)S(1)}, u32[]{:S(2)}, u32[]{:S(2)}) collective-permute-start(bf16[1472,896]{1,0:T(8,128)(2,1)S(1)} %add_convert_fusion.6), channel_id=1, source_target_pairs={{0,2},{2,0},{1,3},{3,1},{4,6},{6,4},{5,7},{7,5},{8,10},{10,8},{9,1... | collective-permute-start | bytes 7913480 | tf_op jit(solution)/shard_map/ppermute | solution.py:618
  575.1 40.1 %copy-start.21 = (f32[1472]{0:T(1024)S(1)}, f32[1472]{0:T(1024)}, u32[]{:S(2)}) copy-start(f32[1472]{0:T(1024)} %copy-done.20) | copy-start | bytes 17668
  575.1 40.1 %copy-start.23 = (f32[1024]{0:T(1024)S(1)}, f32[1024]{0:T(1024)}, u32[]{:S(2)}) copy-start(f32[1024]{0:T(1024)} %copy-done.22) | copy-start | bytes 12292
  575.1 93.6 %collective-permute-start.25 = (bf16[1472,896]{1,0:T(8,128)(2,1)}, bf16[1472,896]{1,0:T(8,128)(2,1)}, u32[]{:S(2)}, u32[]{:S(2)}) collective-permute-start(bf16[1472,896]{1,0:T(8,128)(2,1)} %add_convert_fusion.4), channel_id=1, source_target_pairs={{0,2},{2,0},{1,3},{3,1},{4,6},{6,4},{5,7},{7,5},{8,10},{10,8},{9,1... | collective-permute-start | bytes 7913480 | tf_op jit(solution)/shard_map/ppermute | solution.py:618
  615.1 21.6 %copy-start.31 = (f32[1024]{0:T(1024)S(1)}, f32[1024]{0:T(1024)}, u32[]{:S(2)}) copy-start(f32[1024]{0:T(1024)} %copy-done.30) | copy-start | bytes 12292
  615.1 298.9 %reduce-scatter.21.cloned.1.call-start = ((), (), s32[]{:S(2)}) async-start(), calls=%async_computation.17 | async-start | bytes 2967552
  648.0 25.5 %copy-start.40 = (bf16[1472,512]{1,0:T(8,128)(2,1)S(1)}, bf16[1472,512]{1,0:T(8,128)(2,1)}, u32[]{:S(2)}) copy-start(bf16[1472,512]{1,0:T(8,128)(2,1)} %all-gather.11.cloned.1.call-done) | copy-start | bytes 4521988
  673.5 267.3 %reduce-scatter.11.cloned.1.call-start = ((), (), s32[]{:S(2)}) async-start(), calls=%async_computation.9 | async-start | bytes 7864320 | tf_op jit(solution)/shard_map/reduce_scatter | solution.py:725
  678.3 16.8 %collective-permute-start.11 = (bf16[1024,256]{1,0:T(8,128)(2,1)S(1)}, bf16[1024,256]{1,0:T(8,128)(2,1)S(1)}, u32[]{:S(2)}, u32[]{:S(2)}) collective-permute-start(bf16[1024,256]{1,0:T(8,128)(2,1)S(1)} %get-tuple-element.155), channel_id=1, source_target_pairs={{0,4},{4,0},{1,5},{5,1},{2,6},{6,2},{3,7},{7,3},{8,12},{12,8},{9,1... | collective-permute-start | bytes 1572872 | tf_op jit(solution)/shard_map/ppermute | solution.py:618
  802.3 207.9 %reduce-scatter.17.cloned.1.call-start = ((), (), s32[]{:S(2)}) async-start(), calls=%async_computation.14 | async-start | bytes 3096576 | tf_op jit(solution)/shard_map/reduce_scatter | solution.py:710
  809.2 5.0 collective-permute-start.27
  812.8 11.4 collective-permute-start.26
  818.8 59.6 %collective-permute-start.28 = (bf16[896,1472]{0,1:T(8,128)(2,1)}, bf16[896,1472]{0,1:T(8,128)(2,1)}, u32[]{:S(2)}, u32[]{:S(2)}) collective-permute-start(bf16[896,1472]{0,1:T(8,128)(2,1)} %add_convert_fusion.2), channel_id=1, source_target_pairs={{0,2},{2,0},{1,3},{3,1},{4,6},{6,4},{5,7},{7,5},{8,10},{10,8},{9,1... | collective-permute-start | bytes 7913480 | tf_op jit(solution)/shard_map/ppermute | solution.py:618
  889.1 185.4 %reduce-scatter.15.cloned.1.call-start = ((), (), s32[]{:S(2)}) async-start(), calls=%async_computation.11 | async-start | bytes 442368 | tf_op jit(solution)/shard_map/reduce_scatter | solution.py:710
  894.9 18.9 %copy-start.37 = (s32[128]{0:T(128)S(1)}, s32[128]{0:T(128)}, u32[]{:S(2)}) copy-start(s32[128]{0:T(128)} %copy-done.36) | copy-start | bytes 1540
  895.9 18.5 %copy-start.34 = (s32[64]{0:T(128)S(1)}, s32[64]{0:T(128)}, u32[]{:S(2)}) copy-start(s32[64]{0:T(128)} %copy-done.33) | copy-start | bytes 772
  895.9 18.7 %copy-start.19 = (pred[192,64]{0,1:T(8,128)(4,1)S(1)}, pred[192,64]{0,1:T(8,128)(4,1)}, u32[]{:S(2)}) copy-start(pred[192,64]{0,1:T(8,128)(4,1)} %copy-done.18) | copy-start | bytes 36868
  895.9 2.0 collective-permute-start.18
  895.9 4.5 collective-permute-start.17
  899.8 11.1 collective-permute-start.19
  913.0 256.9 %all-gather.13.cloned.1.call-start = ((), (), s32[]{:S(2)}) async-start(), calls=%async_computation.12 | async-start | bytes 2967552 | tf_op jit(solution)/shard_map/all_gather | solution.py:711
  913.7 273.8 %all-gather.15.cloned.1.call-start = ((), (), s32[]{:S(2)}) async-start(), calls=%async_computation.13 | async-start | bytes 2967552 | tf_op jit(solution)/shard_map/all_gather | solution.py:711
  914.3 330.1 %all-gather.17.cloned.1.call-start = ((), (), s32[]{:S(2)}) async-start(), calls=%async_computation.15 | async-start | bytes 3096576 | tf_op jit(solution)/shard_map/all_gather | solution.py:711
  939.5 71.2 %collective-permute-start.13 = (bf16[1024,256]{1,0:T(8,128)(2,1)}, bf16[1024,256]{1,0:T(8,128)(2,1)}, u32[]{:S(2)}, u32[]{:S(2)}) collective-permute-start(bf16[1024,256]{1,0:T(8,128)(2,1)} %bitcast.29), channel_id=1, source_target_pairs={{0,4},{4,0},{1,5},{5,1},{2,6},{6,2},{3,7},{7,3},{8,12},{12,8},{9,1... | collective-permute-start | bytes 1572872 | tf_op jit(solution)/shard_map/ppermute | solution.py:618
  943.5 67.2 %copy-start.7 = (bf16[1,1024,1472]{1,2,0:T(8,128)(2,1)S(1)}, bf16[1,1024,1472]{1,2,0:T(8,128)(2,1)}, u32[]{:S(2)}) copy-start(bf16[1,1024,1472]{1,2,0:T(8,128)(2,1)} %param.14) | copy-start | bytes 9043972
  943.5 67.2 %copy-start.27 = (f32[1472]{0:T(1024)S(1)}, f32[1472]{0:T(1024)}, u32[]{:S(2)}) copy-start(f32[1472]{0:T(1024)} %copy-done.26) | copy-start | bytes 17668
  943.5 67.2 %copy-start.29 = (f32[1024]{0:T(1024)S(1)}, f32[1024]{0:T(1024)}, u32[]{:S(2)}) copy-start(f32[1024]{0:T(1024)} %copy-done.28) | copy-start | bytes 12292
  943.5 67.2 %collective-permute-start.12 = (bf16[1024,384]{1,0:T(8,128)(2,1)}, bf16[1024,384]{1,0:T(8,128)(2,1)}, u32[]{:S(2)}, u32[]{:S(2)}) collective-permute-start(bf16[1024,384]{1,0:T(8,128)(2,1)} %get-tuple-element.151), channel_id=1, source_target_pairs={{0,4},{4,0},{1,5},{5,1},{2,6},{6,2},{3,7},{7,3},{8,12},{12,8},{9,1... | collective-permute-start | bytes 2359304 | tf_op jit(solution)/shard_map/ppermute | solution.py:618
  1010.2 299.5 %reduce-scatter.13.cloned.1.call-start = ((), (), s32[]{:S(2)}) async-start(), calls=%async_computation.10 | async-start | bytes 1105920 | tf_op jit(solution)/shard_map/reduce_scatter | solution.py:710
  1034.7 7.1 collective-permute-start.15
  1041.2 66.7 %collective-permute-start.14 = (bf16[368,1280]{1,0:T(8,128)(2,1)}, bf16[368,1280]{1,0:T(8,128)(2,1)}, u32[]{:S(2)}, u32[]{:S(2)}) collective-permute-start(bf16[368,1280]{1,0:T(8,128)(2,1)} %get-tuple-element.130), channel_id=1, source_target_pairs={{0,1},{1,0},{2,3},{3,2},{4,5},{5,4},{6,7},{7,6},{8,9},{9,8},{10,11... | collective-permute-start | bytes 2826248 | tf_op jit(solution)/shard_map/ppermute | solution.py:618
  1044.7 63.2 %collective-permute-start.16 = (bf16[368,1280]{1,0:T(8,128)(2,1)}, bf16[368,1280]{1,0:T(8,128)(2,1)}, u32[]{:S(2)}, u32[]{:S(2)}) collective-permute-start(bf16[368,1280]{1,0:T(8,128)(2,1)} %fusion.56), channel_id=1, source_target_pairs={{0,2},{2,0},{1,3},{3,1},{4,6},{6,4},{5,7},{7,5},{8,10},{10,8},{9,1... | collective-permute-start | bytes 2826248 | tf_op jit(solution)/shard_map/ppermute | solution.py:618
  1111.4 51.2 %copy-start.25 = (f32[1024]{0:T(1024)S(1)}, f32[1024]{0:T(1024)}, u32[]{:S(2)}) copy-start(f32[1024]{0:T(1024)} %copy-done.24) | copy-start | bytes 12292
  (36 other events, 165.0 us)
Sparse Core Ops, SparseCore 0:
  24.5 34.7 all-gather.6
  100.7 115.3 all-gather.8
  218.3 25.7 all-gather.10
  615.2 89.1 reduce-scatter.18
  708.3 80.5 reduce-scatter.20
  802.4 122.5 reduce-scatter.10
  929.1 81.0 reduce-scatter.16
  1014.0 60.3 reduce-scatter.14
  1076.7 54.9 all-gather.12
  1133.8 53.7 all-gather.14
  1189.7 54.6 all-gather.16
  1247.6 62.0 reduce-scatter.12

commit v2 on v1

v2 whole, which is shorter than its diff:
```python
import functools
import math

import jax
import jax.numpy as jnp
from jax import lax
from jax.experimental import pallas as pl
from jax.experimental.pallas import tpu as pltpu
from jax.sharding import Mesh, PartitionSpec as P

HEADS = 6
HDIM = 64
PROMPT = 4096
NCONT = 8
BLK = 64
CONTS = 4096
GROUP = 8192
NBLK = GROUP // BLK
PBLK = PROMPT // BLK
LOG2E = 1.4426950408889634
NEG = -3e30
M_INIT = -1e30
WIN = 3
WK = WIN * BLK
FARB = 16
FK = FARB * BLK
thresholds = [math.ceil(16 * 8 ** (step_t / 16)) for step_t in range(1, 16)]
epsilon = 1e-06
BF = jnp.bfloat16
F32 = jnp.float32
HINT = 1 << 20


def dot_nt(a, b):
    return lax.dot_general(a, b, (((1,), (1,)), ((), ())), preferred_element_type=F32)


def dot_nn(a, b):
    return lax.dot_general(a, b, (((1,), (0,)), ((), ())), preferred_element_type=F32)


def dot_tn(a, b):
    return lax.dot_general(a, b, (((0,), (0,)), ((), ())), preferred_element_type=F32)


class Tab:
    def __init__(self, n):
        self.src = 0
        self.slot = NBLK
        self.blk = NBLK + n
        self.nch = NBLK + 2 * n
        self.zf = NBLK + 3 * n
        self.lim = NBLK + 4 * n
        self.size = NBLK + 5 * n


def lane(shape):
    return lax.broadcasted_iota(jnp.int32, shape, len(shape) - 1)


def sub(shape):
    return lax.broadcasted_iota(jnp.int32, shape, len(shape) - 2)


def stack_super(tab, t, src, dst, base, one, hi):
    low = lane((BLK, 128)) < 64
    for j in range(4):
        blk = src[tab[t.slot + base + j]]
        zero = jnp.zeros_like(blk)
        if one:
            dst[0, j * 64 : (j + 1) * 64, :] = jnp.where(low, zero, blk) if hi else jnp.where(low, blk, zero)
        else:
            u, r = j // 2, (j % 2) * 128
            dst[u, r : r + 64, :] = jnp.where(low, blk, zero)
            dst[u, r + 64 : r + 128, :] = jnp.where(low, zero, blk)


def near_parts(one):
    return [(0, 0), (0, 128)] if one else [(0, 0), (0, 128), (1, 0), (1, 128)]


def near_setup(base, one, z_ref, oo_ref, bias, oh):
    low = lane((WK, 128)) < 64
    for j in range(4):
        oh[j] = (sub((128, 128)) == oo_ref[base + j]).astype(BF)
    spread = lambda h, x: dot_nn(z_ref[0, h], x) + dot_nn(z_ref[1, h], x)
    if one:
        for p in range(2):
            bias[1, p] = spread(0, jnp.where(lane((128, 128)) < 64, oh[2 * p], oh[2 * p + 1]))
    else:
        for j in range(4):
            bias[1, j] = jnp.where(low, spread(0, oh[j]), spread(1, oh[j]))


def near_scalars(tab, t, base, i):
    offs, act = [], []
    for j in range(4):
        b = tab[t.blk + base + j]
        off = jnp.where(i == 0, b - (WIN - 1), jnp.where(i == 1, PBLK - WIN, b - (WIN - 1) - WIN * (i - 1)))
        active = i < tab[t.nch + base + j]
        offs.append(jnp.where(active, off, 0))
        act.append(active)
    return offs, act


def near_low(lo_ref, base, j, i, act):
    lo = lo_ref[base + j]
    lo = jnp.where(i == 1, jnp.zeros_like(lo), lo)
    return jnp.where(act[j], lo, jnp.full_like(lo, 1 << 20))


def near_keep(lo_ref, base, one, x, i, act, offs):
    edge = lambda j: near_low(lo_ref, base, j, i, act) - offs[j] * BLK
    if one:
        return sub((WK, 128)) >= jnp.where(lane((1, 128)) < 64, edge(2 * x), edge(2 * x + 1))
    return sub((WK, 128)) >= edge(x)


def near_dot(kv, wins, one, x, a, b, q):
    if one:
        left, right = [dot_nt(rows_of(kv, wins[2 * x + k], a, b), q) for k in range(2)]
        return jnp.where(lane(left.shape) < 64, left, right)
    return dot_nt(rows_of(kv, wins[x], a, b), q)


def near_dot_t(kv, wins, one, x, a, b, p):
    if one:
        left, right = [dot_tn(rows_of(kv, wins[2 * x + k], a, b), p) for k in range(2)]
        return jnp.where(lane(left.shape) < 64, left, right)
    return dot_tn(rows_of(kv, wins[x], a, b), p)


def near_scores(kv, qst, bias, lo_ref, base, one, i, offs, act, wins):
    kind = jnp.minimum(i, 2)
    out = []
    for x, (u, a) in enumerate(near_parts(one)):
        s = near_dot(kv, wins, one, x, 0, 128, qst[u, a : a + 128, :]) * LOG2E + bias[kind, x]
        out.append(jnp.where(near_keep(lo_ref, base, one, x, i, act, offs), s, NEG))
    return out


def far_mask(tab, t, base, one, u, c, shape):
    pos = c * FK + sub(shape)
    ln = lane(shape)
    lim = lambda j: tab[t.lim + base + j]
    if one:
        low = jnp.where(ln < 64, lim(0), lim(1))
        return pos < jnp.where(ln < 128, low, jnp.where(ln < 192, lim(2), lim(3)))
    return pos < jnp.where(ln < 128, lim(2 * u), lim(2 * u + 1))


def far_counts(tab, t, base):
    lims = [tab[t.lim + base + j] for j in range(4)]
    least = jnp.minimum(jnp.minimum(lims[0], lims[1]), jnp.minimum(lims[2], lims[3]))
    most = jnp.maximum(jnp.maximum(lims[0], lims[1]), jnp.maximum(lims[2], lims[3]))
    return least // FK, (most + FK - 1) // FK


def near_count(tab, t, base):
    ns = [tab[t.nch + base + j] for j in range(4)]
    return jnp.maximum(jnp.maximum(ns[0], ns[1]), jnp.maximum(ns[2], ns[3]))


def blocks_of(tab, t, first, count):
    return [tab[t.src + jnp.maximum(first + i, 0)] for i in range(count)]


def rows_of(ref, blocks, a, b):
    return jnp.concatenate([ref[i, :, a:b] for i in blocks], axis=0)


def transpose_far(tab, t, kv, dst, a, b):
    def step(c, carry):
        x = rows_of(kv, blocks_of(tab, t, c * FARB, FARB), a, b)
        dst[:, pl.ds(pl.multiple_of(c * FK, FK), FK)] = jnp.transpose(x)
        return carry

    lax.fori_loop(0, PROMPT // FK, step, 0)


def start_bias(t_ref, bias):
    for x in range(bias.shape[1]):
        bias[0, x] = t_ref[...]
        bias[2, x] = jnp.zeros((WK, 128), F32)


def give_rows(tab, t, base, one, u, val, dst, hi):
    low = lane((BLK, 128)) < 64
    if one:
        for j in range(4):
            piece = val[j * 64 : (j + 1) * 64]
            zero = jnp.zeros_like(piece)
            dst[tab[t.slot + base + j]] = (jnp.where(low, zero, piece) if hi else jnp.where(low, piece, zero)).astype(BF)
    else:
        for k in range(2):
            r = k * 128
            dst[tab[t.slot + base + 2 * u + k]] = jnp.where(low, val[r : r + 64], val[r + 64 : r + 128]).astype(BF)


def fwd_kernel(n, one, tab, kv, qs, t_ref, z_ref, lo_ref, oo_ref, o_ref, lse_ref, qst, vt, bias, oh, m, l, acc):
    t = Tab(n)
    units = 1 if one else 2
    va, vb = (0, 128) if one else (128, 256)
    transpose_far(tab, t, kv, vt, va, vb)
    start_bias(t_ref, bias)

    def update(at, ss, pv):
        olds = [m[u, :, a:b] for u, a, b in at]
        news = [jnp.maximum(old, jnp.max(s, axis=0, keepdims=True)) for old, s in zip(olds, ss)]
        ps = [jnp.exp2(s - new) for s, new in zip(ss, news)]
        al = [jnp.exp2(old - new) for old, new in zip(olds, news)]
        sums = [jnp.sum(p, axis=0, keepdims=True) for p in ps]
        outs = [pv(x, p.astype(BF)) for x, p in enumerate(ps)]
        for x, (u, a, b) in enumerate(at):
            m[u, :, a:b] = news[x]
            l[u, :, a:b] = l[u, :, a:b] * al[x] + sums[x]
            acc[u, :, a:b] = acc[u, :, a:b] * al[x] + outs[x]

    def super_tile(s_i, carry):
        base = s_i * 4
        stack_super(tab, t, qs, qst, base, one, False)
        m[...] = jnp.full(m.shape, M_INIT, F32)
        l[...] = jnp.zeros(l.shape, F32)
        acc[...] = jnp.zeros(acc.shape, F32)
        n_near = near_count(tab, t, base)

        @pl.when(n_near > 1)
        def _():
            near_setup(base, one, z_ref, oo_ref, bias, oh)

        def near(i, carry):
            offs, act = near_scalars(tab, t, base, i)
            wins = [blocks_of(tab, t, off, WIN) for off in offs]
            ss = near_scores(kv, qst, bias, lo_ref, base, one, i, offs, act, wins)
            at = [(u, a, a + 128) for u, a in near_parts(one)]
            update(at, ss, lambda x, p: near_dot_t(kv, wins, one, x, va, vb, p))
            return carry

        lax.fori_loop(0, n_near, near, 0)

        def far(masked, c, carry):
            k = rows_of(kv, blocks_of(tab, t, c * FARB, FARB), 0, 128)
            ss = [dot_nt(k, qst[u]) * LOG2E for u in range(units)]
            if masked:
                ss = [jnp.where(far_mask(tab, t, base, one, u, c, s.shape), s, NEG) for u, s in enumerate(ss)]
            v = vt[:, pl.ds(pl.multiple_of(c * FK, FK), FK)]
            update([(u, 0, 256) for u in range(units)], ss, lambda x, p: dot_nn(v, p))
            return carry

        n_full, n_far = far_counts(tab, t, base)
        lax.fori_loop(0, n_full, functools.partial(far, False), 0)
        lax.fori_loop(n_full, n_far, functools.partial(far, True), 0)
        for u in range(units):
            lse_ref[s_i, u] = m[u] + jnp.log(l[u]) * LOG2E
            give_rows(tab, t, base, one, u, jnp.transpose(acc[u] / l[u]), o_ref, True)
        return carry

    lax.fori_loop(0, n // 4, super_tile, 0)


def bwd_kernel(n, one, tab, kv, qs, dos, ats, t_ref, z_ref, lo_ref, oo_ref, lse_ref,
               dq_ref, dkv_ref, gt_ref, gz_ref, dkv, qst, dst, qm, dm, kt, bias, oh, gn, dq, delta):
    t = Tab(n)
    units = 1 if one else 2
    va, vb = (0, 128) if one else (128, 256)
    parts = near_parts(one)
    transpose_far(tab, t, kv, kt, 0, 128)
    start_bias(t_ref, bias)

    def clear(p, carry):
        dkv[p] = jnp.zeros(dkv.shape[1:], F32)
        return carry

    lax.fori_loop(0, NBLK, clear, 0)
    gn[...] = jnp.zeros(gn.shape, F32)
    gz_ref[...] = jnp.zeros(gz_ref.shape, F32)

    def add_rows(blocks, a, b, val):
        for i, block in enumerate(blocks):
            dkv[block, :, a:b] += val[i * BLK : (i + 1) * BLK]

    def super_tile(s_i, carry):
        base = s_i * 4
        stack_super(tab, t, qs, qst, base, one, False)
        stack_super(tab, t, dos, dst, base, one, True)
        if one:
            half_rows = sub((128, 128)) < 64
            for x in range(2):
                for src, dst_m in ((qst, qm), (dst, dm)):
                    val = src[0, x * 128 : (x + 1) * 128, :]
                    zero = jnp.zeros_like(val)
                    dst_m[x, 0] = jnp.where(half_rows, val, zero)
                    dst_m[x, 1] = jnp.where(half_rows, zero, val)
        low = lane((BLK, 128)) < 64
        zero = jnp.zeros((BLK, 128), F32)
        prods = []
        for j in range(4):
            slot = tab[t.slot + base + j]
            prods.append(dos[slot].astype(F32) * ats[slot].astype(F32))
        for u in range(units):
            if one:
                stacked = [jnp.where(low, zero, p) for p in prods]
            else:
                stacked = [x for p in prods[2 * u : 2 * u + 2] for x in (jnp.where(low, p, zero), jnp.where(low, zero, p))]
            delta[u] = jnp.sum(jnp.transpose(jnp.concatenate(stacked, axis=0)), axis=0, keepdims=True)
        dq[...] = jnp.zeros(dq.shape, F32)
        n_near = near_count(tab, t, base)

        @pl.when(n_near > 1)
        def _():
            near_setup(base, one, z_ref, oo_ref, bias, oh)

        def near(i, carry):
            offs, act = near_scalars(tab, t, base, i)
            wins = [blocks_of(tab, t, off, WIN) for off in offs]
            ss = near_scores(kv, qst, bias, lo_ref, base, one, i, offs, act, wins)
            dps = [near_dot(kv, wins, one, x, va, vb, dst[u, a : a + 128, :]) for x, (u, a) in enumerate(parts)]
            ps = [jnp.exp2(s - lse_ref[s_i, u, :, a : a + 128]) for s, (u, a) in zip(ss, parts)]
            ds = [(p * (dp - delta[u, :, a : a + 128])).astype(BF) for p, dp, (u, a) in zip(ps, dps, parts)]
            pb = [p.astype(BF) for p in ps]
            dqs = [near_dot_t(kv, wins, one, x, 0, 128, ds[x]) for x in range(len(parts))]
            adds = []
            for x, (u, a) in enumerate(parts):
                if one:
                    for k in range(2):
                        adds.append((wins[2 * x + k], 0, 128, dot_nn(ds[x], qm[x, k]) + dot_nn(pb[x], dm[x, k])))
                else:
                    adds.append((wins[x], 0, 128, dot_nn(ds[x], qst[u, a : a + 128, :])))
                    adds.append((wins[x], va, vb, dot_nn(pb[x], dst[u, a : a + 128, :])))
            for add in adds:
                add_rows(*add)
            for x, (u, a) in enumerate(parts):
                slot = jnp.where(i == 0, 0, jnp.where(i == 1, 1 + x, 1 + len(parts)))
                gn[slot] += ds[x].astype(F32)
                dq[u, :, a : a + 128] += dqs[x]
            return carry

        lax.fori_loop(0, n_near, near, 0)

        @pl.when(n_near > 1)
        def _():
            half = lane((128, 128)) < 64
            none = jnp.zeros((128, 128), BF)
            for x in range(len(parts)):
                g = gn[1 + x].astype(BF)
                if one:
                    gz_ref[0] += dot_nt(g, jnp.where(half, oh[2 * x], oh[2 * x + 1]))
                else:
                    gz_ref[0] += dot_nt(g, jnp.where(half, oh[x], none))
                    gz_ref[1] += dot_nt(g, jnp.where(half, none, oh[x]))
                gn[1 + x] = jnp.zeros((WK, 128), F32)

        def far(masked, c, carry):
            blocks = blocks_of(tab, t, c * FARB, FARB)
            k = rows_of(kv, blocks, 0, 128)
            v = k if one else rows_of(kv, blocks, va, vb)
            ss = [dot_nt(k, qst[u]) * LOG2E for u in range(units)]
            dps = [dot_nt(v, dst[u]) for u in range(units)]
            if masked:
                ss = [jnp.where(far_mask(tab, t, base, one, u, c, s.shape), s, NEG) for u, s in enumerate(ss)]
            ps = [jnp.exp2(s - lse_ref[s_i, u]) for u, s in enumerate(ss)]
            ds = [(p * (dp - delta[u])).astype(BF) for u, (p, dp) in enumerate(zip(ps, dps))]
            pb = [p.astype(BF) for p in ps]
            if one:
                add_rows(blocks, 0, 128, dot_nn(ds[0], qst[0]) + dot_nn(pb[0], dst[0]))
            else:
                add_rows(blocks, 0, 128, dot_nn(ds[0], qst[0]) + dot_nn(ds[1], qst[1]))
                add_rows(blocks, va, vb, dot_nn(pb[0], dst[0]) + dot_nn(pb[1], dst[1]))
            for u in range(units):
                dq[u] += dot_nn(kt[:, pl.ds(pl.multiple_of(c * FK, FK), FK)], ds[u])
            return carry

        n_full, n_far = far_counts(tab, t, base)
        lax.fori_loop(0, n_full, functools.partial(far, False), 0)
        lax.fori_loop(n_full, n_far, functools.partial(far, True), 0)
        for u in range(units):
            give_rows(tab, t, base, one, u, jnp.transpose(dq[u]), dq_ref, False)
        return carry

    lax.fori_loop(0, n // 4, super_tile, 0)
    gt_ref[...] = gn[0]

    def give(p, carry):
        dkv_ref[p] = dkv[p].astype(BF)
        return carry

    lax.fori_loop(0, NBLK, give, 0)


VM = pl.BlockSpec(memory_space=pltpu.VMEM)
HB = pl.BlockSpec(memory_space=pl.ANY)
SM = pl.BlockSpec(memory_space=pltpu.SMEM)


def attn_fwd(one, tab, kv, q, t_tab, z_tab, lo, oo):
    n = q.shape[0]
    units, parts = (1, 2) if one else (2, 4)
    return pl.pallas_call(
        functools.partial(fwd_kernel, n, one),
        out_shape=(
            jax.ShapeDtypeStruct((n, BLK, 128), BF),
            jax.ShapeDtypeStruct((n // 4, units, 1, 256), F32),
        ),
        in_specs=[SM] + [VM] * 6,
        out_specs=(VM, VM),
        scratch_shapes=[
            pltpu.VMEM((units, 256, 128), BF),
            pltpu.VMEM((128, PROMPT), BF),
            pltpu.VMEM((3, parts, WK, 128), F32),
            pltpu.VMEM((4, 128, 128), BF),
            pltpu.VMEM((units, 1, 256), F32),
            pltpu.VMEM((units, 1, 256), F32),
            pltpu.VMEM((units, 128, 256), F32),
        ],
        compiler_params=pltpu.CompilerParams(vmem_limit_bytes=30 << 20),
        cost_estimate=pl.CostEstimate(flops=HINT, bytes_accessed=HINT, transcendentals=0),
        name="attn_fwd_one" if one else "attn_fwd_two",
    )(tab, kv, q, t_tab, z_tab, lo, oo)


def attn_bwd(one, tab, kv, q, do, at, t_tab, z_tab, lo, oo, lse):
    n = q.shape[0]
    units, parts = (1, 2) if one else (2, 4)
    lanes = kv.shape[2]
    masked = (2, 2, 128, 128) if one else (1, 1, 16, 128)
    return pl.pallas_call(
        functools.partial(bwd_kernel, n, one),
        out_shape=(
            jax.ShapeDtypeStruct((n, BLK, 128), BF),
            jax.ShapeDtypeStruct((NBLK, BLK, lanes), BF),
            jax.ShapeDtypeStruct((WK, 128), F32),
            jax.ShapeDtypeStruct((units, WK, 128), F32),
        ),
        in_specs=[SM] + [VM] * 9,
        out_specs=(VM, VM, VM, VM),
        scratch_shapes=[
            pltpu.VMEM((NBLK, BLK, lanes), F32),
            pltpu.VMEM((units, 256, 128), BF),
            pltpu.VMEM((units, 256, 128), BF),
            pltpu.VMEM(masked, BF),
            pltpu.VMEM(masked, BF),
            pltpu.VMEM((128, PROMPT), BF),
            pltpu.VMEM((3, parts, WK, 128), F32),
            pltpu.VMEM((4, 128, 128), BF),
            pltpu.VMEM((2 + parts, WK, 128), F32),
            pltpu.VMEM((units, 128, 256), F32),
            pltpu.VMEM((units, 1, 256), F32),
        ],
        compiler_params=pltpu.CompilerParams(vmem_limit_bytes=44 << 20),
        cost_estimate=pl.CostEstimate(flops=HINT, bytes_accessed=HINT, transcendentals=0),
        name="attn_bwd_one" if one else "attn_bwd_two",
    )(tab, kv, q, do, at, t_tab, z_tab, lo, oo, lse)


def bucket_of(distance):
    distance = jnp.maximum(distance, 0)
    far_bucket = jnp.full(distance.shape, 16, jnp.int32)
    for threshold in thresholds:
        far_bucket = far_bucket + (distance >= threshold).astype(jnp.int32)
    return jnp.where(distance < 16, distance, far_bucket)


def near_distance():
    diag = (WIN - 1) * BLK + jnp.arange(BLK)[None, :] - jnp.arange(WK)[:, None]
    tail = WK + jnp.arange(128)[None, :] - jnp.arange(WK)[:, None]
    return diag.astype(jnp.int32), tail.astype(jnp.int32)


def bias_tables(table):
    last = table.shape[0] - 1
    rel = (table - table[last:]) * LOG2E
    diag, tail = near_distance()

    def pick(dist):
        bucket = bucket_of(dist)
        out = jnp.zeros((3,) + dist.shape, F32)
        for b in range(last):
            out = jnp.where(bucket[None] == b, rel[b][:, None, None], out)
        return out

    d = jnp.where(diag[None] >= 0, pick(diag), NEG)
    z = pick(tail)
    two, one = jnp.concatenate([d[0], d[1]], axis=1), jnp.concatenate([d[2], d[2]], axis=1)
    z_hi = z.astype(BF)
    z_lo = (z - z_hi.astype(F32)).astype(BF)
    z = jnp.stack([z_hi, z_lo])
    return (two, z[:, :2]), (one, z[:, 2:])


def bias_grads(gt_two, gz_two, gt_one, gz_one, buckets):
    diag, tail = near_distance()
    gd = jnp.stack([gt_two[:, :64], gt_two[:, 64:], gt_one[:, :64] + gt_one[:, 64:]])
    gz = jnp.concatenate([gz_two, gz_one])
    bd, bt = bucket_of(diag), bucket_of(tail)
    labels = jnp.arange(buckets - 1, dtype=jnp.int32)[:, None, None, None]
    seen = diag >= 0
    one = jnp.sum(jnp.where((bd[None, None] == labels) & seen[None, None], gd[None], 0.0), axis=(2, 3))
    two = jnp.sum(jnp.where(bt[None, None] == labels, gz[None], 0.0), axis=(2, 3))
    near = one + two
    return jnp.concatenate([near, -jnp.sum(near, axis=0, keepdims=True)], axis=0)


def plan(deal_table, seg_row, ctx, nb):
    n = 2 * nb
    par = ctx % 2
    slot = jnp.arange(NBLK, dtype=jnp.int32)
    owner = slot // nb
    where_kv = ((owner // 2) * 2 + (owner % 2 + par) % 2) * nb + slot % nb
    src = jnp.sum(jnp.where(deal_table[None, :] == slot[:, None], where_kv[None, :], 0), axis=1)
    own = lax.dynamic_slice_in_dim(deal_table, ctx * nb, nb)
    other = lax.dynamic_slice_in_dim(deal_table, (ctx + 1 - 2 * par) * nb, nb)
    rb = jnp.concatenate([own, other])
    rank = jnp.sum((rb[None, :] < rb[:, None]).astype(jnp.int32), axis=1)
    pos = jnp.arange(n, dtype=jnp.int32)
    pick = (rank[None, :] == pos[:, None]).astype(jnp.int32)
    rslot = jnp.sum(pick * pos[None, :], axis=1)
    rblk = jnp.sum(pick * rb[None, :], axis=1)
    labels = jnp.arange(NCONT, dtype=jnp.int32)
    starts = jnp.sum((seg_row[None, :] < labels[:, None]).astype(jnp.int32), axis=1)
    cpos = rblk[:, None] * BLK + jnp.arange(BLK, dtype=jnp.int32)[None, :] - PROMPT
    ss = jnp.max(jnp.where(starts[None, None, :] <= cpos[:, :, None], starts[None, None, :], 0), axis=2)
    is_cont = rblk >= PBLK
    lo = jnp.where(is_cont[:, None], PROMPT + ss, 0)
    oo = jnp.where(is_cont[:, None], jnp.minimum(cpos - ss, 127), 127)
    first = (PROMPT + ss[:, 0]) // BLK
    more = jnp.maximum(rblk - (WIN - 1) - first, 0)
    nch = jnp.where(is_cont, 2 + (more + WIN - 1) // WIN, 1)
    zf = jnp.zeros_like(nch)
    lim = jnp.where(is_cont, PROMPT - WK, jnp.maximum(rblk - (WIN - 1), 0) * BLK)
    tab = jnp.concatenate([src, rslot, rblk, nch, zf, lim]).astype(jnp.int32)
    dup = lambda x: jnp.concatenate([x, x], axis=1)[:, None, :].astype(jnp.int32)
    return tab, dup(lo), dup(oo)


def gelu_parts(v):
    c = math.sqrt(2 / math.pi)
    sq = v * v
    th = jnp.tanh(c * v * (1 + 0.044715 * sq))
    half = 0.5 * (1 + th)
    return v * half, half + 0.5 * c * v * (1 - th * th) * (1 + 3 * 0.044715 * sq)


def ffn_kernel(h, dy, wga, wgb, wua, wub, wda, wdb, hida, hidb, dga, dgb, dua, dub, *g_refs):
    rows = h.shape[1]
    step = min(256, rows)
    w_in = jnp.transpose(jnp.concatenate([wga[...], wgb[...], wua[...], wub[...]], axis=1))
    w_down = jnp.transpose(jnp.concatenate([wda[...], wdb[...]], axis=1))
    for r in range(0, rows, step):
        both = dot_nn(w_in, h[:, r : r + step])
        d_hidden = dot_nn(w_down, dy[:, r : r + step])
        gate, up = both[:256], both[256:]
        act, slope = gelu_parts(gate)
        for a, b, val in ((hida, hidb, act * up), (dga, dgb, d_hidden * up * slope), (dua, dub, d_hidden * act)):
            val = val.astype(BF)
            a[:, r : r + step] = val[:128]
            b[:, r : r + step] = val[128:]
    for k, (left, a, b) in enumerate(((h, dga, dgb), (h, dua, dub), (dy, hida, hidb))):
        g = dot_nt(left[...], jnp.concatenate([a[...], b[...]], axis=0)).astype(BF)
        g_refs[k][...] = g[:, :128]
        g_refs[k + 3][...] = g[:, 128:]


def ffn_pair(h, dy, gates, ups, downs):
    width, rows = h.shape
    units = gates[0].shape[1]
    whole = pl.BlockSpec((width, rows), lambda i: (0, 0), pipeline_mode=pl.Buffered(1))
    col = pl.BlockSpec((width, 128), lambda i: (0, i))
    act = pl.BlockSpec((128, rows), lambda i: (i, 0))
    return pl.pallas_call(
        ffn_kernel,
        grid=(units // 128,),
        out_shape=[jax.ShapeDtypeStruct((units, rows), BF)] * 6 + [jax.ShapeDtypeStruct((width, units), BF)] * 6,
        in_specs=[whole, whole] + [col] * 6,
        out_specs=[act] * 6 + [col] * 6,
        compiler_params=pltpu.CompilerParams(vmem_limit_bytes=44 << 20),
        cost_estimate=pl.CostEstimate(flops=HINT, bytes_accessed=HINT, transcendentals=0),
        name="ffn_pair",
    )(h, dy, *gates, *ups, *downs)


def each(count, body):
    def step(i, carry):
        body(i)
        return carry

    lax.fori_loop(0, count, step, 0)


def norm_back(x_at, d_at, gain, g_gain, rows, give):
    width = gain.shape[0]
    part = width // 8
    feats = [slice(f * part, (f + 1) * part) for f in range(8)]
    cols = min(256, rows)
    g_gain[...] = jnp.zeros(g_gain.shape, F32)

    def body(i):
        at = pl.ds(pl.multiple_of(i * cols, cols), cols)
        sq = jnp.zeros((1, cols), F32)
        dot = jnp.zeros((1, cols), F32)
        for f in feats:
            x = x_at[f, at].astype(F32)
            sq = sq + jnp.sum(x * x, axis=0, keepdims=True)
            dot = dot + jnp.sum(d_at[f, at] * gain[f, :] * x, axis=0, keepdims=True)
        rs = lax.rsqrt(sq / width + epsilon)
        coef = rs * rs * rs * dot / width
        for f in feats:
            x, d = x_at[f, at].astype(F32), d_at[f, at]
            give(f, at, rs * (d * gain[f, :]) - x * coef)
            g_gain[f, :] += jnp.sum(d * (x * rs), axis=1, keepdims=True)

    each(rows // cols, body)


def ffn_back_kernel(*refs):
    ds, ws = refs[:8], refs[8:16]
    mid_in, dy_in, gain, w_o_in, d_mid, d_branch, d_att, g_gain, dbuf, wbuf, mid, dy, w_o, acc, sems, late = refs[16:]
    slots = dbuf.shape[0]
    shards = len(ds) // 2

    def copies(i):
        s = i % slots
        return [pltpu.make_async_copy(src[i + k * shards], dst.at[s, k], sems.at[s, w, k])
                for k in range(2) for w, (src, dst) in enumerate(((ds, dbuf), (ws, wbuf)))]

    others = [pltpu.make_async_copy(a, b, late.at[i])
              for i, (a, b) in enumerate(((mid_in, mid), (dy_in, dy), (w_o_in, w_o)))]
    for i in range(slots):
        for c in copies(i):
            c.start()
    for c in others:
        c.start()
    rows = mid.shape[1]
    cols = min(512, rows)

    def add(i, s):
        def body(c):
            at = pl.ds(pl.multiple_of(c * cols, cols), cols)
            part = dot_nn(
                jnp.concatenate([wbuf[s, 0], wbuf[s, 1]], axis=1),
                jnp.concatenate([dbuf[s, 0, :, at], dbuf[s, 1, :, at]], axis=0),
            )
            if i == 0:
                acc[:, at] = part
            else:
                acc[:, at] += part

        each(rows // cols, body)

    for i in range(shards):
        s = i % slots
        for c in copies(i):
            c.wait()
        add(i, s)
        if i + slots < shards:
            for c in copies(i + slots):
                c.start()
    for c in others:
        c.wait()

    def give(f, at, val):
        val = dy[f, at].astype(F32) + val
        d_mid[f, at] = val
        d_branch[f, at] = val.astype(BF)

    norm_back(mid, acc, gain, g_gain, rows, give)

    def out(c):
        at = pl.ds(pl.multiple_of(c * cols, cols), cols)
        d_att[at, :] = dot_tn(d_branch[:, at], w_o[...]).astype(BF)

    each(rows // cols, out)


def ffn_back(d_list, w_list, mid, dy, gain, w_o):
    width, rows = mid.shape
    units = d_list[0].shape[0]
    return pl.pallas_call(
        ffn_back_kernel,
        out_shape=(
            jax.ShapeDtypeStruct((width, rows), F32),
            jax.ShapeDtypeStruct((width, rows), BF),
            jax.ShapeDtypeStruct((rows, w_o.shape[1]), BF),
            jax.ShapeDtypeStruct((width, 1), F32),
        ),
        in_specs=[HB] * 18 + [VM, HB],
        out_specs=(VM, VM, VM, VM),
        scratch_shapes=[
            pltpu.VMEM((2, 2, units, rows), BF),
            pltpu.VMEM((2, 2, width, units), BF),
            pltpu.VMEM((width, rows), F32),
            pltpu.VMEM((width, rows), BF),
            pltpu.VMEM(w_o.shape, BF),
            pltpu.VMEM((width, rows), F32),
            pltpu.SemaphoreType.DMA((2, 2, 2)),
            pltpu.SemaphoreType.DMA((3,)),
        ],
        compiler_params=pltpu.CompilerParams(vmem_limit_bytes=58 << 20),
        cost_estimate=pl.CostEstimate(flops=HINT, bytes_accessed=HINT, transcendentals=0),
        name="ffn_back",
    )(*d_list, *w_list, mid, dy, gain, w_o)


def in_back_kernel(d_qkv, w_qkv, x, h, gain, d_mid, extra, in_grad, g_qkv, acc, g_gain):
    width, rows = x.shape
    cols = min(256, rows)

    def grads(c):
        at = pl.ds(pl.multiple_of(c * 256, 256), 256)
        g_qkv[:, at] = dot_nn(h[...], d_qkv[:, at]).astype(BF)

    each(d_qkv.shape[1] // 256, grads)

    def back(c):
        at = pl.ds(pl.multiple_of(c * cols, cols), cols)
        acc[:, at] = dot_nt(w_qkv[...], d_qkv[at, :])

    each(rows // cols, back)

    def give(f, at, val):
        in_grad[f, at] = (d_mid[f, at] + val).astype(BF)

    norm_back(x, acc, gain, g_gain, rows, give)
    ln = lane((width, 128))
    spare = jnp.where(ln == 64, g_gain[...], extra[...])
    g_qkv[:, 512:640] = jnp.where(ln < 64, g_qkv[:, 512:640].astype(F32), spare).astype(BF)


def in_back(d_qkv, w_qkv, x, h, gain, d_mid, extra):
    width, rows = x.shape
    return pl.pallas_call(
        in_back_kernel,
        out_shape=(
            jax.ShapeDtypeStruct((width, rows), BF),
            jax.ShapeDtypeStruct((width, d_qkv.shape[1]), BF),
        ),
        in_specs=[VM] * 7,
        out_specs=(VM, VM),
        scratch_shapes=[pltpu.VMEM((width, rows), F32), pltpu.VMEM((width, 1), F32)],
        compiler_params=pltpu.CompilerParams(vmem_limit_bytes=56 << 20),
        cost_estimate=pl.CostEstimate(flops=HINT, bytes_accessed=HINT, transcendentals=0),
        name="in_back",
    )(d_qkv, w_qkv, x, h, gain, d_mid, extra)


def pack_kernel(par, w_q, w_k, w_v, w_o, norms, table, qkv_out, o_out):
    low = lane((w_q.shape[0], 128)) < 64
    even = par[0] == 0
    tiles = lambda w: [w[:, i : i + 128].astype(F32) for i in (0, 128, 256)]
    turn = lambda v: pltpu.roll(v, 64, 1)

    def heads(w):
        a, b, c = tiles(w)
        return (a, b, turn(b)), (jnp.where(low, turn(b), turn(c)), turn(c), c)

    def packs(w):
        one, two = heads(w)
        choose = lambda x, y: jnp.where(even, x, y)
        return [tuple(choose(x, y) for x, y in zip(one, two)), tuple(choose(y, x) for x, y in zip(one, two))]

    spare = dot_tn(norms[...], (lane((8, 128)) == sub((8, 128)) + 64).astype(BF))
    pad = jnp.zeros((w_q.shape[0] - table.shape[0], 128), F32)
    spare = spare + jnp.concatenate([table[...], pad], axis=0)
    q, k, v, o = packs(w_q), packs(w_k), packs(w_v), packs(w_o)
    for p in range(2):
        third = jnp.where(low, q[p][1], spare if p == 0 else jnp.zeros_like(spare))
        for i, val in enumerate((k[p][0], v[p][0], q[p][0], jnp.where(low, k[p][1], v[p][2]), third)):
            qkv_out[:, p * 640 + i * 128 : p * 640 + (i + 1) * 128] = val.astype(BF)
        o_out[:, p * 256 : p * 256 + 128] = o[p][0].astype(BF)
        o_out[:, p * 256 + 128 : (p + 1) * 256] = jnp.where(low, jnp.zeros_like(spare), o[p][2]).astype(BF)


def pack(par, w_q, w_k, w_v, w_o, norm_attn, norm_ffn, rel_bias):
    share = w_q.shape[0]
    norms = jnp.pad(jnp.stack([norm_attn, norm_ffn]), ((0, 6), (0, 0)))
    rows = rel_bias.shape[0]
    table = jnp.pad(rel_bias.astype(F32), ((0, (-rows) % 8), (66, 128 - 66 - rel_bias.shape[1])))
    return pl.pallas_call(
        pack_kernel,
        out_shape=(jax.ShapeDtypeStruct((share, 1280), BF), jax.ShapeDtypeStruct((share, 512), BF)),
        in_specs=[SM] + [VM] * 6,
        out_specs=(VM, VM),
        cost_estimate=pl.CostEstimate(flops=HINT, bytes_accessed=HINT, transcendentals=0),
        name="pack",
    )(par.reshape(1), w_q, w_k, w_v, w_o, norms, table)


def swap(x, axis):
    return lax.ppermute(x, axis, [(0, 1), (1, 0)])


def pick_half(par, even, odd):
    return jnp.where(par == 0, even, odd)


def up32(x):
    return x.astype(F32)


def rms_cols(x, gain):
    return x * lax.rsqrt(jnp.mean(x * x, axis=0, keepdims=True) + epsilon) * gain


def after(*values):
    return lax.optimization_barrier(values)


def ctx_bits(cz, par, steps):
    out = [(par, lambda x: swap(x, "cy"))]
    bit = 1
    while bit < steps:
        perm = [(i, i ^ bit) for i in range(steps)]
        out.append(((cz // bit) % 2, lambda x, perm=perm: lax.ppermute(x, "cz", perm)))
        bit *= 2
    return out


def split_by(v, bit):
    half = v.shape[0] // 2
    return pick_half(bit, v[:half], v[half:]), pick_half(bit, v[half:], v[:half])


def ctx_scatter(v, bits):
    for bit, move in bits:
        keep, send = split_by(v, bit)
        v = up32(keep) + up32(move(send.astype(BF)))
    return v.astype(BF)


def ctx_gather(v, bits):
    for bit, move in reversed(bits):
        other = move(v)
        v = jnp.concatenate([pick_half(bit, v, other), pick_half(bit, other, v)])
    return v


def on_device(
    layer_in, out_grad, w_query, w_key, w_value, w_out, w_gate, w_up, w_down,
    norm_attn, norm_ffn, rel_bias, deal_table, seg_ids,
):
    _, rows, width = layer_in.shape
    nb = rows // BLK
    cz, par = lax.axis_index("cz"), lax.axis_index("cy")
    steps = lax.axis_size("cz")
    ctx = cz * 2 + par
    share = w_query.shape[0]
    fs = ("fx", "fc")
    shards = width // share
    bits = ctx_bits(cz, par, steps)

    w_qkv, w_o = pack(par, w_query, w_key, w_value, jnp.transpose(w_out), norm_attn, norm_ffn, rel_bias)
    w_qkv = lax.all_gather(w_qkv, fs, axis=0, tiled=True)
    gain_attn = up32(w_qkv[:, 576:577])
    gain_ffn = up32(w_qkv[:, 577:578])
    bias_rows = rel_bias.shape[0]
    table = w_qkv.reshape(shards, share, 1280)[:, :bias_rows, 578 : 578 + HEADS]
    table = up32(table.reshape(shards * bias_rows, HEADS))
    my_table = pick_half(par, table[:, :3], table[:, 3:])

    own_w = (w_gate, w_up, jnp.transpose(w_down))
    w_qkv, w_o, *sent = after(w_qkv, w_o, *own_w)
    w_o = lax.all_gather(w_o, fs, axis=0, tiled=True)
    quarter = width // 4
    pieces = [swap(sent[2][i * quarter : j * quarter], "fx") for i, j in ((0, 1), (1, 2), (2, 4))]
    far_w = [swap(w, "fx") for w in sent[:2]]

    x = jnp.transpose(layer_in.reshape(rows, width))
    dy = jnp.transpose(out_grad.reshape(rows, width))
    h1 = rms_cols(up32(x), gain_attn).astype(BF)
    qkv = dot_tn(h1, w_qkv).astype(BF)
    two, one = qkv[:, :384], qkv[:, 384:640]
    other, pieces[0] = after(swap(qkv[:, 640:1024], "cy"), pieces[0])
    two = jnp.stack([two, other])
    other, pieces[1] = after(swap(qkv[:, 1024:], "cy"), pieces[1])
    one = jnp.stack([one, other])
    blocks = lambda v: v.reshape(2 * nb, BLK, v.shape[-1])
    gather = lambda v: lax.all_gather(v, "cz", axis=0, tiled=True).reshape(NBLK, BLK, v.shape[-1])
    kv2, q2 = gather(two[:, :, :256]), blocks(two[:, :, 256:])
    kv1, q1 = gather(one[:, :, :128]), blocks(one[:, :, 128:])
    tab, lo, oo = plan(deal_table, seg_ids[0], ctx, nb)
    bias2, bias1 = bias_tables(my_table)
    att2, lse2 = attn_fwd(False, tab, kv2, q2, *bias2, lo, oo)
    kv1, att2 = after(kv1, att2)
    att1, lse1 = attn_fwd(True, tab, kv1, q1, *bias1, lo, oo)
    halves2, halves1 = att2.reshape(2, rows, 128), att1.reshape(2, rows, 128)
    halves1, pair2, *far_w = after(halves1, swap(halves2[1], "cy"), *far_w, *pieces)
    far_w = far_w[:2] + [jnp.concatenate(far_w[2:])]
    att_rows = jnp.concatenate([halves2[0], halves1[0], pair2, swap(halves1[1], "cy")], axis=1)
    core_w = [swap(w, "fc") for w in own_w]
    last_w = [swap(w, "fc") for w in far_w]
    weights = list(zip(own_w, core_w, far_w, last_w))

    mid = up32(x) + dot_nt(w_o, att_rows)
    h2 = rms_cols(mid, gain_ffn).astype(BF)
    o_far = ffn_pair(h2, dy, *[w[2:] for w in weights])
    total = mid
    for r in (2, 3):
        total = total + dot_nn(weights[2][r], o_far[r - 2])
    fold = lambda o, k: up32(o[6 + k]) + up32(swap(o[9 + k], "fc"))
    far_g = [fold(o_far, k) for k in range(3)]
    cut = 2 * width // 3 // 16 * 16
    gate_far = far_g[0].astype(BF)
    to_x = [gate_far[:cut], gate_far[cut:], far_g[1].astype(BF)]
    keep_d, send_d = split_by(far_g[2], par)
    h2, total, keep_d, send_d, *to_x = after(h2, total, keep_d.astype(BF), send_d.astype(BF), *to_x)
    far_d = swap(send_d, "cy")
    gate_a, gate_b, far_up = [swap(g, "fx") for g in to_x]
    o_near = ffn_pair(h2, dy, *[w[:2] for w in weights])
    *o_near, far_d, gate_a = after(*o_near, far_d, gate_a)
    far_d = swap((up32(keep_d) + up32(far_d)).astype(BF), "fx")
    near_g = [fold(o_near, k) for k in range(3)]
    keep_d, send_d = split_by(near_g[2], par)
    near_d = swap(send_d.astype(BF), "cy")
    d_lists = [o_near[2], o_near[3], o_far[2], o_far[3], o_near[4], o_near[5], o_far[4], o_far[5]]
    w_lists = list(weights[0]) + list(weights[1])
    d_mid, d_branch, d_att, g_gain_ffn = ffn_back(d_lists, w_lists, mid, dy, gain_ffn, w_o)
    for r in (0, 1):
        total = total + dot_nn(weights[2][r], o_near[r])
    layer_out = jnp.transpose(total.astype(BF)).reshape(layer_in.shape)

    do1 = blocks(jnp.stack([d_att[:, 128:256], swap(d_att[:, 384:], "cy")]))
    do2 = blocks(jnp.stack([d_att[:, :128], swap(d_att[:, 256:384], "cy")]))
    do1, do2, far_d, near_d, far_gate = after(do1, do2, far_d, near_d, jnp.concatenate([gate_a, gate_b]))
    half_d = (keep_d + up32(near_d) + up32(far_d)).astype(BF)
    scatter = lambda v, dim: lax.psum_scatter(v, "cz", scatter_dimension=dim, tiled=True)
    piece_d = scatter(half_d, 0)
    keep_gate, send = split_by(near_g[0] + up32(far_gate), par)
    recv_gate = swap(send.astype(BF), "cy")
    dq1, dkv1, gt1, gz1 = attn_bwd(True, tab, kv1, q1, do1, att1, *bias1, lo, oo, lse1)
    dkv1, dq1, piece_d, recv_gate, far_up = after(dkv1, dq1, piece_d, recv_gate, far_up)
    dkv1 = scatter(dkv1.reshape(GROUP, 128), 0)
    half_gate = (keep_gate + up32(recv_gate)).astype(BF)
    piece_gate = scatter(half_gate, 0)
    keep_up, send = split_by(near_g[1] + up32(far_up), par)
    recv_up = swap(send.astype(BF), "cy")
    do2, far_up = after(do2, far_up)
    dq2, dkv2, gt2, gz2 = attn_bwd(False, tab, kv2, q2, do2, att2, *bias2, lo, oo, lse2)
    dkv2, dq2, dkv1, recv_up, piece_gate = after(dkv2, dq2, dkv1, recv_up, piece_gate)
    dkv2 = scatter(dkv2.reshape(GROUP, 256), 0)
    half_up = (keep_up + up32(recv_up)).astype(BF)
    g_out = dot_nn(d_branch, att_rows).astype(BF)
    dq1, dq2 = dq1.reshape(2, rows, 128), dq2.reshape(2, rows, 128)
    other1 = [swap(v, "cy") for v in (dkv1[rows:], dq1[1])]
    other_q2 = swap(dq2[1], "cy")
    dkv2, half_up, piece_d, piece_gate = after(dkv2, half_up, piece_d, piece_gate)
    other2 = [swap(dkv2[rows:], "cy"), other_q2]
    d_qkv = jnp.concatenate(
        [dkv2[:rows], dq2[0], dkv1[:rows], dq1[0]] + other2 + other1, axis=1)
    piece_up = scatter(half_up, 0)
    gather_half = lambda piece: lax.all_gather(piece, "cz", axis=0, tiled=True)

    def whole(half, other):
        return up32(jnp.concatenate([pick_half(par, half, other), pick_half(par, other, half)]))

    g_bias = bias_grads(gt2, gz2, gt1, gz1, table.shape[0])
    zero = jnp.zeros_like(g_bias)
    g_bias = jnp.concatenate([pick_half(par, g_bias, zero), pick_half(par, zero, g_bias)], axis=1)
    spare = jnp.pad(g_bias.reshape(shards, bias_rows, HEADS),
                    ((0, 0), (0, share - bias_rows), (66, 128 - 66 - HEADS))).reshape(width, 128)
    spare = jnp.where(jnp.arange(128)[None, :] == 65, g_gain_ffn, spare)
    in_grad, g_qkv = in_back(d_qkv, w_qkv, x, h1, gain_attn, d_mid, spare)
    in_grad = jnp.transpose(in_grad).reshape(layer_in.shape)

    f_here = lax.axis_index("fx") * 2 + lax.axis_index("fc")

    def fold_attn(g):
        blocks = g.reshape(shards, share, g.shape[1])
        away = lambda r: lax.dynamic_index_in_dim(blocks, f_here ^ r, keepdims=False)
        near = up32(away(0)) + up32(swap(away(1), "fc"))
        far = (up32(away(2)) + up32(swap(away(3), "fc"))).astype(BF)
        own = near + up32(swap(far, "fx"))
        half = g.shape[1] // 2
        own = pick_half(par, own, jnp.concatenate([own[:, half:], own[:, :half]], axis=1))
        return jnp.pad(own, ((0, (-share) % 64), (0, 0)))

    g_out = up32(ctx_gather(ctx_scatter(fold_attn(g_out), bits), bits)[:share])
    half_d = gather_half(piece_d)
    g_qkv, half_d, piece_up = after(g_qkv, half_d, piece_up)
    half_gate, half_up = gather_half(piece_gate), gather_half(piece_up)
    g_qkv, other_d = after(fold_attn(g_qkv), swap(half_d, "cy"))
    g_qkv, other_gate = after(ctx_scatter(g_qkv, bits), swap(half_gate, "cy"))
    g_qkv = up32(ctx_gather(g_qkv, bits)[:share])
    grad_down_t, grad_gate = whole(half_d, other_d), whole(half_gate, other_gate)
    grad_up = whole(half_up, swap(half_up, "cy"))
    cols = lambda g, at: g[:, at : at + HDIM]
    p0, p1 = 0, 640
    grad_key = jnp.concatenate([cols(g_qkv, p + o) for p in (p0, p1) for o in (0, 64, 384)], axis=1)
    grad_value = jnp.concatenate([cols(g_qkv, p + o) for p in (p0, p1) for o in (128, 192, 448)], axis=1)
    grad_query = jnp.concatenate([cols(g_qkv, p + o) for p in (p0, p1) for o in (256, 320, 512)], axis=1)
    grad_out = jnp.transpose(
        jnp.concatenate([cols(g_out, p + o) for p in (0, 256) for o in (0, 64, 192)], axis=1))
    rest = cols(g_qkv, 576) + cols(g_qkv, 1216)
    return (
        layer_out, in_grad, grad_query, grad_key, grad_value, grad_out, grad_gate, grad_up,
        jnp.transpose(grad_down_t), rest[:, 0], rest[:, 1], rest[:bias_rows, 2 : 2 + HEADS],
    )


def solution(mesh):
    devices = mesh.devices
    ctx_size, fsdp_size = mesh.shape["ctx"], mesh.shape["fsdp"]
    split = Mesh(devices.reshape(ctx_size // 2, 2, fsdp_size // 2, 2), ("cz", "cy", "fx", "fc"))
    cs, fs = ("cz", "cy"), ("fx", "fc")
    in_specs = (
        P(fs, cs, None), P(fs, cs, None), P(fs, None), P(fs, None), P(fs, None), P(None, fs),
        P(None, fs), P(None, fs), P(fs, None), P(fs), P(fs), P(fs, None), P(), P(fs, None),
    )
    out_specs = (
        P(fs, cs, None), P(fs, cs, None), P(fs, None), P(fs, None), P(fs, None), P(None, fs),
        P(None, fs), P(None, fs), P(fs, None), P(fs), P(fs), P(fs, None),
    )
    return jax.shard_map(
        on_device, mesh=split, in_specs=in_specs, out_specs=out_specs, check_vma=False
    )
```

time: 1360 us -> 915 us (0.67)
  waiting for transfers between devices: 576 us -> 335 us
  matrix products: 271 us -> 38.1 us
  Pallas kernels: 221 us -> 324 us
  blocking collectives: 103 us -> 0 us
  starting transfers between devices: 21.2 us -> 49.6 us
  local copies, waits for them, and re-layouts: 64.4 us -> 48.5 us
  other arithmetic: 80 us -> 95.7 us
    ppermute x29 -> x48, waiting for transfers between devices: 338 us -> 163 us  [swap(): return lax.ppermute(x, axis, [(0, 1), (1, 0)])]
    dot_general x14 -> x1, matrix products: 119 us -> 4.34 us  [dot_nt(): lax.dot_general(a, b, (((1,), (1,)), ((), ())), preferred_element_type=F32)]
    pallas_call x2 -> x9, Pallas kernels: 221 us -> 324 us  [the longest x2 103 us: attn_bwd(): pl.pallas_call(functools.partial(bwd_kernel, n, one), out_shape=(jax.Shap...]
    reduce_scatter x4 -> x2, waiting for transfers between devices: 138 us -> 42.7 us  [on_device(): lax.psum_scatter(v, 'cz', scatter_dimension=dim, tiled=True)]
    all_gather x2 -> x0, blocking collectives: 64.9 us -> none  [over_ctx(): return lax.all_gather(piece, cs, axis=0, tiled=True).astype(F32)]
    dot_general x14 -> x5, matrix products: 91.7 us -> 29.1 us  [dot_nn(): lax.dot_general(a, b, (((1,), (0,)), ((), ())), preferred_element_type=F32)]
    dot_general x14 -> x1, matrix products: 61 us -> 4.59 us  [dot_tn(): lax.dot_general(a, b, (((0,), (0,)), ((), ())), preferred_element_type=F32)]
    psum x1 -> x0, blocking collectives: 38.4 us -> none  [on_device(): small = lax.psum((g_gain_attn, g_gain_ffn, g_bias), cs + fs)]
  transfers between devices with their start and end apart: 41 -> 68, of which waited for: 16 -> 32; matrix products, arithmetic and copies ran while one was open for 28% -> 15% of each run, Pallas kernels for 16% -> 31%
where the time goes in v2:
time: 915 us; the launch traced here: 907 us
  waiting for transfers between devices  335 us (37%)
  Pallas kernels  324 us (35%)
  other arithmetic  95.7 us (10%)
  starting transfers between devices  49.6 us (5%)
  local copies, waits for them, and re-layouts  48.5 us (5%)
  matrix products  38.1 us (4%)
  between operations  16.2 us (2%)
    ppermute x48, waiting for transfers between devices, swap(): return lax.ppermute(x, axis, [(0, 1), (1, 0)])  163 us
    pallas_call x2, Pallas kernels, attn_bwd(): pl.pallas_call(functools.partial(bwd_kernel, n, one), out_shape=(jax.Shap...  103 us
    pallas_call x2, Pallas kernels, ffn_pair(): pl.pallas_call(ffn_kernel, grid=(units // 128,), out_shape=[jax.ShapeDtyp...  86.9 us
    pallas_call x2, Pallas kernels, attn_fwd(): pl.pallas_call(functools.partial(fwd_kernel, n, one), out_shape=(jax.Shap...  69.9 us
    all_gather x2, waiting for transfers between devices, on_device(): lax.all_gather(v, 'cz', axis=0, tiled=True).reshape(NBLK, BLK, v.shape[-1])  49.7 us
    reduce_scatter x2, waiting for transfers between devices, on_device(): lax.psum_scatter(v, 'cz', scatter_dimension=dim, tiled=True)  42.7 us
    ppermute x8, waiting for transfers between devices, ctx_bits(): lax.ppermute(x, 'cz', perm)  38.2 us
    ppermute x48, starting transfers between devices, swap(): return lax.ppermute(x, axis, [(0, 1), (1, 0)])  38.1 us
  transfers between devices with their start and end apart: 68, of which 32 were waited for; matrix products, arithmetic and copies ran while one was open for 15% of the time, Pallas kernels for 31%

profile of v2, /device:TPU:0, one launch (start us, length us, event | category | flops | bytes accessed | tf_op | source)
XLA Modules:
  0.0 906.6 jit_solution(12535973810381318275)
XLA Ops:
  10.5 2.7 pack.1
  13.3 2.7 fusion
  16.0 32.2 %all-gather.8.cloned.1.call-done.w_qkv = bf16[1472,1280]{1,0:T(8,128)(2,1)} async-done(((bf16[368,1280]{1,0:T(8,128)(2,1)}), bf16[1472,1280]{1,0:T(8,128)(2,1)}) %all-gather.8.cloned.1.call-update) | async-done | bytes 3768336 | tf_op jit(solution)/shard_map/all_gather | solution.py:851
  51.9 4.6 convolution_convert_fusion
  59.7 16.7 %collective-permute-done.3 = bf16[368,896]{1,0:T(8,128)(2,1)S(1)} collective-permute-done((bf16[368,896]{1,0:T(8,128)(2,1)S(1)}, bf16[368,896]{1,0:T(8,128)(2,1)S(1)}, u32[]{:S(2)}, u32[]{:S(2)}) %collective-permute-start.3) | collective-permute-done | bytes 659488 | tf_op jit(solution)/shard_map/ppermute | solution.py:788
  82.7 11.3 %collective-permute-done = bf16[1024,256]{1,0:T(8,128)(2,1)S(1)} collective-permute-done((bf16[1024,256]{1,0:T(8,128)(2,1)S(1)}, bf16[1024,256]{1,0:T(8,128)(2,1)S(1)}, u32[]{:S(2)}, u32[]{:S(2)}) %collective-permute-start) | collective-permute-done | bytes 524320 | tf_op jit(solution)/shard_map/ppermute | solution.py:788
  103.8 2.5 slice.496
  115.4 44.7 %all-gather.14.cloned.1.call-done = bf16[8,1024,256]{2,1,0:T(8,128)(2,1)} async-done(((bf16[2,1024,256]{2,1,0:T(8,128)(2,1)}), bf16[8,1024,256]{2,1,0:T(8,128)(2,1)}) %all-gather.14.cloned.1.call-update) | async-done | bytes 4194320 | tf_op jit(solution)/shard_map/all_gather | solution.py:876
  162.3 39.7 %attn_fwd_two.1 = (bf16[32,64,128]{2,1,0:T(8,128)(2,1)S(1)}, f32[8,2,1,256]{3,2,1,0:T(1,128)S(1)}) custom-call(s32[288]{0:T(512)S(1)} %concatenate.90.tab, bf16[128,64,256]{2,1,0:T(8,128)(2,1)S(1)} %bitcast.136, bf16[32,64,128]{2,1,0:T(8,128)(2,1)S(1)} %bitcast.141, f32[192,128]{1,0:T(8,128)S(1)} %pad_maximum_fusion.19.t_ref, ...), custom_call_target="tpu_custom_call" | custom-call | flops 1048576 | bytes 1048576 | tf_op jit(solution)/shard_map/attn_fwd_two/pallas_call | solution.py:398
  202.1 4.9 all-gather.12.cloned.1.call-done
  209.9 30.2 %attn_fwd_one.1 = (bf16[32,64,128]{2,1,0:T(8,128)(2,1)S(1)}, f32[8,1,1,256]{3,2,1,0:T(1,128)S(1)}) custom-call(s32[288]{0:T(512)S(1)} %concatenate.90.tab, bf16[128,64,128]{2,1,0:T(8,128)(2,1)S(1)} %bitcast.137, bf16[32,64,128]{2,1,0:T(8,128)(2,1)S(1)} %bitcast.139, f32[192,128]{1,0:T(8,128)S(1)} %pad_maximum_fusion.20.t_ref, ...), custom_call_target="tpu_custom_call" | custom-call | flops 1048576 | bytes 1048576 | tf_op jit(solution)/shard_map/attn_fwd_one/pallas_call | solution.py:398
  240.1 17.2 %collective-permute-done.7 = bf16[736,896]{1,0:T(8,128)(2,1)} collective-permute-done((bf16[736,896]{1,0:T(8,128)(2,1)}, bf16[736,896]{1,0:T(8,128)(2,1)}, u32[]{:S(2)}, u32[]{:S(2)}) %collective-permute-start.7) | collective-permute-done | bytes 1318944 | tf_op jit(solution)/shard_map/ppermute | solution.py:788
  259.6 2.5 constant_dynamic-update-slice_fusion.wda
  263.8 7.3 collective-permute-done.8
  271.1 4.3 multiply_reduce_fusion
  275.5 2.5 multiply_convert_fusion.h
  278.0 43.7 %ffn_pair.2 = (bf16[896,1024]{1,0:T(8,128)(2,1)S(1)}, bf16[896,1024]{1,0:T(8,128)(2,1)S(1)}, bf16[896,1024]{1,0:T(8,128)(2,1)S(1)}, bf16[896,1024]{1,0:T(8,128)(...) custom-call(bf16[1472,1024]{1,0:T(8,128)(2,1)} %multiply_convert_fus, ...), custom_call_target="tpu_custom_call" | custom-call | flops 1048576 | bytes 1048576 | tf_op jit(solution)/shard_map/ffn_pair/pallas_call | solution.py:569
  323.0 7.6 fusion.74
  330.6 8.1 add_add_fusion
  338.7 2.6 convert_add_fusion.4
  341.3 2.4 add_convert_fusion.1
  355.1 43.2 %ffn_pair.3 = (bf16[896,1024]{1,0:T(8,128)(2,1)S(1)}, bf16[896,1024]{1,0:T(8,128)(2,1)S(1)}, bf16[896,1024]{1,0:T(8,128)(2,1)S(1)}, bf16[896,1024]{1,0:T(8,128)(...) custom-call(bf16[1472,1024]{1,0:T(8,128)(2,1)} %multiply_convert_fus, ...), custom_call_target="tpu_custom_call" | custom-call | flops 1048576 | bytes 1048576 | tf_op jit(solution)/shard_map/ffn_pair/pallas_call | solution.py:569
  399.9 4.8 add_convert_fusion.5
  407.6 3.1 slice_convert_fusion.1
  410.8 38.0 %ffn_back.1 = (f32[1472,1024]{1,0:T(8,128)}, bf16[1472,1024]{1,0:T(8,128)(2,1)}, bf16[1024,512]{1,0:T(8,128)(2,1)}, f32[1472,1]{1,0:T(8,128)}) custom-call(bf16[896,1024]{1,0:T(8,128)(2,1)} %copy-done.7, bf16[896,1024]{1,0:T(8,128)(2,1)} %copy-done.8, bf16[896,1024]{1,0:T(8,128)(2,1)} %copy-done.4, bf16[896,1024]{1,0:T(8,128)(2,1)} %copy-done.5, ...), custom_call_target="tpu_custom_call" | custom-call | flops 1048576 | bytes 1048576 | tf_op jit(solution)/shard_map/ffn_back/pallas_call | solution.py:677
  452.3 2.9 pad_maximum_fusion
  455.2 4.2 collective-permute-done.20
  460.1 4.3 collective-permute-done.21
  464.4 4.5 add_convert_fusion.4
  469.0 4.2 convert_add_fusion.2
  476.4 40.5 %attn_bwd_one.1 = (bf16[32,64,128]{2,1,0:T(8,128)(2,1)S(1)}, bf16[128,64,128]{2,1,0:T(8,128)(2,1)}, f32[192,128]{1,0:T(8,128)S(1)}, f32[1,192,128]{2,1,0:T(8,128)S(1)}) custom-call(s32[288]{0:T(512)S(1)} %copy-done.22, bf16[128,64,128]{2,1,0:T(8,128)(2,1)S(1)} %bitcast.138, bf16[32,64,128]{2,1,0:T(8,128)(2,1)S(1)} %bitcast.140, ...), custom_call_target="tpu_custom_call" | custom-call | flops 1048576 | bytes 1048576 | tf_op jit(solution)/shard_map/attn_bwd_one/pallas_call | solution.py:426
  519.0 4.4 add_convert_fusion.3
  524.2 4.6 collective-permute-done.29
  528.8 4.2 convert_add_fusion.1
  535.4 62.2 %attn_bwd_two.1 = (bf16[32,64,128]{2,1,0:T(8,128)(2,1)S(1)}, bf16[128,64,256]{2,1,0:T(8,128)(2,1)S(1)}, f32[192,128]{1,0:T(8,128)S(1)}, f32[2,192,128]{2,1,0:T(8,128)S(1)}) custom-call(s32[288]{0:T(512)S(1)} %copy-done.23, bf16[128,64,256]{2,1,0:T(8,128)(2,1)} %bitcast.135, bf16[32,64,128]{2,1,0:T(8,128)(2,1)S(1)} %bitcast.142, ...), custom_call_target="tpu_custom_call" | custom-call | flops 1048576 | bytes 1048576 | tf_op jit(solution)/shard_map/attn_bwd_two/pallas_call | solution.py:426
  599.7 3.6 reduce-scatter.12.cloned.1.call-done
  603.8 3.6 convolution_convert_fusion.1
  611.4 2.9 collective-permute-start.48
  614.9 8.5 collective-permute-done.48
  626.0 5.4 collective-permute-done.49
  633.3 8.8 collective-permute-done.50
  642.2 4.5 add_convert_fusion.2
  646.7 39.1 %reduce-scatter.14.cloned.1.call-done = bf16[2048,256]{1,0:T(8,128)(2,1)} async-done(((bf16[8192,256]{1,0:T(8,128)(2,1)}), bf16[2048,256]{1,0:T(8,128)(2,1)}) %reduce-scatter.14.cloned.1.call-update) | async-done | bytes 1048592 | tf_op jit(solution)/shard_map/reduce_scatter | solution.py:924
  685.9 2.9 collective-permute-start.51
  704.7 11.9 %collective-permute-done.31 = bf16[1024,256]{1,0:T(8,128)(2,1)S(1)} collective-permute-done((bf16[1024,256]{1,0:T(8,128)(2,1)S(1)}, bf16[1024,256]{1,0:T(8,128)(2,1)S(1)}, u32[]{:S(2)}, u32[]{:S(2)}) %collective-permute-start.31) | collective-permute-done | bytes 524320 | tf_op jit(solution)/shard_map/ppermute | solution.py:788
  716.6 5.6 collective-permute-done.32
  722.3 2.8 collective-permute-done.33
  727.6 23.6 %in_back.1 = (bf16[1472,1024]{1,0:T(8,128)(2,1)}, bf16[1472,1280]{1,0:T(8,128)(2,1)}) custom-call(bf16[1024,1280]{1,0:T(8,128)(2,1)} %copy-done.43, bf16[1472,1280]{1,0:T(8,128)(2,1)} %all-gather.8.cloned.1.call-done.w_qkv, bf16[1472,1024]{1,0:T(8,128)(2,1)} %bitcast.155, bf16[1472,1024]{1,0:T(8,128)(2,1)} %copy-done.37, f32[1472,1]{1,0:T(8,128)} %get-tuple-element.275.gain, ...), custom_call_target="tpu_custom_call" | custom-call | flops 1048576 | bytes 1048576 | tf_op jit(solution)/shard_map/in_back/pallas_call | solution.py:730
  752.9 2.5 dynamic-slice_bitcast_fusion.1
  755.4 5.2 fusion.75
  763.0 2.4 fusion.6
  766.9 4.6 fusion.4
  774.6 13.9 %collective-permute-done.37 = bf16[368,1280]{1,0:T(8,128)(2,1)S(1)} collective-permute-done((bf16[368,1280]{1,0:T(8,128)(2,1)}, bf16[368,1280]{1,0:T(8,128)(2,1)S(1)}, u32[]{:S(2)}, u32[]{:S(2)}) %collective-permute-start.37) | collective-permute-done | bytes 942112 | tf_op jit(solution)/shard_map/ppermute | solution.py:788
  790.6 16.8 %collective-permute-done.38 = bf16[736,896]{1,0:T(8,128)(2,1)S(1)} collective-permute-done((bf16[736,896]{1,0:T(8,128)(2,1)S(1)}, bf16[736,896]{1,0:T(8,128)(2,1)S(1)}, u32[]{:S(2)}, u32[]{:S(2)}) %collective-permute-start.38) | collective-permute-done | bytes 1318944 | tf_op jit(solution)/shard_map/ppermute | solution.py:788
  812.8 10.1 %collective-permute-done.39 = bf16[192,1280]{1,0:T(8,128)(2,1)} collective-permute-done((bf16[192,1280]{1,0:T(8,128)(2,1)}, bf16[192,1280]{1,0:T(8,128)(2,1)}, u32[]{:S(2)}, u32[]{:S(2)}) %collective-permute-start.39) | collective-permute-done | bytes 491552 | tf_op jit(solution)/shard_map/ppermute | solution.py:788
  825.6 18.0 %collective-permute-done.40 = bf16[96,1280]{1,0:T(8,128)(2,1)S(1)} collective-permute-done((bf16[96,1280]{1,0:T(8,128)(2,1)S(1)}, bf16[96,1280]{1,0:T(8,128)(2,1)S(1)}, u32[]{:S(2)}, u32[]{:S(2)}) %collective-permute-start.40) | collective-permute-done | bytes 245792 | tf_op jit(solution)/shard_map/ppermute | solution.py:812
  843.8 2.7 convert_bitcast_fusion
  846.5 6.1 all-gather.20.cloned.1.call-done
  856.9 5.5 collective-permute-done.43
  862.6 2.7 maximum_convert_fusion
  865.3 5.1 collective-permute-done.44
  871.0 13.6 %collective-permute-done.55 = bf16[736,896]{1,0:T(8,128)(2,1)S(1)} collective-permute-done((bf16[736,896]{1,0:T(8,128)(2,1)}, bf16[736,896]{1,0:T(8,128)(2,1)S(1)}, u32[]{:S(2)}, u32[]{:S(2)}) %collective-permute-start.55) | collective-permute-done | bytes 1318944 | tf_op jit(solution)/shard_map/ppermute | solution.py:788
  884.9 2.7 maximum_convert_fusion.1
  887.6 6.7 collective-permute-done.45
  (467 shorter events, 133.1 us)
Async XLA Ops:
  7.2 41.0 %all-gather.8.cloned.1.call-start = ((), (), s32[]{:S(2)}) async-start(), calls=%async_computation.5 | async-start | bytes 4710400 | tf_op jit(solution)/shard_map/all_gather | solution.py:851
  13.3 146.9 %all-gather.14.cloned.1.call-start = ((), (), s32[]{:S(2)}) async-start(), calls=%async_computation.8 | async-start | bytes 5242880 | tf_op jit(solution)/shard_map/all_gather | solution.py:876
  56.7 19.8 %collective-permute-start.2 = (bf16[1024,384]{1,0:T(8,128)(2,1)S(1)}, bf16[1024,384]{1,0:T(8,128)(2,1)S(1)}, u32[]{:S(2)}, u32[]{:S(2)}) collective-permute-start(bf16[1024,384]{1,0:T(8,128)(2,1)S(1)} %get-tuple-element.287), channel_id=1, source_target_pairs={{0,4},{4,0},{1,5},{5,1},{2,6},{6,2},{3,7},{7,3},{8,12},{12,8},{9,1... | collective-permute-start | bytes 2359304 | tf_op jit(solution)/shard_map/ppermute | solution.py:788
  59.3 17.0 %collective-permute-start.3 = (bf16[368,896]{1,0:T(8,128)(2,1)S(1)}, bf16[368,896]{1,0:T(8,128)(2,1)S(1)}, u32[]{:S(2)}, u32[]{:S(2)}) collective-permute-start(bf16[368,896]{1,0:T(8,128)(2,1)S(1)} %get-tuple-element.285), channel_id=1, source_target_pairs={{0,2},{2,0},{1,3},{3,1},{4,6},{6,4},{5,7},{7,5},{8,10},{10,8},{9,1... | collective-permute-start | bytes 1978376 | tf_op jit(solution)/shard_map/ppermute | solution.py:788
  79.2 127.8 %all-gather.12.cloned.1.call-start = ((), (), s32[]{:S(2)}) async-start(), calls=%async_computation.7 | async-start | bytes 2621440 | tf_op jit(solution)/shard_map/all_gather | solution.py:876
  79.2 16.2 %collective-permute-start.1 = (bf16[368,896]{1,0:T(8,128)(2,1)S(1)}, bf16[368,896]{1,0:T(8,128)(2,1)S(1)}, u32[]{:S(2)}, u32[]{:S(2)}) collective-permute-start(bf16[368,896]{1,0:T(8,128)(2,1)S(1)} %get-tuple-element.286), channel_id=1, source_target_pairs={{0,2},{2,0},{1,3},{3,1},{4,6},{6,4},{5,7},{7,5},{8,10},{10,8},{9,1... | collective-permute-start | bytes 1978376 | tf_op jit(solution)/shard_map/ppermute | solution.py:788
  80.9 13.0 %collective-permute-start = (bf16[1024,256]{1,0:T(8,128)(2,1)S(1)}, bf16[1024,256]{1,0:T(8,128)(2,1)S(1)}, u32[]{:S(2)}, u32[]{:S(2)}) collective-permute-start(bf16[1024,256]{1,0:T(8,128)(2,1)S(1)} %get-tuple-element.289), channel_id=1, source_target_pairs={{0,4},{4,0},{1,5},{5,1},{2,6},{6,2},{3,7},{7,3},{8,12},{12,8},{9,1... | collective-permute-start | bytes 1572872 | tf_op jit(solution)/shard_map/ppermute | solution.py:788
  96.5 167.3 %all-gather.10.cloned.1.call-start = ((), (), s32[]{:S(2)}) async-start(), calls=%async_computation.6 | async-start | bytes 1884160 | tf_op jit(solution)/shard_map/all_gather | solution.py:861
  106.3 150.9 %collective-permute-start.5 = (bf16[1472,896]{1,0:T(8,128)(2,1)}, bf16[1472,896]{1,0:T(8,128)(2,1)}, u32[]{:S(2)}, u32[]{:S(2)}) collective-permute-start(bf16[1472,896]{1,0:T(8,128)(2,1)} %refs_8_.1), channel_id=1, source_target_pairs={{0,2},{2,0},{1,3},{3,1},{4,6},{6,4},{5,7},{7,5},{8,10},{10,8},{9,1... | collective-permute-start | bytes 7913480 | tf_op jit(solution)/shard_map/ppermute | solution.py:788
  106.6 150.6 %collective-permute-start.6 = (bf16[1472,896]{1,0:T(8,128)(2,1)}, bf16[1472,896]{1,0:T(8,128)(2,1)}, u32[]{:S(2)}, u32[]{:S(2)}) collective-permute-start(bf16[1472,896]{1,0:T(8,128)(2,1)} %refs_12_.1), channel_id=1, source_target_pairs={{0,2},{2,0},{1,3},{3,1},{4,6},{6,4},{5,7},{7,5},{8,10},{10,8},{9,1... | collective-permute-start | bytes 7913480 | tf_op jit(solution)/shard_map/ppermute | solution.py:788
  109.4 147.9 %collective-permute-start.7 = (bf16[736,896]{1,0:T(8,128)(2,1)}, bf16[736,896]{1,0:T(8,128)(2,1)}, u32[]{:S(2)}, u32[]{:S(2)}) collective-permute-start(bf16[736,896]{1,0:T(8,128)(2,1)} %slice.496), channel_id=1, source_target_pairs={{0,2},{2,0},{1,3},{3,1},{4,6},{6,4},{5,7},{7,5},{8,10},{10,8},{9,1... | collective-permute-start | bytes 3956744 | tf_op jit(solution)/shard_map/ppermute | solution.py:788
  109.7 409.3 %reduce-scatter.16.cloned.1.call-start = ((), (), s32[]{:S(2)}) async-start(), calls=%async_computation.14 | async-start | bytes 1648640
  207.0 50.2 %collective-permute-start.4 = (bf16[1024,128]{1,0:T(8,128)(2,1)S(1)}, bf16[1024,128]{1,0:T(8,128)(2,1)S(1)}, u32[]{:S(2)}, u32[]{:S(2)}) collective-permute-start(bf16[1024,128]{1,0:T(8,128)(2,1)S(1)} %bitcast.179), channel_id=1, source_target_pairs={{0,4},{4,0},{1,5},{5,1},{2,6},{6,2},{3,7},{7,3},{8,12},{12,8},{9,1... | collective-permute-start | bytes 786440 | tf_op jit(solution)/shard_map/ppermute | solution.py:788
  257.3 20.7 %collective-permute-start.9 = (bf16[1472,896]{1,0:T(8,128)(2,1)}, bf16[1472,896]{1,0:T(8,128)(2,1)}, u32[]{:S(2)}, u32[]{:S(2)}) collective-permute-start(bf16[1472,896]{1,0:T(8,128)(2,1)} %collective-permute-done.5.wga.refs_10_), channel_id=1, source_target_pairs={{0,1},{1,0},{2,3},{3,2},{4,5},{5,4},{6,7},{7,6},{8,9},{9,8},{10,11... | collective-permute-start | bytes 7913480 | tf_op jit(solution)/shard_map/ppermute | solution.py:788
  257.4 20.7 %collective-permute-start.10 = (bf16[1472,896]{1,0:T(8,128)(2,1)}, bf16[1472,896]{1,0:T(8,128)(2,1)}, u32[]{:S(2)}, u32[]{:S(2)}) collective-permute-start(bf16[1472,896]{1,0:T(8,128)(2,1)} %collective-permute-done.6.wua.refs_14_), channel_id=1, source_target_pairs={{0,1},{1,0},{2,3},{3,2},{4,5},{5,4},{6,7},{7,6},{8,9},{9,8},{10,11... | collective-permute-start | bytes 7913480 | tf_op jit(solution)/shard_map/ppermute | solution.py:788
  262.1 15.9 %collective-permute-start.11 = (bf16[1472,896]{1,0:T(8,128)(2,1)}, bf16[1472,896]{1,0:T(8,128)(2,1)}, u32[]{:S(2)}, u32[]{:S(2)}) collective-permute-start(bf16[1472,896]{1,0:T(8,128)(2,1)} %constant_dynamic-update-slice_fusion.wda), channel_id=1, source_target_pairs={{0,1},{1,0},{2,3},{3,2},{4,5},{5,4},{6,7},{7,6},{8,9},{9,8},{10,11... | collective-permute-start | bytes 7913480 | tf_op jit(solution)/shard_map/ppermute | solution.py:788
  262.3 8.8 collective-permute-start.8
  321.8 16.9 %collective-permute-start.12 = (bf16[1472,896]{1,0:T(8,128)(2,1)}, bf16[1472,896]{1,0:T(8,128)(2,1)}, u32[]{:S(2)}, u32[]{:S(2)}) collective-permute-start(bf16[1472,896]{1,0:T(8,128)(2,1)} %get-tuple-element.147), channel_id=1, source_target_pairs={{0,1},{1,0},{2,3},{3,2},{4,5},{5,4},{6,7},{7,6},{8,9},{9,8},{10,11... | collective-permute-start | bytes 7913480 | tf_op jit(solution)/shard_map/ppermute | solution.py:788
  321.9 19.5 %collective-permute-start.13 = (bf16[1472,896]{1,0:T(8,128)(2,1)}, bf16[1472,896]{1,0:T(8,128)(2,1)}, u32[]{:S(2)}, u32[]{:S(2)}) collective-permute-start(bf16[1472,896]{1,0:T(8,128)(2,1)} %get-tuple-element.149), channel_id=1, source_target_pairs={{0,1},{1,0},{2,3},{3,2},{4,5},{5,4},{6,7},{7,6},{8,9},{9,8},{10,11... | collective-permute-start | bytes 7913480 | tf_op jit(solution)/shard_map/ppermute | solution.py:788
  322.4 28.2 %collective-permute-start.17 = (bf16[1472,896]{1,0:T(8,128)(2,1)}, bf16[1472,896]{1,0:T(8,128)(2,1)S(1)}, u32[]{:S(2)}, u32[]{:S(2)}) collective-permute-start(bf16[1472,896]{1,0:T(8,128)(2,1)} %bitcast.160), channel_id=1, source_target_pairs={{0,1},{1,0},{2,3},{3,2},{4,5},{5,4},{6,7},{7,6},{8,9},{9,8},{10,11... | collective-permute-start | bytes 7913480 | tf_op jit(solution)/shard_map/ppermute | solution.py:788
  322.4 28.2 %collective-permute-start.15 = (bf16[1472,896]{1,0:T(8,128)(2,1)}, bf16[1472,896]{1,0:T(8,128)(2,1)S(1)}, u32[]{:S(2)}, u32[]{:S(2)}) collective-permute-start(bf16[1472,896]{1,0:T(8,128)(2,1)} %refs_8_.1), channel_id=1, source_target_pairs={{0,1},{1,0},{2,3},{3,2},{4,5},{5,4},{6,7},{7,6},{8,9},{9,8},{10,11... | collective-permute-start | bytes 7913480 | tf_op jit(solution)/shard_map/ppermute | solution.py:788
  322.9 23.6 %collective-permute-start.14 = (bf16[1472,896]{1,0:T(8,128)(2,1)}, bf16[1472,896]{1,0:T(8,128)(2,1)S(1)}, u32[]{:S(2)}, u32[]{:S(2)}) collective-permute-start(bf16[1472,896]{1,0:T(8,128)(2,1)} %get-tuple-element.151), channel_id=1, source_target_pairs={{0,1},{1,0},{2,3},{3,2},{4,5},{5,4},{6,7},{7,6},{8,9},{9,8},{10,11... | collective-permute-start | bytes 7913480 | tf_op jit(solution)/shard_map/ppermute | solution.py:788
  338.6 15.0 %collective-permute-start.16 = (bf16[1472,896]{1,0:T(8,128)(2,1)S(1)}, bf16[1472,896]{1,0:T(8,128)(2,1)S(1)}, u32[]{:S(2)}, u32[]{:S(2)}) collective-permute-start(bf16[1472,896]{1,0:T(8,128)(2,1)S(1)} %copy-done.39), channel_id=1, source_target_pairs={{0,1},{1,0},{2,3},{3,2},{4,5},{5,4},{6,7},{7,6},{8,9},{9,8},{10,11... | collective-permute-start | bytes 7913480 | tf_op jit(solution)/shard_map/ppermute | solution.py:788
  348.6 49.8 %collective-permute-start.19 = (bf16[976,896]{1,0:T(8,128)(2,1)}, bf16[976,896]{1,0:T(8,128)(2,1)S(1)}, u32[]{:S(2)}, u32[]{:S(2)}) collective-permute-start(bf16[976,896]{1,0:T(8,128)(2,1)} %slice.585), channel_id=1, source_target_pairs={{0,2},{2,0},{1,3},{3,1},{4,6},{6,4},{5,7},{7,5},{8,10},{10,8},{9,1... | collective-permute-start | bytes 5246984 | tf_op jit(solution)/shard_map/ppermute | solution.py:788
  348.9 49.5 %collective-permute-start.18 = (bf16[736,896]{1,0:T(8,128)(2,1)S(1)}, bf16[736,896]{1,0:T(8,128)(2,1)}, u32[]{:S(2)}, u32[]{:S(2)}) collective-permute-start(bf16[736,896]{1,0:T(8,128)(2,1)S(1)} %get-tuple-element.166), channel_id=1, source_target_pairs={{0,4},{4,0},{1,5},{5,1},{2,6},{6,2},{3,7},{7,3},{8,12},{12,8},{9,1... | collective-permute-start | bytes 3956744 | tf_op jit(solution)/shard_map/ppermute | solution.py:788
  398.4 7.9 collective-permute-start.23
  398.4 53.0 %collective-permute-start.25 = (bf16[496,896]{1,0:T(8,128)(2,1)}, bf16[496,896]{1,0:T(8,128)(2,1)}, u32[]{:S(2)}, u32[]{:S(2)}) collective-permute-start(bf16[496,896]{1,0:T(8,128)(2,1)} %slice.586), channel_id=1, source_target_pairs={{0,2},{2,0},{1,3},{3,1},{4,6},{6,4},{5,7},{7,5},{8,10},{10,8},{9,1... | collective-permute-start | bytes 2666504 | tf_op jit(solution)/shard_map/ppermute | solution.py:788
  404.8 59.6 %collective-permute-start.22 = (bf16[736,896]{1,0:T(8,128)(2,1)}, bf16[736,896]{1,0:T(8,128)(2,1)}, u32[]{:S(2)}, u32[]{:S(2)}) collective-permute-start(bf16[736,896]{1,0:T(8,128)(2,1)} %add_convert_fusion.5), channel_id=1, source_target_pairs={{0,2},{2,0},{1,3},{3,1},{4,6},{6,4},{5,7},{7,5},{8,10},{10,8},{9,1... | collective-permute-start | bytes 3956744 | tf_op jit(solution)/shard_map/ppermute | solution.py:788
  406.2 62.8 %collective-permute-start.26 = (bf16[1472,896]{1,0:T(8,128)(2,1)}, bf16[1472,896]{1,0:T(8,128)(2,1)}, u32[]{:S(2)}, u32[]{:S(2)}) collective-permute-start(bf16[1472,896]{1,0:T(8,128)(2,1)} %get-tuple-element.193), channel_id=1, source_target_pairs={{0,1},{1,0},{2,3},{3,2},{4,5},{5,4},{6,7},{7,6},{8,9},{9,8},{10,11... | collective-permute-start | bytes 7913480 | tf_op jit(solution)/shard_map/ppermute | solution.py:788
  407.3 57.2 %collective-permute-start.24 = (bf16[736,896]{1,0:T(8,128)(2,1)S(1)}, bf16[736,896]{1,0:T(8,128)(2,1)S(1)}, u32[]{:S(2)}, u32[]{:S(2)}) collective-permute-start(bf16[736,896]{1,0:T(8,128)(2,1)S(1)} %select_convert_fusion.2), channel_id=1, source_target_pairs={{0,4},{4,0},{1,5},{5,1},{2,6},{6,2},{3,7},{7,3},{8,12},{12,8},{9,1... | collective-permute-start | bytes 3956744 | tf_op jit(solution)/shard_map/ppermute | solution.py:788
  450.2 9.2 %collective-permute-start.20 = (bf16[1024,128]{1,0:T(8,128)(2,1)S(1)}, bf16[1024,128]{1,0:T(8,128)(2,1)S(1)}, u32[]{:S(2)}, u32[]{:S(2)}) collective-permute-start(bf16[1024,128]{1,0:T(8,128)(2,1)S(1)} %get-tuple-element.312), channel_id=1, source_target_pairs={{0,4},{4,0},{1,5},{5,1},{2,6},{6,2},{3,7},{7,3},{8,12},{12,8},{9,1... | collective-permute-start | bytes 786440 | tf_op jit(solution)/shard_map/ppermute | solution.py:788
  451.4 12.9 %collective-permute-start.21 = (bf16[1024,128]{1,0:T(8,128)(2,1)S(1)}, bf16[1024,128]{1,0:T(8,128)(2,1)S(1)}, u32[]{:S(2)}, u32[]{:S(2)}) collective-permute-start(bf16[1024,128]{1,0:T(8,128)(2,1)S(1)} %get-tuple-element.311), channel_id=1, source_target_pairs={{0,4},{4,0},{1,5},{5,1},{2,6},{6,2},{3,7},{7,3},{8,12},{12,8},{9,1... | collective-permute-start | bytes 786440 | tf_op jit(solution)/shard_map/ppermute | solution.py:788
  459.4 59.6 %collective-permute-start.28 = (bf16[1472,896]{1,0:T(8,128)(2,1)}, bf16[1472,896]{1,0:T(8,128)(2,1)}, u32[]{:S(2)}, u32[]{:S(2)}) collective-permute-start(bf16[1472,896]{1,0:T(8,128)(2,1)} %add_convert_fusion), channel_id=1, source_target_pairs={{0,2},{2,0},{1,3},{3,1},{4,6},{6,4},{5,7},{7,5},{8,10},{10,8},{9,1... | collective-permute-start | bytes 7913480 | tf_op jit(solution)/shard_map/ppermute | solution.py:788
  469.0 130.7 %reduce-scatter.18.cloned.1.call-start = ((), (), s32[]{:S(2)}) async-start(), calls=%async_computation.15 | async-start | bytes 1648640
  473.5 45.5 %collective-permute-start.27 = (bf16[736,896]{1,0:T(8,128)(2,1)S(1)}, bf16[736,896]{1,0:T(8,128)(2,1)}, u32[]{:S(2)}, u32[]{:S(2)}) collective-permute-start(bf16[736,896]{1,0:T(8,128)(2,1)S(1)} %select_convert_fusion.1), channel_id=1, source_target_pairs={{0,4},{4,0},{1,5},{5,1},{2,6},{6,2},{3,7},{7,3},{8,12},{12,8},{9,1... | collective-permute-start | bytes 3956744 | tf_op jit(solution)/shard_map/ppermute | solution.py:788
  523.4 79.8 %reduce-scatter.12.cloned.1.call-start = ((), (), s32[]{:S(2)}) async-start(), calls=%async_computation.9 | async-start | bytes 2621440 | tf_op jit(solution)/shard_map/reduce_scatter | solution.py:924
  524.2 161.6 %reduce-scatter.14.cloned.1.call-start = ((), (), s32[]{:S(2)}) async-start(), calls=%async_computation.10 | async-start | bytes 5242880 | tf_op jit(solution)/shard_map/reduce_scatter | solution.py:924
  533.3 66.3 %collective-permute-start.30 = (bf16[736,896]{1,0:T(8,128)(2,1)S(1)}, bf16[736,896]{1,0:T(8,128)(2,1)}, u32[]{:S(2)}, u32[]{:S(2)}) collective-permute-start(bf16[736,896]{1,0:T(8,128)(2,1)S(1)} %select_convert_fusion), channel_id=1, source_target_pairs={{0,4},{4,0},{1,5},{5,1},{2,6},{6,2},{3,7},{7,3},{8,12},{12,8},{9,1... | collective-permute-start | bytes 3956744 | tf_op jit(solution)/shard_map/ppermute | solution.py:788
  603.3 147.9 %all-gather.16.cloned.1.call-start = ((), (), s32[]{:S(2)}) async-start(), calls=%async_computation.11 | async-start | bytes 1648640 | tf_op jit(solution)/shard_map/all_gather | solution.py:949
  611.4 12.0 %collective-permute-start.48 = (bf16[368,512]{1,0:T(8,128)(2,1)S(1)}, bf16[368,512]{1,0:T(8,128)(2,1)S(1)}, u32[]{:S(2)}, u32[]{:S(2)}) collective-permute-start(bf16[368,512]{1,0:T(8,128)(2,1)S(1)} %fusion.10), channel_id=1, source_target_pairs={{0,2},{2,0},{1,3},{3,1},{4,6},{6,4},{5,7},{7,5},{8,10},{10,8},{9,1... | collective-permute-start | bytes 1130504 | tf_op jit(solution)/shard_map/ppermute | solution.py:788
  624.8 6.6 collective-permute-start.49
  631.5 10.6 %collective-permute-start.50 = (bf16[96,512]{1,0:T(8,128)(2,1)S(1)}, bf16[96,512]{1,0:T(8,128)(2,1)S(1)}, u32[]{:S(2)}, u32[]{:S(2)}) collective-permute-start(bf16[96,512]{1,0:T(8,128)(2,1)S(1)} %select_convert_fusion.9), channel_id=1, source_target_pairs={{0,8},{8,0},{16,24},{24,16},{1,9},{9,1},{17,25},{25,17},{2,10},{10... | collective-permute-start | bytes 294920 | tf_op jit(solution)/shard_map/ppermute | solution.py:812
  685.8 67.0 %reduce-scatter.20.cloned.1.call-start = ((), (), s32[]{:S(2)}) async-start(), calls=%async_computation.16 | async-start | bytes 1648640
  692.1 68.6 %collective-permute-start.52 = (bf16[48,512]{1,0:T(8,128)(2,1)}, bf16[48,512]{1,0:T(8,128)(2,1)}, u32[]{:S(2)}, u32[]{:S(2)}) collective-permute-start(bf16[48,512]{1,0:T(8,128)(2,1)} %add_convert_fusion.7), channel_id=1, source_target_pairs={{0,16},{8,24},{16,0},{24,8},{1,17},{9,25},{17,1},{25,9},{2,18},{10... | collective-permute-start | bytes 147464 | tf_op jit(solution)/shard_map/ppermute | solution.py:812
  695.3 29.7 %collective-permute-start.34 = (bf16[1024,128]{1,0:T(8,128)(2,1)}, bf16[1024,128]{1,0:T(8,128)(2,1)}, u32[]{:S(2)}, u32[]{:S(2)}) collective-permute-start(bf16[1024,128]{1,0:T(8,128)(2,1)} %bitcast.49), channel_id=1, source_target_pairs={{0,4},{4,0},{1,5},{5,1},{2,6},{6,2},{3,7},{7,3},{8,12},{12,8},{9,1... | collective-permute-start | bytes 786440 | tf_op jit(solution)/shard_map/ppermute | solution.py:788
  699.6 112.6 %all-gather.18.cloned.1.call-start = ((), (), s32[]{:S(2)}) async-start(), calls=%async_computation.12 | async-start | bytes 1648640 | tf_op jit(solution)/shard_map/all_gather | solution.py:949
  701.6 14.9 %collective-permute-start.31 = (bf16[1024,256]{1,0:T(8,128)(2,1)S(1)}, bf16[1024,256]{1,0:T(8,128)(2,1)S(1)}, u32[]{:S(2)}, u32[]{:S(2)}) collective-permute-start(bf16[1024,256]{1,0:T(8,128)(2,1)S(1)} %get-tuple-element.308), channel_id=1, source_target_pairs={{0,4},{4,0},{1,5},{5,1},{2,6},{6,2},{3,7},{7,3},{8,12},{12,8},{9,1... | collective-permute-start | bytes 1572872 | tf_op jit(solution)/shard_map/ppermute | solution.py:788
  702.3 19.9 %collective-permute-start.32 = (bf16[1024,128]{1,0:T(8,128)(2,1)S(1)}, bf16[1024,128]{1,0:T(8,128)(2,1)S(1)}, u32[]{:S(2)}, u32[]{:S(2)}) collective-permute-start(bf16[1024,128]{1,0:T(8,128)(2,1)S(1)} %bitcast.178), channel_id=1, source_target_pairs={{0,4},{4,0},{1,5},{5,1},{2,6},{6,2},{3,7},{7,3},{8,12},{12,8},{9,1... | collective-permute-start | bytes 786440 | tf_op jit(solution)/shard_map/ppermute | solution.py:788
  704.0 21.0 %collective-permute-start.33 = (bf16[1024,128]{1,0:T(8,128)(2,1)S(1)}, bf16[1024,128]{1,0:T(8,128)(2,1)S(1)}, u32[]{:S(2)}, u32[]{:S(2)}) collective-permute-start(bf16[1024,128]{1,0:T(8,128)(2,1)S(1)} %get-tuple-element.322), channel_id=1, source_target_pairs={{0,4},{4,0},{1,5},{5,1},{2,6},{6,2},{3,7},{7,3},{8,12},{12,8},{9,1... | collective-permute-start | bytes 786440 | tf_op jit(solution)/shard_map/ppermute | solution.py:788
  755.4 7.6 collective-permute-start.36
  761.7 9.8 %collective-permute-start.53 = (bf16[96,512]{1,0:T(8,128)(2,1)S(1)}, bf16[96,512]{1,0:T(8,128)(2,1)S(1)}, u32[]{:S(2)}, u32[]{:S(2)}) collective-permute-start(bf16[96,512]{1,0:T(8,128)(2,1)S(1)} %pad_maximum_fusion.21), channel_id=1, source_target_pairs={{0,8},{8,0},{16,24},{24,16},{1,9},{9,1},{17,25},{25,17},{2,10},{10... | collective-permute-start | bytes 294920 | tf_op jit(solution)/shard_map/ppermute | solution.py:812
  762.6 12.0 %collective-permute-start.35 = (bf16[368,1280]{1,0:T(8,128)(2,1)}, bf16[368,1280]{1,0:T(8,128)(2,1)S(1)}, u32[]{:S(2)}, u32[]{:S(2)}) collective-permute-start(bf16[368,1280]{1,0:T(8,128)(2,1)} %get-tuple-element.273), channel_id=1, source_target_pairs={{0,1},{1,0},{2,3},{3,2},{4,5},{5,4},{6,7},{7,6},{8,9},{9,8},{10,11... | collective-permute-start | bytes 2826248 | tf_op jit(solution)/shard_map/ppermute | solution.py:788
  765.4 23.1 %collective-permute-start.37 = (bf16[368,1280]{1,0:T(8,128)(2,1)}, bf16[368,1280]{1,0:T(8,128)(2,1)S(1)}, u32[]{:S(2)}, u32[]{:S(2)}) collective-permute-start(bf16[368,1280]{1,0:T(8,128)(2,1)} %fusion.6), channel_id=1, source_target_pairs={{0,2},{2,0},{1,3},{3,1},{4,6},{6,4},{5,7},{7,5},{8,10},{10,8},{9,1... | collective-permute-start | bytes 2826248 | tf_op jit(solution)/shard_map/ppermute | solution.py:788
  772.2 37.6 %collective-permute-start.54 = (bf16[192,512]{1,0:T(8,128)(2,1)}, bf16[192,512]{1,0:T(8,128)(2,1)}, u32[]{:S(2)}, u32[]{:S(2)}) collective-permute-start(bf16[192,512]{1,0:T(8,128)(2,1)} %pad_maximum_fusion.15), channel_id=1, source_target_pairs={{0,4},{4,0},{1,5},{5,1},{2,6},{6,2},{3,7},{7,3},{8,12},{12,8},{9,1... | collective-permute-start | bytes 589832 | tf_op jit(solution)/shard_map/ppermute | solution.py:788
  773.8 78.9 %all-gather.20.cloned.1.call-start = ((), (), s32[]{:S(2)}) async-start(), calls=%async_computation.13 | async-start | bytes 1648640 | tf_op jit(solution)/shard_map/all_gather | solution.py:949
  774.0 33.4 %collective-permute-start.38 = (bf16[736,896]{1,0:T(8,128)(2,1)S(1)}, bf16[736,896]{1,0:T(8,128)(2,1)S(1)}, u32[]{:S(2)}, u32[]{:S(2)}) collective-permute-start(bf16[736,896]{1,0:T(8,128)(2,1)S(1)} %copy-done.55), channel_id=1, source_target_pairs={{0,4},{4,0},{1,5},{5,1},{2,6},{6,2},{3,7},{7,3},{8,12},{12,8},{9,1... | collective-permute-start | bytes 3956744 | tf_op jit(solution)/shard_map/ppermute | solution.py:788
  808.4 14.5 %collective-permute-start.39 = (bf16[192,1280]{1,0:T(8,128)(2,1)}, bf16[192,1280]{1,0:T(8,128)(2,1)}, u32[]{:S(2)}, u32[]{:S(2)}) collective-permute-start(bf16[192,1280]{1,0:T(8,128)(2,1)} %select_convert_fusion.5), channel_id=1, source_target_pairs={{0,4},{4,0},{1,5},{5,1},{2,6},{6,2},{3,7},{7,3},{8,12},{12,8},{9,1... | collective-permute-start | bytes 1474568 | tf_op jit(solution)/shard_map/ppermute | solution.py:788
  812.2 41.9 %collective-permute-start.42 = (bf16[736,896]{1,0:T(8,128)(2,1)}, bf16[736,896]{1,0:T(8,128)(2,1)}, u32[]{:S(2)}, u32[]{:S(2)}) collective-permute-start(bf16[736,896]{1,0:T(8,128)(2,1)} %all-gather.18.cloned.1.call-done), channel_id=1, source_target_pairs={{0,4},{4,0},{1,5},{5,1},{2,6},{6,2},{3,7},{7,3},{8,12},{12,8},{9,1... | collective-permute-start | bytes 3956744 | tf_op jit(solution)/shard_map/ppermute | solution.py:788
  824.1 19.5 %collective-permute-start.40 = (bf16[96,1280]{1,0:T(8,128)(2,1)S(1)}, bf16[96,1280]{1,0:T(8,128)(2,1)S(1)}, u32[]{:S(2)}, u32[]{:S(2)}) collective-permute-start(bf16[96,1280]{1,0:T(8,128)(2,1)S(1)} %select_convert_fusion.6), channel_id=1, source_target_pairs={{0,8},{8,0},{16,24},{24,16},{1,9},{9,1},{17,25},{25,17},{2,10},{10... | collective-permute-start | bytes 737288 | tf_op jit(solution)/shard_map/ppermute | solution.py:812
  843.7 10.4 %collective-permute-start.41 = (bf16[48,1280]{1,0:T(8,128)(2,1)S(1)}, bf16[48,1280]{1,0:T(8,128)(2,1)S(1)}, u32[]{:S(2)}, u32[]{:S(2)}) collective-permute-start(bf16[48,1280]{1,0:T(8,128)(2,1)S(1)} %select_convert_fusion.8), channel_id=1, source_target_pairs={{0,16},{8,24},{16,0},{24,8},{1,17},{9,25},{17,1},{25,9},{2,18},{10... | collective-permute-start | bytes 368648 | tf_op jit(solution)/shard_map/ppermute | solution.py:812
  852.6 32.0 %collective-permute-start.55 = (bf16[736,896]{1,0:T(8,128)(2,1)}, bf16[736,896]{1,0:T(8,128)(2,1)S(1)}, u32[]{:S(2)}, u32[]{:S(2)}) collective-permute-start(bf16[736,896]{1,0:T(8,128)(2,1)} %all-gather.20.cloned.1.call-done), channel_id=1, source_target_pairs={{0,4},{4,0},{1,5},{5,1},{2,6},{6,2},{3,7},{7,3},{8,12},{12,8},{9,1... | collective-permute-start | bytes 3956744 | tf_op jit(solution)/shard_map/ppermute | solution.py:788
  854.2 8.3 collective-permute-start.43
  862.5 7.9 collective-permute-start.44
  870.6 23.7 %collective-permute-start.45 = (bf16[192,1280]{1,0:T(8,128)(2,1)S(1)}, bf16[192,1280]{1,0:T(8,128)(2,1)S(1)}, u32[]{:S(2)}, u32[]{:S(2)}) collective-permute-start(bf16[192,1280]{1,0:T(8,128)(2,1)S(1)} %pad_maximum_fusion.10), channel_id=1, source_target_pairs={{0,4},{4,0},{1,5},{5,1},{2,6},{6,2},{3,7},{7,3},{8,12},{12,8},{9,1... | collective-permute-start | bytes 1474568 | tf_op jit(solution)/shard_map/ppermute | solution.py:788
  (88 other events, 1180.4 us)
Sparse Core Ops, SparseCore 0:
  13.4 34.7 all-gather.7
  79.3 80.7 all-gather.13
  162.3 44.6 all-gather.11
  209.0 26.0 all-gather.9
  469.1 30.8 reduce-scatter.15
  523.6 33.7 reduce-scatter.17
  559.7 43.5 reduce-scatter.11
  606.2 79.4 reduce-scatter.13
  687.4 33.2 all-gather.15
  722.8 30.0 reduce-scatter.19
  773.9 31.2 all-gather.17
  812.9 39.6 all-gather.19

commit v3 on v2

--- a/solution.py
+++ b/solution.py
@@ -466,25 +466,46 @@
     return diag.astype(jnp.int32), tail.astype(jnp.int32)
 
 
+def bucket_in(distance, low, high):
+    bucket = jnp.minimum(jnp.maximum(distance, 0), 16)
+    for threshold in thresholds:
+        if threshold <= high:
+            bucket = bucket + (distance >= threshold).astype(jnp.int32)
+    return bucket
+
+
+def tables_kernel(last, table, two, z_two, one, z_one):
+    diag = (WIN - 1) * BLK + lane((WK, 128)) % 64 - sub((WK, 128))
+    tail = WK + lane((WK, 128)) - sub((WK, 128))
+    left = lane((WK, 128)) < 64
+    near, end = bucket_in(diag, -WK, WK), bucket_in(tail, 1, WK + 128)
+    rel = lambda b, h: (table[b * 3 + h] - table[last * 3 + h]) * LOG2E
+    zero = jnp.zeros((WK, 128), F32)
+    picks = [zero] * 6
+    for b in range(last):
+        at_near, at_end = near == b, end == b
+        picks = [jnp.where(at_near, rel(b, h), picks[h]) for h in range(3)] + [
+            jnp.where(at_end, rel(b, h), picks[3 + h]) for h in range(3)]
+    seen = diag >= 0
+    two[...] = jnp.where(seen, jnp.where(left, picks[0], picks[1]), NEG)
+    one[...] = jnp.where(seen, picks[2], NEG)
+    for ref, i, val in ((z_two, 0, picks[3]), (z_two, 1, picks[4]), (z_one, 0, picks[5])):
+        high = val.astype(BF)
+        ref[0, i] = high
+        ref[1, i] = (val - high.astype(F32)).astype(BF)
+
+
 def bias_tables(table):
-    last = table.shape[0] - 1
-    rel = (table - table[last:]) * LOG2E
-    diag, tail = near_distance()
-
-    def pick(dist):
-        bucket = bucket_of(dist)
-        out = jnp.zeros((3,) + dist.shape, F32)
-        for b in range(last):
-            out = jnp.where(bucket[None] == b, rel[b][:, None, None], out)
-        return out
-
-    d = jnp.where(diag[None] >= 0, pick(diag), NEG)
-    z = pick(tail)
-    two, one = jnp.concatenate([d[0], d[1]], axis=1), jnp.concatenate([d[2], d[2]], axis=1)
-    z_hi = z.astype(BF)
-    z_lo = (z - z_hi.astype(F32)).astype(BF)
-    z = jnp.stack([z_hi, z_lo])
-    return (two, z[:, :2]), (one, z[:, 2:])
+    shape = jax.ShapeDtypeStruct
+    two, z_two, one, z_one = pl.pallas_call(
+        functools.partial(tables_kernel, table.shape[0] - 1),
+        out_shape=(shape((WK, 128), F32), shape((2, 2, WK, 128), BF), shape((WK, 128), F32), shape((2, 1, WK, 128), BF)),
+        in_specs=[SM],
+        out_specs=(VM, VM, VM, VM),
+        cost_estimate=pl.CostEstimate(flops=HINT, bytes_accessed=HINT, transcendentals=0),
+        name="tables",
+    )(table.reshape(-1))
+    return (two, z_two), (one, z_one)
 
 
 def bias_grads(gt_two, gz_two, gt_one, gz_one, buckets):
@@ -700,8 +721,8 @@
     )(*d_list, *w_list, mid, dy, gain, w_o)
 
 
-def in_back_kernel(d_qkv, w_qkv, x, h, gain, d_mid, extra, in_grad, g_qkv, acc, g_gain):
-    width, rows = x.shape
+def in_part_kernel(d_qkv, w_qkv, h, part, g_qkv):
+    rows = h.shape[1]
     cols = min(256, rows)
 
     def grads(c):
@@ -712,7 +733,41 @@
 
     def back(c):
         at = pl.ds(pl.multiple_of(c * cols, cols), cols)
-        acc[:, at] = dot_nt(w_qkv[...], d_qkv[at, :])
+        part[:, at] = dot_nt(w_qkv[...], d_qkv[at, :])
+
+    each(rows // cols, back)
+
+
+def in_part(d_qkv, w_qkv, h):
+    width, rows = h.shape
+    return pl.pallas_call(
+        in_part_kernel,
+        out_shape=(
+            jax.ShapeDtypeStruct((width, rows), F32),
+            jax.ShapeDtypeStruct((width, d_qkv.shape[1]), BF),
+        ),
+        in_specs=[VM] * 3,
+        out_specs=(VM, VM),
+        compiler_params=pltpu.CompilerParams(vmem_limit_bytes=40 << 20),
+        cost_estimate=pl.CostEstimate(flops=HINT, bytes_accessed=HINT, transcendentals=0),
+        name="in_part",
+    )(d_qkv, w_qkv, h)
+
+
+def in_back_kernel(d_qkv, w_qkv, part, x, h, gain, d_mid, extra, in_grad, g_qkv, acc, g_gain):
+    width, rows = x.shape
+    cols = min(256, rows)
+    count = d_qkv.shape[1]
+
+    def grads(c):
+        at = pl.ds(pl.multiple_of(c * 256, 256), 256)
+        g_qkv[:, at] = dot_nn(h[...], d_qkv[:, at]).astype(BF)
+
+    each(count // 256, grads)
+
+    def back(c):
+        at = pl.ds(pl.multiple_of(c * cols, cols), cols)
+        acc[:, at] = part[:, at] + dot_nt(w_qkv[...], d_qkv[at, :])
 
     each(rows // cols, back)
 
@@ -721,25 +776,24 @@
 
     norm_back(x, acc, gain, g_gain, rows, give)
     ln = lane((width, 128))
-    spare = jnp.where(ln == 64, g_gain[...], extra[...])
-    g_qkv[:, 512:640] = jnp.where(ln < 64, g_qkv[:, 512:640].astype(F32), spare).astype(BF)
-
-
-def in_back(d_qkv, w_qkv, x, h, gain, d_mid, extra):
+    g_qkv[:, count : count + 128] = jnp.where(ln == 0, g_gain[...], extra[...]).astype(BF)
+
+
+def in_back(d_qkv, w_qkv, part, x, h, gain, d_mid, extra):
     width, rows = x.shape
     return pl.pallas_call(
         in_back_kernel,
         out_shape=(
             jax.ShapeDtypeStruct((width, rows), BF),
-            jax.ShapeDtypeStruct((width, d_qkv.shape[1]), BF),
+            jax.ShapeDtypeStruct((width, d_qkv.shape[1] + 128), BF),
         ),
-        in_specs=[VM] * 7,
+        in_specs=[VM] * 8,
         out_specs=(VM, VM),
         scratch_shapes=[pltpu.VMEM((width, rows), F32), pltpu.VMEM((width, 1), F32)],
         compiler_params=pltpu.CompilerParams(vmem_limit_bytes=56 << 20),
         cost_estimate=pl.CostEstimate(flops=HINT, bytes_accessed=HINT, transcendentals=0),
         name="in_back",
-    )(d_qkv, w_qkv, x, h, gain, d_mid, extra)
+    )(d_qkv, w_qkv, part, x, h, gain, d_mid, extra)
 
 
 def pack_kernel(par, w_q, w_k, w_v, w_o, norms, table, qkv_out, o_out):
@@ -878,6 +932,9 @@
     kv1, q1 = gather(one[:, :, :128]), blocks(one[:, :, 128:])
     tab, lo, oo = plan(deal_table, seg_ids[0], ctx, nb)
     bias2, bias1 = bias_tables(my_table)
+    w_early = jnp.concatenate([w_qkv[:, 256:640], w_qkv[:, 896:]], axis=1)
+    w_late = jnp.concatenate([w_qkv[:, :256], w_qkv[:, 640:896]], axis=1)
+    kv2, w_early, w_late = after(kv2, w_early, w_late)
     att2, lse2 = attn_fwd(False, tab, kv2, q2, *bias2, lo, oo)
     kv1, att2 = after(kv1, att2)
     att1, lse1 = attn_fwd(True, tab, kv1, q1, *bias1, lo, oo)
@@ -891,6 +948,13 @@
 
     mid = up32(x) + dot_nt(w_o, att_rows)
     h2 = rms_cols(mid, gain_ffn).astype(BF)
+
+    def split_ffn(v):
+        v = v.reshape(steps, 2, -1, v.shape[1])
+        flat_rows = lambda u: u.reshape(-1, u.shape[-1])
+        even, odd = flat_rows(v[:, 0]), flat_rows(v[:, 1])
+        return pick_half(par, even, odd), pick_half(par, odd, even)
+
     o_far = ffn_pair(h2, dy, *[w[2:] for w in weights])
     total = mid
     for r in (2, 3):
@@ -900,7 +964,7 @@
     cut = 2 * width // 3 // 16 * 16
     gate_far = far_g[0].astype(BF)
     to_x = [gate_far[:cut], gate_far[cut:], far_g[1].astype(BF)]
-    keep_d, send_d = split_by(far_g[2], par)
+    keep_d, send_d = split_ffn(far_g[2])
     h2, total, keep_d, send_d, *to_x = after(h2, total, keep_d.astype(BF), send_d.astype(BF), *to_x)
     far_d = swap(send_d, "cy")
     gate_a, gate_b, far_up = [swap(g, "fx") for g in to_x]
@@ -908,7 +972,7 @@
     *o_near, far_d, gate_a = after(*o_near, far_d, gate_a)
     far_d = swap((up32(keep_d) + up32(far_d)).astype(BF), "fx")
     near_g = [fold(o_near, k) for k in range(3)]
-    keep_d, send_d = split_by(near_g[2], par)
+    keep_d, send_d = split_ffn(near_g[2])
     near_d = swap(send_d.astype(BF), "cy")
     d_lists = [o_near[2], o_near[3], o_far[2], o_far[3], o_near[4], o_near[5], o_far[4], o_far[5]]
     w_lists = list(weights[0]) + list(weights[1])
@@ -922,73 +986,74 @@
     do1, do2, far_d, near_d, far_gate = after(do1, do2, far_d, near_d, jnp.concatenate([gate_a, gate_b]))
     half_d = (keep_d + up32(near_d) + up32(far_d)).astype(BF)
     scatter = lambda v, dim: lax.psum_scatter(v, "cz", scatter_dimension=dim, tiled=True)
-    piece_d = scatter(half_d, 0)
-    keep_gate, send = split_by(near_g[0] + up32(far_gate), par)
+    half_d = lax.psum(half_d, "cz")
+    keep_gate, send = split_ffn(near_g[0] + up32(far_gate))
     recv_gate = swap(send.astype(BF), "cy")
     dq1, dkv1, gt1, gz1 = attn_bwd(True, tab, kv1, q1, do1, att1, *bias1, lo, oo, lse1)
-    dkv1, dq1, piece_d, recv_gate, far_up = after(dkv1, dq1, piece_d, recv_gate, far_up)
+    dkv1, dq1, recv_gate, far_up = after(dkv1, dq1, recv_gate, far_up)
     dkv1 = scatter(dkv1.reshape(GROUP, 128), 0)
     half_gate = (keep_gate + up32(recv_gate)).astype(BF)
     piece_gate = scatter(half_gate, 0)
-    keep_up, send = split_by(near_g[1] + up32(far_up), par)
+    keep_up, send = split_ffn(near_g[1] + up32(far_up))
     recv_up = swap(send.astype(BF), "cy")
     do2, far_up = after(do2, far_up)
     dq2, dkv2, gt2, gz2 = attn_bwd(False, tab, kv2, q2, do2, att2, *bias2, lo, oo, lse2)
-    dkv2, dq2, dkv1, recv_up, piece_gate = after(dkv2, dq2, dkv1, recv_up, piece_gate)
+    dkv2, dq2, dkv1, recv_up, piece_gate, half_d = after(dkv2, dq2, dkv1, recv_up, piece_gate, half_d)
     dkv2 = scatter(dkv2.reshape(GROUP, 256), 0)
-    half_up = (keep_up + up32(recv_up)).astype(BF)
-    g_out = dot_nn(d_branch, att_rows).astype(BF)
-    dq1, dq2 = dq1.reshape(2, rows, 128), dq2.reshape(2, rows, 128)
-    other1 = [swap(v, "cy") for v in (dkv1[rows:], dq1[1])]
-    other_q2 = swap(dq2[1], "cy")
-    dkv2, half_up, piece_d, piece_gate = after(dkv2, half_up, piece_d, piece_gate)
-    other2 = [swap(dkv2[rows:], "cy"), other_q2]
-    d_qkv = jnp.concatenate(
-        [dkv2[:rows], dq2[0], dkv1[:rows], dq1[0]] + other2 + other1, axis=1)
-    piece_up = scatter(half_up, 0)
-    gather_half = lambda piece: lax.all_gather(piece, "cz", axis=0, tiled=True)
-
-    def whole(half, other):
-        return up32(jnp.concatenate([pick_half(par, half, other), pick_half(par, other, half)]))
-
-    g_bias = bias_grads(gt2, gz2, gt1, gz1, table.shape[0])
-    zero = jnp.zeros_like(g_bias)
-    g_bias = jnp.concatenate([pick_half(par, g_bias, zero), pick_half(par, zero, g_bias)], axis=1)
-    spare = jnp.pad(g_bias.reshape(shards, bias_rows, HEADS),
-                    ((0, 0), (0, share - bias_rows), (66, 128 - 66 - HEADS))).reshape(width, 128)
-    spare = jnp.where(jnp.arange(128)[None, :] == 65, g_gain_ffn, spare)
-    in_grad, g_qkv = in_back(d_qkv, w_qkv, x, h1, gain_attn, d_mid, spare)
-    in_grad = jnp.transpose(in_grad).reshape(layer_in.shape)
-
+    piece_up = scatter((keep_up + up32(recv_up)).astype(BF), 0)
     f_here = lax.axis_index("fx") * 2 + lax.axis_index("fc")
 
-    def fold_attn(g):
+    def fold_attn(g, *counts):
         blocks = g.reshape(shards, share, g.shape[1])
         away = lambda r: lax.dynamic_index_in_dim(blocks, f_here ^ r, keepdims=False)
         near = up32(away(0)) + up32(swap(away(1), "fc"))
         far = (up32(away(2)) + up32(swap(away(3), "fc"))).astype(BF)
         own = near + up32(swap(far, "fx"))
-        half = g.shape[1] // 2
-        own = pick_half(par, own, jnp.concatenate([own[:, half:], own[:, :half]], axis=1))
+        at, swapped = 0, []
+        for count in counts:
+            mid_at = at + count // 2
+            swapped += [own[:, mid_at : at + count], own[:, at:mid_at]]
+            at += count
+        if at < own.shape[1]:
+            swapped.append(own[:, at:])
+        own = pick_half(par, own, jnp.concatenate(swapped, axis=1))
         return jnp.pad(own, ((0, (-share) % 64), (0, 0)))
 
-    g_out = up32(ctx_gather(ctx_scatter(fold_attn(g_out), bits), bits)[:share])
-    half_d = gather_half(piece_d)
-    g_qkv, half_d, piece_up = after(g_qkv, half_d, piece_up)
-    half_gate, half_up = gather_half(piece_gate), gather_half(piece_up)
-    g_qkv, other_d = after(fold_attn(g_qkv), swap(half_d, "cy"))
-    g_qkv, other_gate = after(ctx_scatter(g_qkv, bits), swap(half_gate, "cy"))
-    g_qkv = up32(ctx_gather(g_qkv, bits)[:share])
-    grad_down_t, grad_gate = whole(half_d, other_d), whole(half_gate, other_gate)
-    grad_up = whole(half_up, swap(half_up, "cy"))
-    cols = lambda g, at: g[:, at : at + HDIM]
-    p0, p1 = 0, 640
-    grad_key = jnp.concatenate([cols(g_qkv, p + o) for p in (p0, p1) for o in (0, 64, 384)], axis=1)
-    grad_value = jnp.concatenate([cols(g_qkv, p + o) for p in (p0, p1) for o in (128, 192, 448)], axis=1)
-    grad_query = jnp.concatenate([cols(g_qkv, p + o) for p in (p0, p1) for o in (256, 320, 512)], axis=1)
-    grad_out = jnp.transpose(
-        jnp.concatenate([cols(g_out, p + o) for p in (0, 256) for o in (0, 64, 192)], axis=1))
-    rest = cols(g_qkv, 576) + cols(g_qkv, 1216)
+    dq1, dq2 = dq1.reshape(2, rows, 128), dq2.reshape(2, rows, 128)
+    early = [dq2[0], dkv1[:rows], dq1[0]] + [swap(v, "cy") for v in (dq2[1], dkv1[rows:], dq1[1])]
+    d_part, g_early = in_part(jnp.concatenate(early, axis=1), w_early, h1)
+    g_out = dot_nn(d_branch, att_rows).astype(BF)
+    g_early = jnp.concatenate([g_early, g_out], axis=1)
+    g_bias = bias_grads(gt2, gz2, gt1, gz1, table.shape[0])
+    zero = jnp.zeros_like(g_bias)
+    g_bias = jnp.concatenate([pick_half(par, g_bias, zero), pick_half(par, zero, g_bias)], axis=1)
+    spare = jnp.pad(g_bias.reshape(shards, bias_rows, HEADS),
+                    ((0, 0), (0, share - bias_rows), (2, 126 - HEADS))).reshape(width, 128)
+    spare = jnp.where(jnp.arange(128)[None, :] == 1, g_gain_ffn, spare)
+    dkv2, d_part, spare, g_early = after(
+        dkv2, d_part, spare, fold_attn(g_early, 768, 512))
+    late = jnp.concatenate([dkv2[:rows], swap(dkv2[rows:], "cy")], axis=1)
+    def whole(half, other):
+        both = [v.reshape(steps, 1, -1, v.shape[-1]) for v in (half, other)]
+        both = jnp.concatenate([pick_half(par, *both), pick_half(par, *both[::-1])], axis=1)
+        return up32(both.reshape(-1, half.shape[-1]))
+
+    in_grad, g_late = in_back(late, w_late, d_part, x, h1, gain_attn, d_mid, spare)
+    in_grad = jnp.transpose(in_grad).reshape(layer_in.shape)
+    g_late, g_early, half_d, piece_up = after(g_late, g_early, half_d, piece_up)
+    last = lax.all_gather(jnp.stack([piece_gate, piece_up]), ("cz", "cy"), axis=1, tiled=True)
+    other_d = swap(half_d, "cy")
+    g_late = up32(ctx_gather(ctx_scatter(fold_attn(g_late, 512), bits), bits)[:share])
+    g_early = up32(ctx_gather(ctx_scatter(g_early, bits), bits)[:share])
+    grad_down_t, grad_gate, grad_up = whole(half_d, other_d), up32(last[0]), up32(last[1])
+    cols = lambda g, *starts: jnp.concatenate([g[:, a : a + HDIM] for a in starts], axis=1)
+    k, v = lambda p: cols(g_late, 256 * p, 256 * p + 64), lambda p: cols(g_late, 256 * p + 128, 256 * p + 192)
+    third = lambda p, a: cols(g_early, 384 * p + a)
+    grad_key = jnp.concatenate([k(0), third(0, 128), k(1), third(1, 128)], axis=1)
+    grad_value = jnp.concatenate([v(0), third(0, 192), v(1), third(1, 192)], axis=1)
+    grad_query = cols(g_early, 0, 64, 256, 384, 448, 640)
+    grad_out = jnp.transpose(cols(g_early, *[768 + a for a in (0, 64, 192, 256, 320, 448)]))
+    rest = g_late[:, 512:]
     return (
         layer_out, in_grad, grad_query, grad_key, grad_value, grad_out, grad_gate, grad_up,
         jnp.transpose(grad_down_t), rest[:, 0], rest[:, 1], rest[:bias_rows, 2 : 2 + HEADS],

time: 915 us -> 884 us (0.966)
  waiting for transfers between devices: 335 us -> 231 us
  local copies, waits for them, and re-layouts: 48.5 us -> 88 us
  Pallas kernels: 324 us -> 346 us
  other arithmetic: 95.7 us -> 114 us
  starting transfers between devices: 49.6 us -> 35.4 us
    ppermute x48 -> x46, waiting for transfers between devices: 163 us -> 109 us  [swap(): return lax.ppermute(x, axis, [(0, 1), (1, 0)])]
    reduce_scatter x2, waiting for transfers between devices: 42.7 us -> 0.01 us  [on_device(): lax.psum_scatter(v, 'cz', scatter_dimension=dim, tiled=True)]
    unnamed x178 -> x221, local copies, waits for them, and re-layouts: 24.1 us -> 50.3 us
    all_gather x2, waiting for transfers between devices: 49.7 us -> 28.6 us  [on_device(): lax.all_gather(v, 'cz', axis=0, tiled=True).reshape(NBLK, BLK, v.shape[-1])]
    ppermute x8, waiting for transfers between devices: 38.2 us -> 53.8 us  [ctx_bits(): lax.ppermute(x, 'cz', perm)]
    pallas_call x0 -> x2, Pallas kernels: none -> 12.7 us  [the longest x1 10.4 us: in_part(): pl.pallas_call(in_part_kernel, out_shape=(jax.ShapeDtypeStruct((width, ro...]
    ppermute x48 -> x46, starting transfers between devices: 38.1 us -> 32.3 us  [swap(): return lax.ppermute(x, axis, [(0, 1), (1, 0)])]
  transfers between devices with their start and end apart: 68 -> 64, of which waited for: 32 -> 25; matrix products, arithmetic and copies ran while one was open for 15% -> 21% of each run, Pallas kernels for 31% -> 34%
where the time goes in v3:
time: 884 us; the launch traced here: 875 us
  Pallas kernels  346 us (39%)
  waiting for transfers between devices  231 us (26%)
  other arithmetic  114 us (13%)
  local copies, waits for them, and re-layouts  88 us (10%)
  matrix products  44.6 us (5%)
  starting transfers between devices  35.4 us (4%)
  between operations  16.1 us (2%)
    pallas_call x2, Pallas kernels, attn_bwd(): pl.pallas_call(functools.partial(bwd_kernel, n, one), out_shape=(jax.Shap...  110 us
    ppermute x46, waiting for transfers between devices, swap(): return lax.ppermute(x, axis, [(0, 1), (1, 0)])  109 us
    pallas_call x2, Pallas kernels, ffn_pair(): pl.pallas_call(ffn_kernel, grid=(units // 128,), out_shape=[jax.ShapeDtyp...  86.9 us
    pallas_call x2, Pallas kernels, attn_fwd(): pl.pallas_call(functools.partial(fwd_kernel, n, one), out_shape=(jax.Shap...  76.3 us
    ppermute x8, waiting for transfers between devices, ctx_bits(): lax.ppermute(x, 'cz', perm)  53.8 us
    unnamed x221, local copies, waits for them, and re-layouts  50.3 us
    pallas_call x1, Pallas kernels, ffn_back(): pl.pallas_call(ffn_back_kernel, out_shape=(jax.ShapeDtypeStruct((width, r...  38.1 us
    dot_general x5, matrix products, dot_nn(): lax.dot_general(a, b, (((1,), (0,)), ((), ())), preferred_element_type=F32)  35.5 us
  transfers between devices with their start and end apart: 64, of which 25 were waited for; matrix products, arithmetic and copies ran while one was open for 21% of the time, Pallas kernels for 34%

profile of v3, /device:TPU:0, one launch (start us, length us, event | category | flops | bytes accessed | tf_op | source)
XLA Modules:
  0.0 875.5 jit_solution(14137614775363015036)
XLA Ops:
  10.5 2.7 pack.1
  13.3 2.5 fusion
  15.8 32.3 %all-gather.6.cloned.1.call-done = bf16[1472,1280]{1,0:T(8,128)(2,1)} async-done(((bf16[368,1280]{1,0:T(8,128)(2,1)}), bf16[1472,1280]{1,0:T(8,128)(2,1)}) %all-gather.6.cloned.1.call-update) | async-done | bytes 3768336 | tf_op jit(solution)/shard_map/all_gather | solution.py:905
  50.4 2.7 fusion.2.h
  53.4 4.6 convolution_convert_fusion
  62.3 16.7 %collective-permute-done.3 = bf16[368,896]{1,0:T(8,128)(2,1)S(1)} collective-permute-done((bf16[368,896]{1,0:T(8,128)(2,1)S(1)}, bf16[368,896]{1,0:T(8,128)(2,1)S(1)}, u32[]{:S(2)}, u32[]{:S(2)}) %collective-permute-start.3) | collective-permute-done | bytes 659488 | tf_op jit(solution)/shard_map/ppermute | solution.py:842
  87.4 9.3 %collective-permute-done = bf16[1024,256]{1,0:T(8,128)(2,1)S(1)} collective-permute-done((bf16[1024,256]{1,0:T(8,128)(2,1)S(1)}, bf16[1024,256]{1,0:T(8,128)(2,1)S(1)}, u32[]{:S(2)}, u32[]{:S(2)}) %collective-permute-start) | collective-permute-done | bytes 524320 | tf_op jit(solution)/shard_map/ppermute | solution.py:842
  110.9 2.5 slice.337
  116.5 2.7 fusion.66
  119.2 3.3 fusion.67
  128.1 3.3 pad_maximum_fusion.3.w_qkv
  134.1 28.6 %all-gather.12.cloned.1.call-done = bf16[8,1024,256]{2,1,0:T(8,128)(2,1)} async-done(((bf16[2,1024,256]{2,1,0:T(8,128)(2,1)}), bf16[8,1024,256]{2,1,0:T(8,128)(2,1)}) %all-gather.12.cloned.1.call-update) | async-done | bytes 4194320 | tf_op jit(solution)/shard_map/all_gather | solution.py:930
  169.2 43.3 %attn_fwd_two.1 = (bf16[32,64,128]{2,1,0:T(8,128)(2,1)S(1)}, f32[8,2,1,256]{3,2,1,0:T(1,128)S(1)}) custom-call(s32[288]{0:T(512)S(1)} %copy-done.43, bf16[128,64,256]{2,1,0:T(8,128)(2,1)S(1)} %bitcast.170, bf16[32,64,128]{2,1,0:T(8,128)(2,1)S(1)} %bitcast.175, f32[192,128]{1,0:T(8,128)S(1)} %copy-done.37, bf16[2,2,192,128]{3,2,1,0:T(8,128)(2,1)S(1)} %copy-done.21, ...), custom_call_target="tpu_custom_call" | custom-call | flops 1048576 | bytes 1048576 | tf_op jit(solution)/shard_map/attn_fwd_two/pallas_call | solution.py:398
  222.2 33.0 %attn_fwd_one.1 = (bf16[32,64,128]{2,1,0:T(8,128)(2,1)S(1)}, f32[8,1,1,256]{3,2,1,0:T(1,128)S(1)}) custom-call(s32[288]{0:T(512)S(1)} %copy-done.44, bf16[128,64,128]{2,1,0:T(8,128)(2,1)S(1)} %bitcast.171, bf16[32,64,128]{2,1,0:T(8,128)(2,1)S(1)} %bitcast.173, f32[192,128]{1,0:T(8,128)S(1)} %copy-done.29, bf16[2,1,192,128]{3,2,1,0:T(8,128)(2,1)S(1)} %copy-done.31, ...), custom_call_target="tpu_custom_call" | custom-call | flops 1048576 | bytes 1048576 | tf_op jit(solution)/shard_map/attn_fwd_one/pallas_call | solution.py:398
  255.3 3.1 collective-permute-done.7
  260.8 2.5 constant_dynamic-update-slice_fusion.wda
  265.6 7.5 collective-permute-done.8
  273.1 4.5 multiply_reduce_fusion
  277.7 2.6 multiply_convert_fusion.h
  280.2 43.5 %ffn_pair.2 = (bf16[896,1024]{1,0:T(8,128)(2,1)S(1)}, bf16[896,1024]{1,0:T(8,128)(2,1)S(1)}, bf16[896,1024]{1,0:T(8,128)(2,1)S(1)}, bf16[896,1024]{1,0:T(8,128)(...) custom-call(bf16[1472,1024]{1,0:T(8,128)(2,1)} %multiply_convert_fus, ...), custom_call_target="tpu_custom_call" | custom-call | flops 1048576 | bytes 1048576 | tf_op jit(solution)/shard_map/ffn_pair/pallas_call | solution.py:590
  325.0 7.6 fusion.84
  332.6 8.0 add_add_fusion
  340.7 2.6 convert_add_fusion.4
  343.3 2.4 add_convert_fusion.1
  357.2 43.4 %ffn_pair.3 = (bf16[896,1024]{1,0:T(8,128)(2,1)S(1)}, bf16[896,1024]{1,0:T(8,128)(2,1)S(1)}, bf16[896,1024]{1,0:T(8,128)(2,1)S(1)}, bf16[896,1024]{1,0:T(8,128)(...) custom-call(bf16[1472,1024]{1,0:T(8,128)(2,1)} %multiply_convert_fus, ...), custom_call_target="tpu_custom_call" | custom-call | flops 1048576 | bytes 1048576 | tf_op jit(solution)/shard_map/ffn_pair/pallas_call | solution.py:590
  402.3 4.8 add_convert_fusion.2
  410.2 3.2 slice_convert_fusion.1
  413.4 38.1 %ffn_back.1 = (f32[1472,1024]{1,0:T(8,128)}, bf16[1472,1024]{1,0:T(8,128)(2,1)}, bf16[1024,512]{1,0:T(8,128)(2,1)}, f32[1472,1]{1,0:T(8,128)}) custom-call(bf16[896,1024]{1,0:T(8,128)(2,1)} %copy-done.18, bf16[896,1024]{1,0:T(8,128)(2,1)} %copy-done.19, bf16[896,1024]{1,0:T(8,128)(2,1)} %copy-done.15, bf16[896,1024]{1,0:T(8,128)(2,1)} %copy-done.16, ...), custom_call_target="tpu_custom_call" | custom-call | flops 1048576 | bytes 1048576 | tf_op jit(solution)/shard_map/ffn_back/pallas_call | solution.py:698
  456.4 5.7 collective-permute-done.20
  463.3 3.7 collective-permute-done.21
  467.9 2.9 slice_select_fusion.2
  471.2 2.6 convert_add_fusion.2
  473.8 2.4 copy-done.57
  478.6 3.0 fusion.9
  489.3 42.8 %attn_bwd_one.1 = (bf16[32,64,128]{2,1,0:T(8,128)(2,1)S(1)}, bf16[128,64,128]{2,1,0:T(8,128)(2,1)S(1)}, f32[192,128]{1,0:T(8,128)S(1)}, f32[1,192,128]{2,1,0:T(8,128)S(1)}) custom-call(s32[288]{0:T(512)S(1)} %copy-done.45, bf16[128,64,128]{2,1,0:T(8,128)(2,1)S(1)} %bitcast.172, bf16[32,64,128]{2,1,0:T(8,128)(2,1)S(1)} %bitcast.174, ...), custom_call_target="tpu_custom_call" | custom-call | flops 1048576 | bytes 1048576 | tf_op jit(solution)/shard_map/attn_bwd_one/pallas_call | solution.py:426
  532.2 3.8 slice_select_fusion.1
  536.0 2.9 fusion.10
  539.8 4.6 collective-permute-done.29
  544.4 4.2 convert_add_fusion.1
  551.6 67.4 %attn_bwd_two.1 = (bf16[32,64,128]{2,1,0:T(8,128)(2,1)S(1)}, bf16[128,64,256]{2,1,0:T(8,128)(2,1)S(1)}, f32[192,128]{1,0:T(8,128)S(1)}, f32[2,192,128]{2,1,0:T(8,128)S(1)}) custom-call(s32[288]{0:T(512)S(1)} %copy-done.46, bf16[128,64,256]{2,1,0:T(8,128)(2,1)} %bitcast.169, bf16[32,64,128]{2,1,0:T(8,128)(2,1)S(1)} %bitcast.176, ...), custom_call_target="tpu_custom_call" | custom-call | flops 1048576 | bytes 1048576 | tf_op jit(solution)/shard_map/attn_bwd_two/pallas_call | solution.py:426
  627.8 5.5 convolution_convert_fusion.1
  642.9 5.2 collective-permute-done.31
  649.8 2.4 collective-permute-done.32
  657.2 10.4 %in_part.1 = (f32[1472,1024]{1,0:T(8,128)}, bf16[1472,768]{1,0:T(8,128)(2,1)S(1)}) custom-call(bf16[1024,768]{1,0:T(8,128)(2,1)} %constant_dynamic-update-slice_fusion.3.d_qkv, bf16[1472,768]{1,0:T(8,128)(2,1)S(1)} %copy-done.2, bf16[1472,1024]{1,0:T(8,128)(2,1)S(1)} %fusion.2.h), custom_call_target="tpu_custom_call" | custom-call | flops 1048576 | bytes 1048576 | tf_op jit(solution)/shard_map/in_part/pallas_call | solution.py:743
  672.6 2.8 slice_select_fusion
  676.0 2.6 fusion.12
  681.5 2.9 fusion.7
  684.5 17.3 %collective-permute-done.36 = bf16[368,1280]{1,0:T(8,128)(2,1)} collective-permute-done((bf16[368,1280]{1,0:T(8,128)(2,1)}, bf16[368,1280]{1,0:T(8,128)(2,1)}, u32[]{:S(2)}, u32[]{:S(2)}) %collective-permute-start.36) | collective-permute-done | bytes 942112 | tf_op jit(solution)/shard_map/ppermute | solution.py:842
  708.4 11.5 %collective-permute-done.37 = bf16[1024,256]{1,0:T(8,128)(2,1)S(1)} collective-permute-done((bf16[1024,256]{1,0:T(8,128)(2,1)S(1)}, bf16[1024,256]{1,0:T(8,128)(2,1)S(1)}, u32[]{:S(2)}, u32[]{:S(2)}) %collective-permute-start.37) | collective-permute-done | bytes 524320 | tf_op jit(solution)/shard_map/ppermute | solution.py:842
  721.0 18.8 %in_back.1 = (bf16[1472,1024]{1,0:T(8,128)(2,1)}, bf16[1472,640]{1,0:T(8,128)(2,1)}) custom-call(bf16[1024,512]{1,0:T(8,128)(2,1)} %pad_maximum_fusion.6.d_qkv, bf16[1472,512]{1,0:T(8,128)(2,1)} %pad_maximum_fusion.4.w_qkv, f32[1472,1024]{1,0:T(8,128)} %get-tuple-element.231.part, bf16[1472,1024]{1,0:T(8,128)(2,1)} %bitcast.196, bf16[1472,1024]{1,0:T(8,128)(2,1)} %copy-done, ...), custom_call_target="tpu_custom_call" | custom-call | flops 1048576 | bytes 1048576 | tf_op jit(solution)/shard_map/in_back/pallas_call | solution.py:784
  743.0 6.9 fusion.85
  757.1 3.5 collective-permute-done.39
  762.8 7.5 fusion.4
  770.9 5.2 collective-permute-done.40
  777.8 12.9 %collective-permute-done.41 = bf16[48,1280]{1,0:T(8,128)(2,1)S(1)} collective-permute-done((bf16[48,1280]{1,0:T(8,128)(2,1)S(1)}, bf16[48,1280]{1,0:T(8,128)(2,1)S(1)}, u32[]{:S(2)}, u32[]{:S(2)}) %collective-permute-start.41) | collective-permute-done | bytes 122912 | tf_op jit(solution)/shard_map/ppermute | solution.py:866
  790.8 15.8 %collective-permute-done.47 = bf16[192,640]{1,0:T(8,128)(2,1)S(1)} collective-permute-done((bf16[192,640]{1,0:T(8,128)(2,1)S(1)}, bf16[192,640]{1,0:T(8,128)(2,1)S(1)}, u32[]{:S(2)}, u32[]{:S(2)}) %collective-permute-start.47) | collective-permute-done | bytes 245792 | tf_op jit(solution)/shard_map/ppermute | solution.py:842
  807.3 12.6 %collective-permute-done.48 = bf16[96,640]{1,0:T(8,128)(2,1)S(1)} collective-permute-done((bf16[96,640]{1,0:T(8,128)(2,1)S(1)}, bf16[96,640]{1,0:T(8,128)(2,1)S(1)}, u32[]{:S(2)}, u32[]{:S(2)}) %collective-permute-start.48) | collective-permute-done | bytes 122912 | tf_op jit(solution)/shard_map/ppermute | solution.py:866
  820.3 6.5 collective-permute-done.49
  827.2 7.8 collective-permute-done.50
  835.2 2.9 convert_bitcast_fusion
  838.1 5.3 collective-permute-done.51
  846.4 3.4 collective-permute-done.52
  853.5 7.3 all-gather.14.cloned.1.call-done
  860.8 7.3 fusion.5
  (468 shorter events, 167.6 us)
Async XLA Ops:
  7.2 41.0 %all-gather.6.cloned.1.call-start = ((), (), s32[]{:S(2)}) async-start(), calls=%async_computation.4 | async-start | bytes 4710400 | tf_op jit(solution)/shard_map/all_gather | solution.py:905
  13.3 149.5 %all-gather.12.cloned.1.call-start = ((), (), s32[]{:S(2)}) async-start(), calls=%async_computation.7 | async-start | bytes 5242880 | tf_op jit(solution)/shard_map/all_gather | solution.py:930
  58.2 20.7 %collective-permute-start.2 = (bf16[1024,384]{1,0:T(8,128)(2,1)S(1)}, bf16[1024,384]{1,0:T(8,128)(2,1)S(1)}, u32[]{:S(2)}, u32[]{:S(2)}) collective-permute-start(bf16[1024,384]{1,0:T(8,128)(2,1)S(1)} %get-tuple-element.268), channel_id=1, source_target_pairs={{0,4},{4,0},{1,5},{5,1},{2,6},{6,2},{3,7},{7,3},{8,12},{12,8},{9,1... | collective-permute-start | bytes 2359304 | tf_op jit(solution)/shard_map/ppermute | solution.py:842
  62.0 17.0 %collective-permute-start.3 = (bf16[368,896]{1,0:T(8,128)(2,1)S(1)}, bf16[368,896]{1,0:T(8,128)(2,1)S(1)}, u32[]{:S(2)}, u32[]{:S(2)}) collective-permute-start(bf16[368,896]{1,0:T(8,128)(2,1)S(1)} %get-tuple-element.266), channel_id=1, source_target_pairs={{0,2},{2,0},{1,3},{3,1},{4,6},{6,4},{5,7},{7,5},{8,10},{10,8},{9,1... | collective-permute-start | bytes 1978376 | tf_op jit(solution)/shard_map/ppermute | solution.py:842
  81.8 132.1 %all-gather.10.cloned.1.call-start = ((), (), s32[]{:S(2)}) async-start(), calls=%async_computation.6 | async-start | bytes 2621440 | tf_op jit(solution)/shard_map/all_gather | solution.py:930
  82.0 16.4 %collective-permute-start.1 = (bf16[368,896]{1,0:T(8,128)(2,1)}, bf16[368,896]{1,0:T(8,128)(2,1)S(1)}, u32[]{:S(2)}, u32[]{:S(2)}) collective-permute-start(bf16[368,896]{1,0:T(8,128)(2,1)} %get-tuple-element.267), channel_id=1, source_target_pairs={{0,2},{2,0},{1,3},{3,1},{4,6},{6,4},{5,7},{7,5},{8,10},{10,8},{9,1... | collective-permute-start | bytes 1978376 | tf_op jit(solution)/shard_map/ppermute | solution.py:842
  83.6 13.0 %collective-permute-start = (bf16[1024,256]{1,0:T(8,128)(2,1)S(1)}, bf16[1024,256]{1,0:T(8,128)(2,1)S(1)}, u32[]{:S(2)}, u32[]{:S(2)}) collective-permute-start(bf16[1024,256]{1,0:T(8,128)(2,1)S(1)} %get-tuple-element.270), channel_id=1, source_target_pairs={{0,4},{4,0},{1,5},{5,1},{2,6},{6,2},{3,7},{7,3},{8,12},{12,8},{9,1... | collective-permute-start | bytes 1572872 | tf_op jit(solution)/shard_map/ppermute | solution.py:842
  99.4 166.2 %all-gather.8.cloned.1.call-start = ((), (), s32[]{:S(2)}) async-start(), calls=%async_computation.5 | async-start | bytes 1884160 | tf_op jit(solution)/shard_map/all_gather | solution.py:915
  107.5 150.9 %collective-permute-start.5 = (bf16[1472,896]{1,0:T(8,128)(2,1)}, bf16[1472,896]{1,0:T(8,128)(2,1)}, u32[]{:S(2)}, u32[]{:S(2)}) collective-permute-start(bf16[1472,896]{1,0:T(8,128)(2,1)} %refs_8_.1), channel_id=1, source_target_pairs={{0,2},{2,0},{1,3},{3,1},{4,6},{6,4},{5,7},{7,5},{8,10},{10,8},{9,1... | collective-permute-start | bytes 7913480 | tf_op jit(solution)/shard_map/ppermute | solution.py:842
  107.8 150.6 %collective-permute-start.6 = (bf16[1472,896]{1,0:T(8,128)(2,1)}, bf16[1472,896]{1,0:T(8,128)(2,1)}, u32[]{:S(2)}, u32[]{:S(2)}) collective-permute-start(bf16[1472,896]{1,0:T(8,128)(2,1)} %refs_12_.1), channel_id=1, source_target_pairs={{0,2},{2,0},{1,3},{3,1},{4,6},{6,4},{5,7},{7,5},{8,10},{10,8},{9,1... | collective-permute-start | bytes 7913480 | tf_op jit(solution)/shard_map/ppermute | solution.py:842
  116.2 142.2 %collective-permute-start.7 = (bf16[736,896]{1,0:T(8,128)(2,1)}, bf16[736,896]{1,0:T(8,128)(2,1)}, u32[]{:S(2)}, u32[]{:S(2)}) collective-permute-start(bf16[736,896]{1,0:T(8,128)(2,1)} %slice.337), channel_id=1, source_target_pairs={{0,2},{2,0},{1,3},{3,1},{4,6},{6,4},{5,7},{7,5},{8,10},{10,8},{9,1... | collective-permute-start | bytes 3956744 | tf_op jit(solution)/shard_map/ppermute | solution.py:842
  125.7 496.5 %all-reduce.9.cloned.1.call-start = ((), (), s32[]{:S(2)}) async-start(), calls=%async_computation.9 | async-start | bytes 2637824 | tf_op jit(solution)/shard_map/psum | solution.py:989
  215.7 42.7 %collective-permute-start.4 = (bf16[1024,128]{1,0:T(8,128)(2,1)S(1)}, bf16[1024,128]{1,0:T(8,128)(2,1)S(1)}, u32[]{:S(2)}, u32[]{:S(2)}) collective-permute-start(bf16[1024,128]{1,0:T(8,128)(2,1)S(1)} %bitcast.227), channel_id=1, source_target_pairs={{0,4},{4,0},{1,5},{5,1},{2,6},{6,2},{3,7},{7,3},{8,12},{12,8},{9,1... | collective-permute-start | bytes 786440 | tf_op jit(solution)/shard_map/ppermute | solution.py:842
  258.4 21.8 %collective-permute-start.9 = (bf16[1472,896]{1,0:T(8,128)(2,1)}, bf16[1472,896]{1,0:T(8,128)(2,1)}, u32[]{:S(2)}, u32[]{:S(2)}) collective-permute-start(bf16[1472,896]{1,0:T(8,128)(2,1)} %collective-permute-done.5.wga.refs_10_), channel_id=1, source_target_pairs={{0,1},{1,0},{2,3},{3,2},{4,5},{5,4},{6,7},{7,6},{8,9},{9,8},{10,11... | collective-permute-start | bytes 7913480 | tf_op jit(solution)/shard_map/ppermute | solution.py:842
  258.5 21.8 %collective-permute-start.10 = (bf16[1472,896]{1,0:T(8,128)(2,1)}, bf16[1472,896]{1,0:T(8,128)(2,1)}, u32[]{:S(2)}, u32[]{:S(2)}) collective-permute-start(bf16[1472,896]{1,0:T(8,128)(2,1)} %collective-permute-done.6.wua.refs_14_), channel_id=1, source_target_pairs={{0,1},{1,0},{2,3},{3,2},{4,5},{5,4},{6,7},{7,6},{8,9},{9,8},{10,11... | collective-permute-start | bytes 7913480 | tf_op jit(solution)/shard_map/ppermute | solution.py:842
  263.2 17.0 %collective-permute-start.11 = (bf16[1472,896]{1,0:T(8,128)(2,1)}, bf16[1472,896]{1,0:T(8,128)(2,1)}, u32[]{:S(2)}, u32[]{:S(2)}) collective-permute-start(bf16[1472,896]{1,0:T(8,128)(2,1)} %constant_dynamic-update-slice_fusion.wda), channel_id=1, source_target_pairs={{0,1},{1,0},{2,3},{3,2},{4,5},{5,4},{6,7},{7,6},{8,9},{9,8},{10,11... | collective-permute-start | bytes 7913480 | tf_op jit(solution)/shard_map/ppermute | solution.py:842
  264.2 9.0 %collective-permute-start.8 = (bf16[1024,128]{1,0:T(8,128)(2,1)}, bf16[1024,128]{1,0:T(8,128)(2,1)}, u32[]{:S(2)}, u32[]{:S(2)}) collective-permute-start(bf16[1024,128]{1,0:T(8,128)(2,1)} %get-tuple-element.313), channel_id=1, source_target_pairs={{0,4},{4,0},{1,5},{5,1},{2,6},{6,2},{3,7},{7,3},{8,12},{12,8},{9,1... | collective-permute-start | bytes 786440 | tf_op jit(solution)/shard_map/ppermute | solution.py:842
  323.8 16.8 %collective-permute-start.12 = (bf16[1472,896]{1,0:T(8,128)(2,1)}, bf16[1472,896]{1,0:T(8,128)(2,1)}, u32[]{:S(2)}, u32[]{:S(2)}) collective-permute-start(bf16[1472,896]{1,0:T(8,128)(2,1)} %get-tuple-element.158), channel_id=1, source_target_pairs={{0,1},{1,0},{2,3},{3,2},{4,5},{5,4},{6,7},{7,6},{8,9},{9,8},{10,11... | collective-permute-start | bytes 7913480 | tf_op jit(solution)/shard_map/ppermute | solution.py:842
  323.9 19.4 %collective-permute-start.13 = (bf16[1472,896]{1,0:T(8,128)(2,1)}, bf16[1472,896]{1,0:T(8,128)(2,1)}, u32[]{:S(2)}, u32[]{:S(2)}) collective-permute-start(bf16[1472,896]{1,0:T(8,128)(2,1)} %get-tuple-element.160), channel_id=1, source_target_pairs={{0,1},{1,0},{2,3},{3,2},{4,5},{5,4},{6,7},{7,6},{8,9},{9,8},{10,11... | collective-permute-start | bytes 7913480 | tf_op jit(solution)/shard_map/ppermute | solution.py:842
  324.4 28.2 %collective-permute-start.17 = (bf16[1472,896]{1,0:T(8,128)(2,1)}, bf16[1472,896]{1,0:T(8,128)(2,1)S(1)}, u32[]{:S(2)}, u32[]{:S(2)}) collective-permute-start(bf16[1472,896]{1,0:T(8,128)(2,1)} %bitcast.204), channel_id=1, source_target_pairs={{0,1},{1,0},{2,3},{3,2},{4,5},{5,4},{6,7},{7,6},{8,9},{9,8},{10,11... | collective-permute-start | bytes 7913480 | tf_op jit(solution)/shard_map/ppermute | solution.py:842
  324.5 28.2 %collective-permute-start.15 = (bf16[1472,896]{1,0:T(8,128)(2,1)}, bf16[1472,896]{1,0:T(8,128)(2,1)S(1)}, u32[]{:S(2)}, u32[]{:S(2)}) collective-permute-start(bf16[1472,896]{1,0:T(8,128)(2,1)} %refs_8_.1), channel_id=1, source_target_pairs={{0,1},{1,0},{2,3},{3,2},{4,5},{5,4},{6,7},{7,6},{8,9},{9,8},{10,11... | collective-permute-start | bytes 7913480 | tf_op jit(solution)/shard_map/ppermute | solution.py:842
  324.9 23.5 %collective-permute-start.14 = (bf16[1472,896]{1,0:T(8,128)(2,1)}, bf16[1472,896]{1,0:T(8,128)(2,1)S(1)}, u32[]{:S(2)}, u32[]{:S(2)}) collective-permute-start(bf16[1472,896]{1,0:T(8,128)(2,1)} %get-tuple-element.162), channel_id=1, source_target_pairs={{0,1},{1,0},{2,3},{3,2},{4,5},{5,4},{6,7},{7,6},{8,9},{9,8},{10,11... | collective-permute-start | bytes 7913480 | tf_op jit(solution)/shard_map/ppermute | solution.py:842
  340.6 15.1 %collective-permute-start.16 = (bf16[1472,896]{1,0:T(8,128)(2,1)S(1)}, bf16[1472,896]{1,0:T(8,128)(2,1)S(1)}, u32[]{:S(2)}, u32[]{:S(2)}) collective-permute-start(bf16[1472,896]{1,0:T(8,128)(2,1)S(1)} %copy-done.62), channel_id=1, source_target_pairs={{0,1},{1,0},{2,3},{3,2},{4,5},{5,4},{6,7},{7,6},{8,9},{9,8},{10,11... | collective-permute-start | bytes 7913480 | tf_op jit(solution)/shard_map/ppermute | solution.py:842
  350.6 50.1 %collective-permute-start.19 = (bf16[976,896]{1,0:T(8,128)(2,1)}, bf16[976,896]{1,0:T(8,128)(2,1)S(1)}, u32[]{:S(2)}, u32[]{:S(2)}) collective-permute-start(bf16[976,896]{1,0:T(8,128)(2,1)} %slice.424), channel_id=1, source_target_pairs={{0,2},{2,0},{1,3},{3,1},{4,6},{6,4},{5,7},{7,5},{8,10},{10,8},{9,1... | collective-permute-start | bytes 5246984 | tf_op jit(solution)/shard_map/ppermute | solution.py:842
  350.9 49.8 %collective-permute-start.18 = (bf16[736,896]{1,0:T(8,128)(2,1)S(1)}, bf16[736,896]{1,0:T(8,128)(2,1)}, u32[]{:S(2)}, u32[]{:S(2)}) collective-permute-start(bf16[736,896]{1,0:T(8,128)(2,1)S(1)} %bitcast.218), channel_id=1, source_target_pairs={{0,4},{4,0},{1,5},{5,1},{2,6},{6,2},{3,7},{7,3},{8,12},{12,8},{9,1... | collective-permute-start | bytes 3956744 | tf_op jit(solution)/shard_map/ppermute | solution.py:842
  400.7 7.8 collective-permute-start.23
  400.8 53.0 %collective-permute-start.25 = (bf16[496,896]{1,0:T(8,128)(2,1)}, bf16[496,896]{1,0:T(8,128)(2,1)}, u32[]{:S(2)}, u32[]{:S(2)}) collective-permute-start(bf16[496,896]{1,0:T(8,128)(2,1)} %slice.425), channel_id=1, source_target_pairs={{0,2},{2,0},{1,3},{3,1},{4,6},{6,4},{5,7},{7,5},{8,10},{10,8},{9,1... | collective-permute-start | bytes 2666504 | tf_op jit(solution)/shard_map/ppermute | solution.py:842
  407.1 63.7 %collective-permute-start.22 = (bf16[736,896]{1,0:T(8,128)(2,1)}, bf16[736,896]{1,0:T(8,128)(2,1)}, u32[]{:S(2)}, u32[]{:S(2)}) collective-permute-start(bf16[736,896]{1,0:T(8,128)(2,1)} %add_convert_fusion.2), channel_id=1, source_target_pairs={{0,2},{2,0},{1,3},{3,1},{4,6},{6,4},{5,7},{7,5},{8,10},{10,8},{9,1... | collective-permute-start | bytes 3956744 | tf_op jit(solution)/shard_map/ppermute | solution.py:842
  408.6 62.3 %collective-permute-start.26 = (bf16[1472,896]{1,0:T(8,128)(2,1)}, bf16[1472,896]{1,0:T(8,128)(2,1)}, u32[]{:S(2)}, u32[]{:S(2)}) collective-permute-start(bf16[1472,896]{1,0:T(8,128)(2,1)} %get-tuple-element.202), channel_id=1, source_target_pairs={{0,1},{1,0},{2,3},{3,2},{4,5},{5,4},{6,7},{7,6},{8,9},{9,8},{10,11... | collective-permute-start | bytes 7913480 | tf_op jit(solution)/shard_map/ppermute | solution.py:842
  409.6 61.2 %collective-permute-start.24 = (bf16[736,896]{1,0:T(8,128)(2,1)S(1)}, bf16[736,896]{1,0:T(8,128)(2,1)S(1)}, u32[]{:S(2)}, u32[]{:S(2)}) collective-permute-start(bf16[736,896]{1,0:T(8,128)(2,1)S(1)} %bitcast.217), channel_id=1, source_target_pairs={{0,4},{4,0},{1,5},{5,1},{2,6},{6,2},{3,7},{7,3},{8,12},{12,8},{9,1... | collective-permute-start | bytes 3956744 | tf_op jit(solution)/shard_map/ppermute | solution.py:842
  452.9 9.2 %collective-permute-start.20 = (bf16[1024,128]{1,0:T(8,128)(2,1)S(1)}, bf16[1024,128]{1,0:T(8,128)(2,1)S(1)}, u32[]{:S(2)}, u32[]{:S(2)}) collective-permute-start(bf16[1024,128]{1,0:T(8,128)(2,1)S(1)} %get-tuple-element.292), channel_id=1, source_target_pairs={{0,4},{4,0},{1,5},{5,1},{2,6},{6,2},{3,7},{7,3},{8,12},{12,8},{9,1... | collective-permute-start | bytes 786440 | tf_op jit(solution)/shard_map/ppermute | solution.py:842
  453.8 13.2 %collective-permute-start.21 = (bf16[1024,128]{1,0:T(8,128)(2,1)S(1)}, bf16[1024,128]{1,0:T(8,128)(2,1)S(1)}, u32[]{:S(2)}, u32[]{:S(2)}) collective-permute-start(bf16[1024,128]{1,0:T(8,128)(2,1)S(1)} %get-tuple-element.291), channel_id=1, source_target_pairs={{0,4},{4,0},{1,5},{5,1},{2,6},{6,2},{3,7},{7,3},{8,12},{12,8},{9,1... | collective-permute-start | bytes 786440 | tf_op jit(solution)/shard_map/ppermute | solution.py:842
  462.1 73.9 %collective-permute-start.28 = (bf16[1472,896]{1,0:T(8,128)(2,1)}, bf16[1472,896]{1,0:T(8,128)(2,1)}, u32[]{:S(2)}, u32[]{:S(2)}) collective-permute-start(bf16[1472,896]{1,0:T(8,128)(2,1)} %add_convert_fusion), channel_id=1, source_target_pairs={{0,2},{2,0},{1,3},{3,1},{4,6},{6,4},{5,7},{7,5},{8,10},{10,8},{9,1... | collective-permute-start | bytes 7913480 | tf_op jit(solution)/shard_map/ppermute | solution.py:842
  477.5 58.6 %collective-permute-start.27 = (bf16[736,896]{1,0:T(8,128)(2,1)}, bf16[736,896]{1,0:T(8,128)(2,1)}, u32[]{:S(2)}, u32[]{:S(2)}) collective-permute-start(bf16[736,896]{1,0:T(8,128)(2,1)} %bitcast.46), channel_id=1, source_target_pairs={{0,4},{4,0},{1,5},{5,1},{2,6},{6,2},{3,7},{7,3},{8,12},{12,8},{9,1... | collective-permute-start | bytes 3956744 | tf_op jit(solution)/shard_map/ppermute | solution.py:842
  481.6 140.7 %reduce-scatter.13.cloned.1.call-start = ((), (), s32[]{:S(2)}) async-start(), calls=%async_computation.12 | async-start | bytes 1648640
  539.0 83.3 %reduce-scatter.9.cloned.1.call-start = ((), (), s32[]{:S(2)}) async-start(), calls=%async_computation.8 | async-start | bytes 2621440 | tf_op jit(solution)/shard_map/reduce_scatter | solution.py:988
  539.0 5.3 collective-permute-start.29
  539.7 165.9 %reduce-scatter.11.cloned.1.call-start = ((), (), s32[]{:S(2)}) async-start(), calls=%async_computation.10 | async-start | bytes 5242880 | tf_op jit(solution)/shard_map/reduce_scatter | solution.py:988
  550.0 72.2 %collective-permute-start.30 = (bf16[736,896]{1,0:T(8,128)(2,1)}, bf16[736,896]{1,0:T(8,128)(2,1)}, u32[]{:S(2)}, u32[]{:S(2)}) collective-permute-start(bf16[736,896]{1,0:T(8,128)(2,1)} %bitcast.50), channel_id=1, source_target_pairs={{0,4},{4,0},{1,5},{5,1},{2,6},{6,2},{3,7},{7,3},{8,12},{12,8},{9,1... | collective-permute-start | bytes 3956744 | tf_op jit(solution)/shard_map/ppermute | solution.py:842
  622.3 117.5 %reduce-scatter.15.cloned.1.call-start = ((), (), s32[]{:S(2)}) async-start(), calls=%async_computation.13 | async-start | bytes 1648640
  634.2 19.7 %collective-permute-start.33 = (bf16[1024,128]{1,0:T(8,128)(2,1)}, bf16[1024,128]{1,0:T(8,128)(2,1)}, u32[]{:S(2)}, u32[]{:S(2)}) collective-permute-start(bf16[1024,128]{1,0:T(8,128)(2,1)} %bitcast.57), channel_id=1, source_target_pairs={{0,4},{4,0},{1,5},{5,1},{2,6},{6,2},{3,7},{7,3},{8,12},{12,8},{9,1... | collective-permute-start | bytes 786440 | tf_op jit(solution)/shard_map/ppermute | solution.py:842
  637.5 10.6 %collective-permute-start.31 = (bf16[1024,128]{1,0:T(8,128)(2,1)}, bf16[1024,128]{1,0:T(8,128)(2,1)}, u32[]{:S(2)}, u32[]{:S(2)}) collective-permute-start(bf16[1024,128]{1,0:T(8,128)(2,1)} %bitcast.56), channel_id=1, source_target_pairs={{0,4},{4,0},{1,5},{5,1},{2,6},{6,2},{3,7},{7,3},{8,12},{12,8},{9,1... | collective-permute-start | bytes 786440 | tf_op jit(solution)/shard_map/ppermute | solution.py:842
  640.6 11.7 %collective-permute-start.32 = (bf16[1024,128]{1,0:T(8,128)(2,1)}, bf16[1024,128]{1,0:T(8,128)(2,1)}, u32[]{:S(2)}, u32[]{:S(2)}) collective-permute-start(bf16[1024,128]{1,0:T(8,128)(2,1)} %get-tuple-element.306), channel_id=1, source_target_pairs={{0,4},{4,0},{1,5},{5,1},{2,6},{6,2},{3,7},{7,3},{8,12},{12,8},{9,1... | collective-permute-start | bytes 786440 | tf_op jit(solution)/shard_map/ppermute | solution.py:842
  671.1 4.9 collective-permute-start.35
  675.5 9.0 %collective-permute-start.34 = (bf16[368,1280]{1,0:T(8,128)(2,1)}, bf16[368,1280]{1,0:T(8,128)(2,1)}, u32[]{:S(2)}, u32[]{:S(2)}) collective-permute-start(bf16[368,1280]{1,0:T(8,128)(2,1)} %get-tuple-element.256), channel_id=1, source_target_pairs={{0,1},{1,0},{2,3},{3,2},{4,5},{5,4},{6,7},{7,6},{8,9},{9,8},{10,11... | collective-permute-start | bytes 2826248 | tf_op jit(solution)/shard_map/ppermute | solution.py:842
  678.7 23.1 %collective-permute-start.36 = (bf16[368,1280]{1,0:T(8,128)(2,1)}, bf16[368,1280]{1,0:T(8,128)(2,1)}, u32[]{:S(2)}, u32[]{:S(2)}) collective-permute-start(bf16[368,1280]{1,0:T(8,128)(2,1)} %fusion.12), channel_id=1, source_target_pairs={{0,2},{2,0},{1,3},{3,1},{4,6},{6,4},{5,7},{7,5},{8,10},{10,8},{9,1... | collective-permute-start | bytes 2826248 | tf_op jit(solution)/shard_map/ppermute | solution.py:842
  684.4 176.4 %all-gather.14.cloned.1.call-start = ((), (), s32[]{:S(2)}) async-start(), calls=%async_computation.11 | async-start | bytes 5935104 | tf_op jit(solution)/shard_map/all_gather | solution.py:1044
  706.9 13.1 %collective-permute-start.37 = (bf16[1024,256]{1,0:T(8,128)(2,1)S(1)}, bf16[1024,256]{1,0:T(8,128)(2,1)S(1)}, u32[]{:S(2)}, u32[]{:S(2)}) collective-permute-start(bf16[1024,256]{1,0:T(8,128)(2,1)S(1)} %get-tuple-element.289), channel_id=1, source_target_pairs={{0,4},{4,0},{1,5},{5,1},{2,6},{6,2},{3,7},{7,3},{8,12},{12,8},{9,1... | collective-permute-start | bytes 1572872 | tf_op jit(solution)/shard_map/ppermute | solution.py:842
  741.4 11.6 %collective-permute-start.38 = (bf16[192,1280]{1,0:T(8,128)(2,1)S(1)}, bf16[192,1280]{1,0:T(8,128)(2,1)S(1)}, u32[]{:S(2)}, u32[]{:S(2)}) collective-permute-start(bf16[192,1280]{1,0:T(8,128)(2,1)S(1)} %select_convert_fusion.5), channel_id=1, source_target_pairs={{0,4},{4,0},{1,5},{5,1},{2,6},{6,2},{3,7},{7,3},{8,12},{12,8},{9,1... | collective-permute-start | bytes 1474568 | tf_op jit(solution)/shard_map/ppermute | solution.py:842
  751.0 2.4 collective-permute-start.45
  751.0 25.2 %collective-permute-start.44 = (bf16[368,640]{1,0:T(8,128)(2,1)}, bf16[368,640]{1,0:T(8,128)(2,1)}, u32[]{:S(2)}, u32[]{:S(2)}) collective-permute-start(bf16[368,640]{1,0:T(8,128)(2,1)} %get-tuple-element.282), channel_id=1, source_target_pairs={{0,1},{1,0},{2,3},{3,2},{4,5},{5,4},{6,7},{7,6},{8,9},{9,8},{10,11... | collective-permute-start | bytes 1413128 | tf_op jit(solution)/shard_map/ppermute | solution.py:842
  753.3 7.3 collective-permute-start.39
  755.5 20.7 %collective-permute-start.46 = (bf16[368,640]{1,0:T(8,128)(2,1)S(1)}, bf16[368,640]{1,0:T(8,128)(2,1)S(1)}, u32[]{:S(2)}, u32[]{:S(2)}) collective-permute-start(bf16[368,640]{1,0:T(8,128)(2,1)S(1)} %fusion.16), channel_id=1, source_target_pairs={{0,2},{2,0},{1,3},{3,1},{4,6},{6,4},{5,7},{7,5},{8,10},{10,8},{9,1... | collective-permute-start | bytes 1413128 | tf_op jit(solution)/shard_map/ppermute | solution.py:842
  760.7 15.4 %collective-permute-start.40 = (bf16[48,1280]{1,0:T(8,128)(2,1)S(1)}, bf16[48,1280]{1,0:T(8,128)(2,1)S(1)}, u32[]{:S(2)}, u32[]{:S(2)}) collective-permute-start(bf16[48,1280]{1,0:T(8,128)(2,1)S(1)} %select_convert_fusion.9), channel_id=1, source_target_pairs={{0,16},{8,24},{16,0},{24,8},{1,17},{9,25},{17,1},{25,9},{2,18},{10... | collective-permute-start | bytes 368648 | tf_op jit(solution)/shard_map/ppermute | solution.py:866
  770.2 49.8 %collective-permute-start.53 = (bf16[736,896]{1,0:T(8,128)(2,1)S(1)}, bf16[736,896]{1,0:T(8,128)(2,1)S(1)}, u32[]{:S(2)}, u32[]{:S(2)}) collective-permute-start(bf16[736,896]{1,0:T(8,128)(2,1)S(1)} %copy-done.87), channel_id=1, source_target_pairs={{0,4},{4,0},{1,5},{5,1},{2,6},{6,2},{3,7},{7,3},{8,12},{12,8},{9,1... | collective-permute-start | bytes 3956744 | tf_op jit(solution)/shard_map/ppermute | solution.py:842
  776.1 14.6 %collective-permute-start.41 = (bf16[48,1280]{1,0:T(8,128)(2,1)S(1)}, bf16[48,1280]{1,0:T(8,128)(2,1)S(1)}, u32[]{:S(2)}, u32[]{:S(2)}) collective-permute-start(bf16[48,1280]{1,0:T(8,128)(2,1)S(1)} %add_convert_fusion.3), channel_id=1, source_target_pairs={{0,16},{8,24},{16,0},{24,8},{1,17},{9,25},{17,1},{25,9},{2,18},{10... | collective-permute-start | bytes 368648 | tf_op jit(solution)/shard_map/ppermute | solution.py:866
  777.7 29.0 %collective-permute-start.47 = (bf16[192,640]{1,0:T(8,128)(2,1)S(1)}, bf16[192,640]{1,0:T(8,128)(2,1)S(1)}, u32[]{:S(2)}, u32[]{:S(2)}) collective-permute-start(bf16[192,640]{1,0:T(8,128)(2,1)S(1)} %select_convert_fusion.6), channel_id=1, source_target_pairs={{0,4},{4,0},{1,5},{5,1},{2,6},{6,2},{3,7},{7,3},{8,12},{12,8},{9,1... | collective-permute-start | bytes 737288 | tf_op jit(solution)/shard_map/ppermute | solution.py:842
  790.7 16.1 %collective-permute-start.42 = (bf16[96,1280]{1,0:T(8,128)(2,1)S(1)}, bf16[96,1280]{1,0:T(8,128)(2,1)S(1)}, u32[]{:S(2)}, u32[]{:S(2)}) collective-permute-start(bf16[96,1280]{1,0:T(8,128)(2,1)S(1)} %pad_maximum_fusion.20), channel_id=1, source_target_pairs={{0,8},{8,0},{16,24},{24,16},{1,9},{9,1},{17,25},{25,17},{2,10},{10... | collective-permute-start | bytes 737288 | tf_op jit(solution)/shard_map/ppermute | solution.py:866
  806.8 13.1 %collective-permute-start.48 = (bf16[96,640]{1,0:T(8,128)(2,1)S(1)}, bf16[96,640]{1,0:T(8,128)(2,1)S(1)}, u32[]{:S(2)}, u32[]{:S(2)}) collective-permute-start(bf16[96,640]{1,0:T(8,128)(2,1)S(1)} %select_convert_fusion.8), channel_id=1, source_target_pairs={{0,8},{8,0},{16,24},{24,16},{1,9},{9,1},{17,25},{25,17},{2,10},{10... | collective-permute-start | bytes 368648 | tf_op jit(solution)/shard_map/ppermute | solution.py:866
  807.0 36.7 %collective-permute-start.43 = (bf16[192,1280]{1,0:T(8,128)(2,1)S(1)}, bf16[192,1280]{1,0:T(8,128)(2,1)S(1)}, u32[]{:S(2)}, u32[]{:S(2)}) collective-permute-start(bf16[192,1280]{1,0:T(8,128)(2,1)S(1)} %pad_maximum_fusion.16), channel_id=1, source_target_pairs={{0,4},{4,0},{1,5},{5,1},{2,6},{6,2},{3,7},{7,3},{8,12},{12,8},{9,1... | collective-permute-start | bytes 1474568 | tf_op jit(solution)/shard_map/ppermute | solution.py:842
  819.9 6.8 collective-permute-start.49
  826.8 8.1 collective-permute-start.50
  835.0 8.4 collective-permute-start.51
  843.5 6.3 collective-permute-start.52
  (106 other events, 1215.0 us)
Sparse Core Ops, SparseCore 0:
  13.4 34.7 all-gather.5
  81.9 80.7 all-gather.11
  164.9 44.4 all-gather.9
  211.4 26.1 all-gather.7
  481.7 60.2 all-reduce.8
  544.2 30.6 reduce-scatter.12
  577.8 43.5 reduce-scatter.8
  624.3 76.0 reduce-scatter.10
  702.8 31.4 reduce-scatter.14
  752.5 108.2 all-gather.13
